TPU v7x, 32 devices: a whole 2x2x4 slice. The times are simulated.
32 devices in a mesh: pipe: 4 (over y, x), ctx: 8 (over z, core).
Axes of the slice: x: 2, y: 2, z: 4, core: 2. Of those that a mesh axis runs over, the one named last changes fastest.
Arguments:
- inner_x: bfloat16 [4, 1024, 8192], P('pipe', 'ctx'), may hold values from -6 to 6
- dt_raw: bfloat16 [4, 1024, 8192], P('pipe', 'ctx'), may hold values from -8 to -0.4
- grad_out: bfloat16 [4, 1024, 8192], P('pipe', 'ctx'), may hold values from -6 to 6
- state_maps: float32 [4, 2, 16, 1024], P('pipe', None, None, 'ctx'), may hold values from -6 to 6
- saved_states: float32 [4, 8, 16, 8192], P('pipe', 'ctx'), may hold values from -0.3 to 0.3
- a_log: float32 [4, 16, 8192], P('pipe'), may hold values from -0.5 to 0.5
- conv_weight: float32 [4, 4, 8192], P('pipe'), may hold values from -3 to 3
- conv_bias: float32 [4, 8192], P('pipe'), may hold values from -3 to 3
- skip_gain: float32 [4, 8192], P('pipe'), may hold values from 0.5 to 1.5
- doc_lengths: int32 [4, 8], P('pipe'), may hold values from 1 to 385, 1024 in all within a row
Outputs:
- upstream: bfloat16 [4, 1024, 8192], P('pipe', 'ctx')
- grad_dt: bfloat16 [4, 1024, 8192], P('pipe', 'ctx')
- grad_maps: float32 [4, 2, 16, 1024], P('pipe', None, None, 'ctx')
- grad_params: float32 [4, 22, 8192], P('pipe', None, 'ctx')
Inputs may be any that keep to these rules, and one draw needn't show every extreme that they name: `doc_lengths`: each section's lengths sum to 1024; the longest is exactly 385, so that no document touches more than 4 context shards and some document touches exactly 4.
All inputs are finite; a program needn't handle non-finite values.
Results may differ from a plain program's by a relative error of at most 0.001.
Values may be sent and summed in bfloat16 or wider, within the bound.
No kernel may reach another device: no remote copies, remote signals or barrier semaphores. Data moves between devices by JAX's collectives and lax.ppermute only.
A program may use at most 256 MiB of HBM per device.

v0:
```python
import jax
import jax.numpy as jnp
from jax import lax
from jax.sharding import PartitionSpec as P


def from_behind(x, axis, by):
    length = lax.axis_size(axis)
    pairs = [(i, i + by) for i in range(length) if 0 <= i + by < length]
    return lax.ppermute(x, axis, pairs)


def entering(x, axis, combine, identity):
    length, place = (lax.axis_size(axis), lax.axis_index(axis))
    everything = jax.tree.map(lambda part: lax.all_gather(part, axis), x)
    start = jax.tree.map(
        lambda part, zero: jnp.broadcast_to(jnp.asarray(zero, part.dtype), part.shape), x, identity
    )

    def turn(k, before):
        at = length - 1 - k
        reached = at > place
        new = combine(before, jax.tree.map(lambda part: part[at], everything))
        return jax.tree.map(lambda a, b: jnp.where(reached, a, b), new, before)

    return lax.fori_loop(0, length, turn, start)


def silu_slope(scalar_element):
    sigm = jax.nn.sigmoid(scalar_element)
    return sigm * (1.0 + scalar_element * (1.0 - sigm))


def on_device(
    inner_x,
    dt_raw,
    grad_out,
    state_maps,
    saved_states,
    a_log,
    conv_weight,
    conv_bias,
    skip_gain,
    doc_lengths,
):
    row_count = inner_x.shape[1]
    channels = inner_x.shape[2]
    conv_taps = conv_weight.shape[1]
    offset = lax.axis_index("ctx") * row_count
    lengths = doc_lengths[0]
    starts = jnp.cumsum(lengths) - lengths
    position = offset + jnp.arange(row_count, dtype=jnp.int32)
    doc_start = jnp.max(jnp.where(position[:, None] >= starts[None, :], starts[None, :], 0), axis=1)
    resets = jnp.any(position[:, None] == starts[None, :], axis=1)
    keeping = 1.0 - resets.astype(jnp.float32)
    x_rows = inner_x[0]
    history = from_behind(x_rows[row_count - conv_taps + 1 :], "ctx", 1)
    extended = jnp.concatenate([history, x_rows], 0)
    valid_masks = [
        (position - (conv_taps - 1 - j) >= doc_start).astype(jnp.float32)[:, None]
        for j in range(conv_taps)
    ]
    taps_weight = conv_weight[0]
    conv_out = jnp.broadcast_to(conv_bias[0][None, :], (row_count, channels))
    for j in range(conv_taps):
        conv_out = (
            conv_out
            + taps_weight[j][None, :]
            * extended[j : j + row_count].astype(jnp.float32)
            * valid_masks[j]
        )
    activated = jax.nn.silu(conv_out)
    step_size = jax.nn.softplus(dt_raw[0].astype(jnp.float32))
    decay_rate = -jnp.exp(a_log[0])
    grad_y = grad_out[0].astype(jnp.float32)
    b_rows = state_maps[0, 0].T
    c_rows = state_maps[0, 1].T
    lower = (jnp.arange(row_count)[:, None] >= jnp.arange(row_count)[None, :]).astype(jnp.float32)
    running = jnp.dot(lower, step_size, precision=lax.Precision.HIGHEST) - step_size[0][None, :]
    seen = jnp.cumsum(resets.astype(jnp.int32)) - resets[0].astype(jnp.int32)
    alive = (seen == 0).astype(jnp.float32)
    block = max(8, row_count // 16)
    blocks = row_count // block

    def cut(array, index):
        return lax.dynamic_slice_in_dim(array, index * block, block, 0)

    def local_sum(total, index):
        weight = (
            jnp.exp(decay_rate[None] * cut(running, index)[:, None, :])
            * cut(alive, index)[:, None, None]
        )
        source = cut(c_rows, index)[:, :, None] * cut(grad_y, index)[:, None, :]
        return (total + jnp.sum(weight * source, axis=0), None)

    zeros_state = jnp.zeros_like(decay_rate)
    head_adjoint, _ = lax.scan(local_sum, zeros_state, jnp.arange(blocks))
    first_decay = keeping[0] * jnp.exp(step_size[0][None, :] * decay_rate)
    carried = first_decay * head_adjoint
    through = jnp.exp(decay_rate * (running[-1] + step_size[0])[None, :]) * jnp.min(keeping)

    def compose(earlier, later):
        return (later[0] * earlier[0], later[0] * earlier[1] + later[1])

    prefix = entering(
        (through, carried), "ctx", compose, (jnp.ones_like(through), jnp.zeros_like(carried))
    )
    incoming = prefix[1]

    def forward_block(state, index):
        step_b = cut(step_size, index)
        act_b = cut(activated, index)
        keep_b = cut(keeping, index)
        b_blk = cut(b_rows, index)
        start_state = state
        for t in range(block):
            decay = keep_b[t] * jnp.exp(step_b[t][None, :] * decay_rate)
            state = decay * state + (step_b[t] * act_b[t])[None, :] * b_blk[t][:, None]
        return (state, start_state)

    _, checkpoints = lax.scan(forward_block, saved_states[0, 0], jnp.arange(blocks))

    def backward_block(carry_pair, index):
        adjoint, rate_grad = carry_pair
        step_b = cut(step_size, index)
        act_b = cut(activated, index)
        keep_b = cut(keeping, index)
        b_blk = cut(b_rows, index)
        c_blk = cut(c_rows, index)
        y_blk = cut(grad_y, index)
        state = lax.dynamic_index_in_dim(checkpoints, index, 0, keepdims=False)
        befores = []
        decays = []
        for t in range(block):
            decay = keep_b[t] * jnp.exp(step_b[t][None, :] * decay_rate)
            befores.append(state)
            decays.append(decay)
            state = decay * state + (step_b[t] * act_b[t])[None, :] * b_blk[t][:, None]
        afters = befores[1:] + [state]
        grads_u = [None] * block
        grads_step = [None] * block
        grads_b = [None] * block
        grads_c = [None] * block
        for t in range(block - 1, -1, -1):
            adjoint_now = c_blk[t][:, None] * y_blk[t][None, :] + adjoint
            scaled = adjoint_now * step_b[t][None, :]
            prior = decays[t] * befores[t]
            grads_u[t] = skip_gain[0] * y_blk[t] + jnp.sum(scaled * b_blk[t][:, None], axis=0)
            grads_step[t] = jnp.sum(
                adjoint_now * (b_blk[t][:, None] * act_b[t][None, :] + decay_rate * prior), axis=0
            )
            rate_grad = rate_grad + scaled * prior
            grads_b[t] = jnp.sum(scaled * act_b[t][None, :], axis=1)
            grads_c[t] = jnp.sum(afters[t] * y_blk[t][None, :], axis=1)
            adjoint = decays[t] * adjoint_now
        return (
            (adjoint, rate_grad),
            (jnp.stack(grads_u), jnp.stack(grads_step), jnp.stack(grads_b), jnp.stack(grads_c)),
        )

    (_, rate_grad), results = lax.scan(
        backward_block, (incoming, zeros_state), jnp.arange(blocks), reverse=True
    )
    grad_u = results[0].reshape(row_count, channels)
    grad_step = results[1].reshape(row_count, channels)
    grad_b = results[2].reshape(row_count, -1)
    grad_c = results[3].reshape(row_count, -1)
    grad_dt = (grad_step * jax.nn.sigmoid(dt_raw[0].astype(jnp.float32))).astype(jnp.bfloat16)
    grad_conv = grad_u * silu_slope(conv_out)
    grad_ext = jnp.zeros((row_count + conv_taps - 1, channels), jnp.float32)
    tap_grads = []
    for j in range(conv_taps):
        masked = grad_conv * valid_masks[j]
        grad_ext = grad_ext + jnp.pad(
            masked * taps_weight[j][None, :], ((j, conv_taps - 1 - j), (0, 0))
        )
        tap_grads.append(jnp.sum(masked * extended[j : j + row_count].astype(jnp.float32), axis=0))
    spilled = from_behind(grad_ext[: conv_taps - 1], "ctx", -1)
    grad_x = grad_ext[conv_taps - 1 :] + jnp.pad(spilled, ((row_count - conv_taps + 1, 0), (0, 0)))
    upstream = from_behind(grad_x.astype(jnp.bfloat16)[None], "pipe", -1)
    stacked = jnp.concatenate(
        [
            rate_grad * decay_rate,
            jnp.stack(tap_grads, 0),
            jnp.sum(grad_y * activated, axis=0)[None, :],
            jnp.sum(grad_conv, axis=0)[None, :],
        ],
        0,
    )
    shares = lax.psum_scatter(stacked, "ctx", scatter_dimension=1, tiled=True)
    grad_maps = jnp.stack([grad_b.T, grad_c.T], 0)[None]
    return (upstream, grad_dt[None], grad_maps, shares[None])


def solution(mesh):
    in_specs = (
        P("pipe", "ctx", None),
        P("pipe", "ctx", None),
        P("pipe", "ctx", None),
        P("pipe", None, None, "ctx"),
        P("pipe", "ctx", None, None),
        P("pipe", None, None),
        P("pipe", None, None),
        P("pipe", None),
        P("pipe", None),
        P("pipe", None),
    )
    out_specs = (
        P("pipe", "ctx", None),
        P("pipe", "ctx", None),
        P("pipe", None, None, "ctx"),
        P("pipe", None, "ctx"),
    )
    return jax.shard_map(
        on_device, mesh=mesh, in_specs=in_specs, out_specs=out_specs, check_vma=False
    )
```

profile of v0, /device:TPU:13, one launch (start us, length us, event | category | flops | bytes accessed | tf_op | source)
XLA Modules:
  0.0 1422.2 jit_solution(5173856762494313416)
XLA Ops:
  29.5 67.5 %while.65 = (s32[]{:T(128)}, f32[16,8192]{1,0:T(8,128)S(1)}, f32[16,8192]{1,0:T(8,128)S(1)}, s32[16]{0:T(128)S(1)}, f32[128,8192]{1,0:T(8,128)}, /*index=5*/f32[...) while((s32[]{:T(128)}, f32[16,8192]{1,0:T(8,128)S(1)}, ...), condition=%wide.region_6.7_spmd.clone, body=%wide.region_4.6_spmd.clone.sunk | while | flops 5373959 | bytes 4196141 | solution.py:97
  99.9 10.1 multiply_reduce_fusion.33
  110.1 217.2 %while.64 = (s32[]{:T(128)}, f32[16,8192]{1,0:T(8,128)S(1)}, f32[16,16,8192]{2,1,0:T(8,128)}, s32[16]{0:T(128)S(1)}, f32[128]{0:T(128)}, /*index=5*/f32[128,8192...) while((s32[]{:T(128)}, f32[16,8192]{1,0:T(8,128)S(1)}, ...), condition=%wide.region_11.12_spmd, body=%wide.region_10.11_spmd.sunk | while | flops 5308429 | bytes 4197399 | solution.py:121
  327.3 13.5 while.66
  347.4 985.8 %while.67 = (s32[]{:T(128)}, f32[16,8192]{1,0:T(8,128)S(1)}, f32[16,8192]{1,0:T(8,128)S(1)}, f32[16,8,8192]{2,1,0:T(8,128)}, f32[16,8,8192]{2,1,0:T(8,128)}, /*i...) while((s32[]{:T(128)}, f32[16,8192]{1,0:T(8,128)S(1)}, ...), condition=%wide.region_45.46_spmd.clone, body=%wide.region_12.45_spmd.clone.sunk | while | flops 44367632 | bytes 29053016 | solution.py:161
  360.5 7.9 multiply_reduce_fusion.44
  421.8 7.9 multiply_reduce_fusion.44
  483.2 7.9 multiply_reduce_fusion.44
  544.7 7.9 multiply_reduce_fusion.44
  606.2 7.9 multiply_reduce_fusion.44
  667.8 7.9 multiply_reduce_fusion.44
  730.0 7.9 multiply_reduce_fusion.44
  791.4 7.9 multiply_reduce_fusion.44
  852.9 7.9 multiply_reduce_fusion.44
  914.2 7.9 multiply_reduce_fusion.44
  975.6 7.9 multiply_reduce_fusion.44
  1037.4 7.9 multiply_reduce_fusion.44
  1099.3 7.9 multiply_reduce_fusion.44
  1161.5 7.9 multiply_reduce_fusion.44
  1223.0 7.9 multiply_reduce_fusion.44
  1284.4 7.9 multiply_reduce_fusion.44
  1334.1 10.2 fusion.27
  1369.8 16.2 %reduce-scatter.2.cloned.1.call-done = f32[22,1024]{1,0:T(8,128)} async-done(((f32[22,8192]{1,0:T(8,128)}), f32[22,1024]{1,0:T(8,128)}) %reduce-scatter.2.cloned.1.call-update) | async-done | bytes 90128 | tf_op jit(solution)/shard_map/reduce_scatter | solution.py:190
  1387.7 24.9 %collective-permute-done.2 = bf16[1,128,8192]{2,1,0:T(8,128)(2,1)} collective-permute-done((bf16[1,128,8192]{2,1,0:T(8,128)(2,1)}, bf16[1,128,8192]{2,1,0:T(8,128)(2,1)}, u32[]{:S(2)}, u32[]{:S(2)}) %collective-permute-start.2) | collective-permute-done | bytes 2097184 | tf_op jit(solution)/shard_map/ppermute | solution.py:10
  (773 shorter events, 1155.4 us)
Async XLA Ops:
  7.2 320.2 %all-gather.4.cloned.1.call-start = ((), (), s32[]{:S(2)}) async-start(), calls=%async_computation.1 | async-start | bytes 4718592 | tf_op jit(solution)/shard_map/all_gather | solution.py:15
  8.2 91.8 %collective-permute-start = (bf16[3,8192]{1,0:T(4,128)(2,1)S(1)}, bf16[3,8192]{1,0:T(4,128)(2,1)S(1)}, u32[]{:S(2)}, u32[]{:S(2)}) collective-permute-start(bf16[3,8192]{1,0:T(4,128)(2,1)S(1)} %slice_bitcast_fusion.24), channel_id=1, source_target_pairs={{0,1},{1,2},{2,3},{3,4},{4,5},{5,6},{6,7},{8,9},{9,10},{10,11},{11... | collective-permute-start | bytes 147464 | tf_op jit(solution)/shard_map/ppermute | solution.py:10
  25.9 301.5 %all-gather.6.cloned.1.call-start = ((), (), s32[]{:S(2)}) async-start(), calls=%async_computation.3 | async-start | bytes 4718592 | tf_op jit(solution)/shard_map/all_gather | solution.py:15
  29.5 67.6 %copy-start.8 = (f32[1,16,8192]{2,1,0:T(8,128)S(1)}, f32[1,16,8192]{2,1,0:T(8,128)}, u32[]{:S(2)}) copy-start(f32[1,16,8192]{2,1,0:T(8,128)} %param.23) | copy-start | bytes 1572868
  29.5 69.5 %copy-start.22 = (f32[1,4,8192]{2,1,0:T(4,128)S(1)}, f32[1,4,8192]{2,1,0:T(4,128)}, u32[]{:S(2)}) copy-start(f32[1,4,8192]{2,1,0:T(4,128)} %param.24) | copy-start | bytes 393220
  29.5 70.4 %copy-start.23 = (f32[1,8192]{1,0:T(1,128)S(1)}, f32[1,8192]{1,0:T(1,128)}, u32[]{:S(2)}) copy-start(f32[1,8192]{1,0:T(1,128)} %param.25) | copy-start | bytes 98308
  98.6 1287.4 %reduce-scatter.2.cloned.1.call-start = ((), (), s32[]{:S(2)}) async-start(), calls=%async_computation.2 | async-start | bytes 884736 | tf_op jit(solution)/shard_map/reduce_scatter | solution.py:190
  99.1 11.0 copy-start.10
  99.1 11.0 copy-start.12
  99.1 11.0 copy-start.14
  99.1 11.0 copy-start.16
  99.1 10.9 copy-start.25
  99.1 10.9 copy-start.27
  99.1 10.9 copy-start.29
  99.1 10.9 copy-start.31
  1334.1 10.2 copy-start.15
  1334.1 10.2 copy-start.17
  1334.1 10.3 copy-start.26
  1334.1 10.3 copy-start.28
  1334.1 10.3 copy-start.30
  1334.1 10.3 copy-start.32
  1348.3 11.1 collective-permute-start.1
  1356.5 10.9 copy-start.6
  1363.7 48.8 %collective-permute-start.2 = (bf16[1,128,8192]{2,1,0:T(8,128)(2,1)}, bf16[1,128,8192]{2,1,0:T(8,128)(2,1)}, u32[]{:S(2)}, u32[]{:S(2)}) collective-permute-start(bf16[1,128,8192]{2,1,0:T(8,128)(2,1)} %fusion.43), channel_id=1, source_target_pairs={{8,0},{16,8},{24,16},{9,1},{17,9},{25,17},{10,2},{18,10},{26,18},{... | collective-permute-start | bytes 6291464 | tf_op jit(solution)/shard_map/ppermute | solution.py:10
  (15 other events, 108.4 us)
Sparse Core Ops, SparseCore 0:
  26.0 45.5 all-gather.3
  98.8 45.6 all-gather.5
  1359.6 26.4 reduce-scatter.1
where the time goes:
time: 1440 us; the launch traced here: 1420 us
  other arithmetic  983 us (68%)
  local copies, waits for them, and re-layouts  306 us (21%)
  loops' own time  64 us (4%)
  waiting for transfers between devices  41.2 us (3%)
    reduce_sum x64, other arithmetic, backward_block(): grads_c[t] = jnp.sum(afters[t] * y_blk[t][None, :], axis=1)  325 us
    reduce_sum x48, other arithmetic, backward_block(): jnp.sum(adjoint_now * (b_blk[t][:, None] * act_b[t][None, :] + decay_rate...  215 us
    add x16, other arithmetic, backward_block(): rate_grad = rate_grad + scaled * prior  115 us
    add x16, other arithmetic, forward_block(): state = decay * state + (step_b[t] * act_b[t])[None, :] * b_blk[t][:, None]  93.6 us
    dynamic_slice x128, local copies, waits for them, and re-layouts, cut(): return lax.dynamic_slice_in_dim(array, index * block, block, 0)  85.2 us
    mul x16, other arithmetic, backward_block(): state = decay * state + (step_b[t] * act_b[t])[None, :] * b_blk[t][:, None]  61 us
    mul x16, other arithmetic, forward_block(): state = decay * state + (step_b[t] * act_b[t])[None, :] * b_blk[t][:, None]  56.5 us
    another operation x1, loops' own time, on_device(): lax.scan(backward_block, (incoming, zeros_state), jnp.arange(blocks), rev...  42.3 us
  transfers between devices with their start and end apart: 6, of which 2 were waited for; matrix products, arithmetic and copies ran while one was open for 22% of the time, Pallas kernels for 0%

commit v1 on v0

v1 whole, which is shorter than its diff:
```python
import functools

import jax
import jax.numpy as jnp
from jax import lax
from jax.experimental import pallas as pl
from jax.experimental.pallas import tpu as pltpu
from jax.sharding import PartitionSpec as P

LANES = 128
LOG2E = 1.4426950408889634
LN2 = 0.6931471805599453
RESET_STEP = 1e4
PAST = 8


def shift_to(x, axis, by):
    length = lax.axis_size(axis)
    pairs = [(i, i + by) for i in range(length) if 0 <= i + by < length]
    return lax.ppermute(x, axis, pairs)


def fill_keep(off_ref, len_ref, keep_ref, rows):
    def clear(i, _):
        keep_ref[i] = jnp.float32(1.0)
        return 0

    lax.fori_loop(0, rows + PAST, clear, 0)

    def mark(d, start):
        at = start - off_ref[0] + PAST

        @pl.when(jnp.logical_and(at >= 0, at < rows + PAST))
        def _():
            keep_ref[at] = jnp.float32(0.0)

        return start + len_ref[0, d]

    lax.fori_loop(0, len_ref.shape[1], mark, jnp.int32(0))


def softplus_of(dt):
    return jnp.log1p(jnp.exp(dt))


def head_kernel(group, unroll, off_ref, len_ref, maps_ref, dt_ref, gy_ref, alog_ref, head_ref,
                thr_ref, keep_ref, dt_s, gy_s, al_s, a2_s, tot_s):
    rows = dt_ref.shape[0]
    states = alog_ref.shape[0]

    @pl.when(pl.program_id(0) == 0)
    def _():
        fill_keep(off_ref, len_ref, keep_ref, rows)

    for j in range(group):
        cols = slice(j * LANES, (j + 1) * LANES)
        dt_s[j * rows:(j + 1) * rows, :] = dt_ref[:, cols].astype(jnp.float32)
        gy_s[j * rows:(j + 1) * rows, :] = gy_ref[:, cols].astype(jnp.float32)
        al_s[j * states:(j + 1) * states, :] = -LOG2E * jnp.exp(alog_ref[:, cols])
    for n in range(states):
        a2_s[n] = al_s[pl.ds(n, group, stride=states), :]

    def token(i, carry):
        cars, total = carry
        t = rows - 1 - i
        gy = gy_s[pl.ds(t, group, stride=rows), :]
        step = softplus_of(dt_s[pl.ds(t, group, stride=rows), :])
        step = step + (1.0 - keep_ref[PAST + t]) * RESET_STEP
        out = []
        for n in range(states):
            decay = jnp.exp2(step * a2_s[n])
            out.append(decay * (maps_ref[states + n, t] * gy + cars[n]))
        return tuple(out), total + step

    zero = jnp.zeros((group, LANES), jnp.float32)
    cars, total = lax.fori_loop(0, rows, token, ((zero,) * states, zero), unroll=unroll)
    for n in range(states):
        head_ref[0, n] = cars[n]
        thr_ref[0, n] = jnp.exp2(total * a2_s[n])


def head_call(group, off, lengths, maps, dt, gy, alog, base, blocks):
    rows = dt.shape[0]
    states = alog.shape[0]
    width = group * LANES
    smem = pl.BlockSpec(memory_space=pltpu.SMEM)
    col = lambda i: (0, base + i)
    carry = jax.ShapeDtypeStruct((blocks, states, group, LANES), jnp.float32)
    return pl.pallas_call(
        functools.partial(head_kernel, group, 4),
        grid=(blocks,),
        out_shape=(carry, carry),
        in_specs=[smem, smem, smem, pl.BlockSpec((rows, width), col),
                  pl.BlockSpec((rows, width), col), pl.BlockSpec((states, width), col)],
        out_specs=(pl.BlockSpec((1, states, group, LANES), lambda i: (i, 0, 0, 0)),) * 2,
        scratch_shapes=[
            pltpu.SMEM((rows + PAST,), jnp.float32),
            pltpu.VMEM((group * rows, LANES), jnp.float32),
            pltpu.VMEM((group * rows, LANES), jnp.float32),
            pltpu.VMEM((group * states, LANES), jnp.float32),
            pltpu.VMEM((states, group, LANES), jnp.float32),
            pltpu.VMEM((group, LANES), jnp.float32),
        ],
        compiler_params=pltpu.CompilerParams(
            dimension_semantics=("arbitrary",), vmem_limit_bytes=16 << 20),
        cost_estimate=pl.CostEstimate(
            flops=blocks * rows * states * width * 6, transcendentals=0,
            bytes_accessed=blocks * width * (rows * 4 + states * 12)),
        name="head",
    )(off, lengths, maps, dt, gy, alog)


def main_kernel(group, part, off_ref, len_ref, maps_ref, x_ref, hist_ref, dt_ref, gy_ref,
                start_ref, alog_ref, cw_ref, cb_ref, sk_ref, gin_ref,
                gx_ref, gdt_ref, edge_ref, gp_ref, gm_ref,
                keep_ref, x_s, dt_s, gy_s, al_s, st_s, row_s, a2_s, hist_s, wt_s,
                step_t, du_t, gy_t, u_t, sig_t, slope_t, w_t, v_t, dec_s, h_s, acc_s, out_s, gp_s):
    rows = x_ref.shape[0]
    states = alog_ref.shape[0]
    first = pl.program_id(0) == 0
    f32 = jnp.float32

    @pl.when(first)
    def _():
        fill_keep(off_ref, len_ref, keep_ref, rows)

    for j in range(group):
        cols = slice(j * LANES, (j + 1) * LANES)
        tall = slice(j * rows, (j + 1) * rows)
        x_s[tall, :] = x_ref[:, cols].astype(f32)
        dt_s[tall, :] = dt_ref[:, cols].astype(f32)
        gy_s[tall, :] = gy_ref[:, cols].astype(f32)
        al_s[j * states:(j + 1) * states, :] = -LOG2E * jnp.exp(alog_ref[:, cols])
        st_s[j * states:(j + 1) * states, :] = start_ref[:, cols]
        hist_s[j:j + 1, :] = hist_ref[0:1, cols].astype(f32)
        hist_s[group + j:group + j + 1, :] = hist_ref[1:2, cols].astype(f32)
        hist_s[2 * group + j:2 * group + j + 1, :] = hist_ref[2:3, cols].astype(f32)
        for k in range(4):
            wt_s[k * group + j:k * group + j + 1, :] = cw_ref[k:k + 1, cols]
        wt_s[4 * group + j:4 * group + j + 1, :] = cb_ref[:, cols]
        wt_s[5 * group + j:5 * group + j + 1, :] = sk_ref[:, cols]
    for n in range(states):
        a2_s[n] = al_s[pl.ds(n, group, stride=states), :]
        h_s[0, n] = st_s[pl.ds(n, group, stride=states), :]

    def weight(k):
        return wt_s[k * group:(k + 1) * group, :]

    def past(k):
        return hist_s[k * group:(k + 1) * group, :]

    def rows_of(t, carry):
        before, x1, x2 = carry
        keep = keep_ref[PAST + t]
        own = pl.ds(t, group, stride=rows)
        x = x_s[own, :]
        y = gy_s[own, :]
        dt = dt_s[own, :]
        k1 = keep * before
        k2 = keep * x1
        k3 = keep * x2
        conv = weight(4) + weight(0) * k3 + weight(1) * k2 + weight(2) * k1 + weight(3) * x
        sig = 1.0 / (1.0 + jnp.exp(-conv))
        u = conv * sig
        e = jnp.exp(dt)
        step = jnp.log1p(e)
        step_t[t] = step + (1.0 - keep) * RESET_STEP
        du_t[t] = step * u
        gy_t[t] = y
        u_t[t] = u
        sig_t[t] = e / (1.0 + e)
        slope_t[t] = sig * (1.0 + conv * (1.0 - sig))
        return x, k1, k2

    k_1 = keep_ref[PAST - 1]
    k_2 = keep_ref[PAST - 2]
    lax.fori_loop(0, rows, rows_of, (past(2), k_1 * past(1), k_1 * k_2 * past(0)), unroll=2)

    @pl.when(first)
    def _():
        def wipe(t, _):
            for n in range(2 * states):
                acc_s[n, t] = jnp.zeros((8, LANES), f32)
            return 0
        lax.fori_loop(0, rows, wipe, 0)

    def fold(p):
        out = p[0:8]
        for k in range(1, group // 8):
            out = out + p[k * 8:(k + 1) * 8]
        return out

    for lo in range(0, states, part):
        hi = lo + part

        def forward(t, hs):
            step = step_t[t]
            du = du_t[t]
            out = []
            for n in range(lo, hi):
                decay = jnp.exp2(step * a2_s[n])
                h = decay * hs[n - lo] + maps_ref[n, t] * du
                dec_s[t, n - lo] = decay
                h_s[t + 1, n] = h
                out.append(h)
            return tuple(out)

        lax.fori_loop(0, rows, forward, tuple(h_s[0, n] for n in range(lo, hi)), unroll=2)

        def backward(i, carry):
            cars, rates = carry
            t = rows - 1 - i
            step = step_t[t]
            du = du_t[t]
            y = gy_t[t]
            new_cars, new_rates = [], []
            w = jnp.zeros_like(y) if lo == 0 else w_t[t]
            v = jnp.zeros_like(y) if lo == 0 else v_t[t]
            for n in range(lo, hi):
                m = n - lo
                g = maps_ref[states + n, t] * y + cars[m]
                acc_s[n, t] += fold(g * du)
                acc_s[states + n, t] += fold(h_s[t + 1, n] * y)
                w = w + maps_ref[n, t] * g
                car = dec_s[t, m] * g
                aq = a2_s[n] * (car * h_s[t, n])
                v = v + aq
                new_cars.append(car)
                new_rates.append(rates[m] + step * aq)
            w_t[t] = w
            v_t[t] = v
            return tuple(new_cars), tuple(new_rates)

        zero = jnp.zeros((group, LANES), f32)
        _, rates = lax.fori_loop(
            0, rows, backward,
            (tuple(gin_ref[0, n] for n in range(lo, hi)), (zero,) * part), unroll=2)
        for n in range(lo, hi):
            gp_s[pl.ds(n, group, stride=24), :] = rates[n - lo] * LN2

    def finish(i, carry):
        d1, d2, d3, taps, bias, skip = carry
        t = rows - 1 - i
        own = pl.ds(t, group, stride=rows)
        x = x_s[own, :]
        y = gy_t[t]
        u = u_t[t]
        w = w_t[t]
        du = du_t[t]
        sig = sig_t[t]
        step = step_t[t] - (1.0 - keep_ref[PAST + t]) * RESET_STEP
        step = jnp.where(step_t[t] > 0.5 * RESET_STEP, softplus_of(dt_s[own, :]), step)
        grad_u = weight(5) * y + step * w
        grad_step = u * w + LN2 * v_t[t]
        dt_s[own, :] = grad_step * sig
        gc = grad_u * slope_t[t]
        x_s[own, :] = weight(3) * gc + weight(2) * d1 + weight(1) * d2 + weight(0) * d3
        taps = (taps[0] + x * d3, taps[1] + x * d2, taps[2] + x * d1, taps[3] + x * gc)
        keep = keep_ref[PAST + t]
        return keep * gc, keep * d1, keep * d2, taps, bias + gc, skip + y * u

    zero = past(0) * 0.0
    d1, d2, d3, taps, bias, skip = lax.fori_loop(
        0, rows, finish, (zero, zero, zero, (zero,) * 4, zero, zero), unroll=2)
    taps = list(taps)
    for k in range(3):
        out = weight(0) * d3
        taps[0] = taps[0] + past(2 - k) * d3
        if k < 2:
            out = out + weight(1) * d2
            taps[1] = taps[1] + past(2 - k) * d2
        if k < 1:
            out = out + weight(2) * d1
            taps[2] = taps[2] + past(2 - k) * d1
        row_s[pl.ds(2 - k, group, stride=8), :] = out
        keep = keep_ref[PAST - 1 - k]
        d1, d2, d3 = d1, keep * d1, keep * d2
    for k in range(4):
        gp_s[pl.ds(states + k, group, stride=24), :] = taps[k]
    gp_s[pl.ds(states + 4, group, stride=24), :] = skip
    gp_s[pl.ds(states + 5, group, stride=24), :] = bias
    for k in range(3):
        row_s[pl.ds(3 + k, group, stride=8), :] = x_s[pl.ds(rows - 3 + k, group, stride=rows), :]

    for j in range(group):
        cols = slice(j * LANES, (j + 1) * LANES)
        tall = slice(j * rows, (j + 1) * rows)
        gx_ref[:, cols] = x_s[tall, :].astype(jnp.bfloat16)
        gdt_ref[:, cols] = dt_s[tall, :].astype(jnp.bfloat16)
        edge_ref[:, cols] = row_s[j * 8:j * 8 + 6, :]
        gp_ref[:, cols] = gp_s[j * 24:j * 24 + states + 6, :]

    @pl.when(pl.program_id(0) == pl.num_programs(0) - 1)
    def _():
        def reduce_state(n, _):
            for tb in range(rows // 8):
                total = acc_s[n, tb * 8:tb * 8 + 8]
                out_s[tb * 8:tb * 8 + 8, :] = jnp.sum(total, axis=1)
            flat = out_s[...].T
            gm_ref[pl.ds(n, 1), :] = jnp.sum(flat, axis=0, keepdims=True)
            return 0
        lax.fori_loop(0, 2 * states, reduce_state, 0)


def main_call(group, part, off, lengths, maps, x, hist, dt, gy, start, alog, cw, cb, sk, gin,
              base, blocks):
    rows = x.shape[0]
    states = alog.shape[0]
    width = group * LANES
    smem = pl.BlockSpec(memory_space=pltpu.SMEM)
    col = lambda i: (0, base + i)
    out_col = lambda i: (0, i)
    f32 = jnp.float32
    table = pltpu.VMEM((rows, group, LANES), f32)
    return pl.pallas_call(
        functools.partial(main_kernel, group, part),
        grid=(blocks,),
        out_shape=(
            jax.ShapeDtypeStruct((rows, blocks * width), jnp.bfloat16),
            jax.ShapeDtypeStruct((rows, blocks * width), jnp.bfloat16),
            jax.ShapeDtypeStruct((6, blocks * width), f32),
            jax.ShapeDtypeStruct((states + 6, blocks * width), f32),
            jax.ShapeDtypeStruct((2 * states, rows), f32),
        ),
        in_specs=[smem, smem, smem,
                  pl.BlockSpec((rows, width), col),
                  pl.BlockSpec((3, width), col),
                  pl.BlockSpec((rows, width), col),
                  pl.BlockSpec((rows, width), col),
                  pl.BlockSpec((states, width), col),
                  pl.BlockSpec((states, width), col),
                  pl.BlockSpec((4, width), col),
                  pl.BlockSpec((1, width), col),
                  pl.BlockSpec((1, width), col),
                  pl.BlockSpec((1, states, group, LANES), lambda i: (i, 0, 0, 0))],
        out_specs=(pl.BlockSpec((rows, width), out_col),
                   pl.BlockSpec((rows, width), out_col),
                   pl.BlockSpec((6, width), out_col),
                   pl.BlockSpec((states + 6, width), out_col),
                   pl.BlockSpec((2 * states, rows), lambda i: (0, 0))),
        scratch_shapes=[
            pltpu.SMEM((rows + PAST,), f32),
            pltpu.VMEM((group * rows, LANES), f32),
            pltpu.VMEM((group * rows, LANES), f32),
            pltpu.VMEM((group * rows, LANES), f32),
            pltpu.VMEM((group * states, LANES), f32),
            pltpu.VMEM((group * states, LANES), f32),
            pltpu.VMEM((group * 8, LANES), f32),
            pltpu.VMEM((states, group, LANES), f32),
            pltpu.VMEM((3 * group, LANES), f32),
            pltpu.VMEM((6 * group, LANES), f32),
            table, table, table, table, table, table, table, table,
            pltpu.VMEM((rows, part, group, LANES), f32),
            pltpu.VMEM((rows + 1, states, group, LANES), f32),
            pltpu.VMEM((2 * states, rows, 8, LANES), f32),
            pltpu.VMEM((rows, LANES), f32),
            pltpu.VMEM((group * 24, LANES), f32),
        ],
        compiler_params=pltpu.CompilerParams(
            dimension_semantics=("arbitrary",), vmem_limit_bytes=60 << 20),
        cost_estimate=pl.CostEstimate(
            flops=blocks * rows * states * width * 24, transcendentals=0,
            bytes_accessed=blocks * width * (rows * 10 + states * 16)),
        name="main",
    )(off, lengths, maps, x, hist, dt, gy, start, alog, cw, cb, sk, gin)


def on_device(inner_x, dt_raw, grad_out, state_maps, saved_states, a_log, conv_weight, conv_bias,
              skip_gain, doc_lengths):
    rows = inner_x.shape[1]
    channels = inner_x.shape[2]
    states = a_log.shape[1]
    group = 8
    blocks = channels // (group * LANES)
    off = (lax.axis_index("ctx") * rows).astype(jnp.int32).reshape(1)
    maps = state_maps[0].reshape(2 * states, rows)
    x, dt, gy = inner_x[0], dt_raw[0], grad_out[0]
    hist = shift_to(x[rows - 3:], "ctx", 1)

    head, through = head_call(group, off, doc_lengths, maps, dt, gy, a_log[0], 0, blocks)
    arrived = shift_to(head, "ctx", -1)
    for _ in range(2):
        arrived = shift_to(head + through * arrived, "ctx", -1)

    gx, gdt, edge, gp, gm = main_call(
        group, states, off, doc_lengths, maps, x, hist, dt, gy, saved_states[0, 0], a_log[0],
        conv_weight[0], conv_bias, skip_gain, arrived, 0, blocks)

    spilled = shift_to(edge[:3], "ctx", -1)
    tail = (edge[3:] + spilled).astype(jnp.bfloat16)
    upstream = shift_to(gx, "pipe", -1)
    tail = shift_to(tail, "pipe", -1)
    upstream = lax.dynamic_update_slice(upstream, tail, (rows - 3, 0))
    shares = lax.psum_scatter(gp, "ctx", scatter_dimension=1, tiled=True)
    return upstream[None], gdt[None], gm.reshape(1, 2, states, rows), shares[None]


def solution(mesh):
    in_specs = (
        P("pipe", "ctx", None),
        P("pipe", "ctx", None),
        P("pipe", "ctx", None),
        P("pipe", None, None, "ctx"),
        P("pipe", "ctx", None, None),
        P("pipe", None, None),
        P("pipe", None, None),
        P("pipe", None),
        P("pipe", None),
        P("pipe", None),
    )
    out_specs = (
        P("pipe", "ctx", None),
        P("pipe", "ctx", None),
        P("pipe", None, None, "ctx"),
        P("pipe", None, "ctx"),
    )
    return jax.shard_map(
        on_device, mesh=mesh, in_specs=in_specs, out_specs=out_specs, check_vma=False
    )
```

time: 1440 us -> 254 us (0.18); the launches traced: 1420 us -> 252 us
  other arithmetic: 983 us -> 1.16 us
  local copies, waits for them, and re-layouts: 306 us -> 11.9 us
  Pallas kernels: 0 us -> 148 us
  loops' own time: 64 us -> 0 us
  waiting for transfers between devices: 41.2 us -> 59.8 us
    reduce_sum x146 -> x0, other arithmetic: 595 us -> none  [the longest x64 325 us: backward_block(): grads_c[t] = jnp.sum(afters[t] * y_blk[t][None, :], axis=1)]
    add x67 -> x2, other arithmetic: 234 us -> 0.16 us  [on_device(): arrived = shift_to(head + through * arrived, 'ctx', -1)]
    pallas_call x0 -> x2, Pallas kernels: none -> 148 us  [the longest x1 124 us: main_call(): pl.pallas_call(functools.partial(main_kernel, group, part), grid=(blocks,...]
    dynamic_slice x176 -> x0, local copies, waits for them, and re-layouts: 124 us -> none  [the longest x128 85.2 us: cut(): return lax.dynamic_slice_in_dim(array, index * block, block, 0)]
    mul x35 -> x0, other arithmetic: 122 us -> none  [the longest x16 61 us: backward_block(): state = decay * state + (step_b[t] * act_b[t])[None, :] * b_blk[t][:, None]]
    another operation x4 -> x0, loops' own time: 64 us -> none  [the longest x1 42.3 us: on_device(): lax.scan(backward_block, (incoming, zeros_state), jnp.arange(blocks), rev...]
    slice x52 -> x2, local copies, waits for them, and re-layouts: 59.9 us -> 1.92 us  [the longest x1 0.97 us: on_device(): spilled = shift_to(edge[:3], 'ctx', -1)]
    dynamic_update_slice x80 -> x1, local copies, waits for them, and re-layouts: 55.7 us -> 0.61 us  [on_device(): upstream = lax.dynamic_update_slice(upstream, tail, (rows - 3, 0))]
  transfers between devices with their start and end apart: 6 -> 8, of which waited for: 2 -> 7; matrix products, arithmetic and copies ran while one was open for 22% -> 2% of each run, Pallas kernels for 0% -> 0%
where the time goes in v1:
time: 254 us; the launch traced here: 252 us
  Pallas kernels  148 us (58%)
  waiting for transfers between devices  59.8 us (24%)
  starting transfers between devices  17.2 us (7%)
  between operations  14.1 us (6%)
  local copies, waits for them, and re-layouts  11.9 us (5%)
    pallas_call x1, Pallas kernels, main_call(): pl.pallas_call(functools.partial(main_kernel, group, part), grid=(blocks,...  124 us
    ppermute x7, waiting for transfers between devices, shift_to(): return lax.ppermute(x, axis, pairs)  41.9 us
    pallas_call x1, Pallas kernels, head_call(): pl.pallas_call(functools.partial(head_kernel, group, 4), grid=(blocks,),...  24.5 us
    reduce_scatter x1, waiting for transfers between devices, on_device(): shares = lax.psum_scatter(gp, 'ctx', scatter_dimension=1, tiled=True)  17.9 us
    ppermute x7, starting transfers between devices, shift_to(): return lax.ppermute(x, axis, pairs)  17.2 us
    unnamed x16, local copies, waits for them, and re-layouts  9.35 us
  transfers between devices with their start and end apart: 8, of which 7 were waited for; matrix products, arithmetic and copies ran while one was open for 2% of the time, Pallas kernels for 0%

profile of v1, /device:TPU:13, one launch (start us, length us, event | category | flops | bytes accessed | tf_op | source)
XLA Modules:
  0.0 252.3 jit_solution(772237546611582832)
XLA Ops:
  7.2 1.6 copy-done
  8.8 1.6 copy-done.1
  10.4 1.0 copy-done.2
  12.8 24.5 %head.1 = (f32[8,16,8,128]{3,2,1,0:T(8,128)S(1)}, f32[8,16,8,128]{3,2,1,0:T(8,128)S(1)}) custom-call(s32[1]{0:T(128)} %bitcast.off_ref, s32[1,8]{1,0:T(1,128)S(1)} %copy-done.4, f32[32,128]{1,0:T(8,128)S(1)} %bitcast.22, bf16[128,8192]{1,0:T(8,128)(2,1)S(1)} %bitcast.16, bf16[128,8192]{1,0:T(8,128)(2,1)S(1)} %bitcast.18, f32[16,8192]{1,0:T(8,128)S(1)} %bitcast.20), custom_call_target="tpu_custom_call" | custom-call | flops 100663296 | bytes 5767168 | tf_op jit(solution)/shard_map/head/pallas_call | solution.py:89
  37.3 2.6 %collective-permute-start.1 = (f32[8,16,8,128]{3,2,1,0:T(8,128)S(1)}, f32[8,16,8,128]{3,2,1,0:T(8,128)S(1)}, u32[]{:S(2)}, u32[]{:S(2)}) collective-permute-start(f32[8,16,8,128]{3,2,1,0:T(8,128)S(1)} %get-tuple-element.11), channel_id=1, source_target_pairs={{1,0},{2,1},{3,2},{4,3},{5,4},{6,5},{7,6},{9,8},{10,9},{11,10},{12... | collective-permute-start | bytes 1572872 | tf_op jit(solution)/shard_map/ppermute | solution.py:20
  39.9 8.0 %collective-permute-done.1 = f32[8,16,8,128]{3,2,1,0:T(8,128)S(1)} collective-permute-done((f32[8,16,8,128]{3,2,1,0:T(8,128)S(1)}, f32[8,16,8,128]{3,2,1,0:T(8,128)S(1)}, u32[]{:S(2)}, u32[]{:S(2)}) %collective-permute-start.1) | collective-permute-done | bytes 524320 | tf_op jit(solution)/shard_map/ppermute | solution.py:20
  48.0 1.9 collective-permute-start.2
  49.9 8.6 %collective-permute-done.2 = f32[8,16,8,128]{3,2,1,0:T(8,128)S(1)} collective-permute-done((f32[8,16,8,128]{3,2,1,0:T(8,128)S(1)}, f32[8,16,8,128]{3,2,1,0:T(8,128)S(1)}, u32[]{:S(2)}, u32[]{:S(2)}) %collective-permute-start.2) | collective-permute-done | bytes 524320 | tf_op jit(solution)/shard_map/ppermute | solution.py:20
  58.6 1.9 collective-permute-start.3
  60.5 0.9 slice_bitcast_fusion
  61.5 3.6 %collective-permute-start = (bf16[3,8192]{1,0:T(4,128)(2,1)S(1)}, bf16[3,8192]{1,0:T(4,128)(2,1)S(1)}, u32[]{:S(2)}, u32[]{:S(2)}) collective-permute-start(bf16[3,8192]{1,0:T(4,128)(2,1)S(1)} %slice_bitcast_fusion), channel_id=1, source_target_pairs={{0,1},{1,2},{2,3},{3,4},{4,5},{5,6},{6,7},{8,9},{9,10},{10,11},{11... | collective-permute-start | bytes 147464 | tf_op jit(solution)/shard_map/ppermute | solution.py:20
  65.1 1.3 collective-permute-done.hist_ref
  66.4 2.7 %collective-permute-done.3.gin_ref = f32[8,16,8,128]{3,2,1,0:T(8,128)S(1)} collective-permute-done((f32[8,16,8,128]{3,2,1,0:T(8,128)S(1)}, f32[8,16,8,128]{3,2,1,0:T(8,128)S(1)}, u32[]{:S(2)}, u32[]{:S(2)}) %collective-permute-start.3) | collective-permute-done | bytes 524320 | tf_op jit(solution)/shard_map/ppermute | solution.py:20
  69.9 123.7 %main.1 = (bf16[128,8192]{1,0:T(8,128)(2,1)}, bf16[128,8192]{1,0:T(8,128)(2,1)}, f32[6,8192]{1,0:T(8,128)}, f32[22,8192]{1,0:T(8,128)}, f32[32,128]{1,0:T(8,128)}) custom-call(s32[1]{0:T(128)} %bitcast.off_ref, s32[1,8]{1,0:T(1,128)} %len_ref.3, f32[32,128]{1,0:T(8,128)} %bitcast.21, bf16[128,8192]{1,0:T(8,128)(2,1)} %bitcast.23, bf16[3,8192]{1,0:T(4,128)(2,1)} %copy-done.6, ...), custom_call_target="tpu_custom_call" | custom-call | flops 402653184 | bytes 12582912 | tf_op jit(solution)/shard_map/main/pallas_call | solution.py:315
  193.6 3.1 %collective-permute-start.4 = (bf16[128,8192]{1,0:T(8,128)(2,1)}, bf16[128,8192]{1,0:T(8,128)(2,1)S(1)}, u32[]{:S(2)}, u32[]{:S(2)}) collective-permute-start(bf16[128,8192]{1,0:T(8,128)(2,1)} %get-tuple-element.13), channel_id=1, source_target_pairs={{8,0},{16,8},{24,16},{9,1},{17,9},{25,17},{10,2},{18,10},{26,18},{... | collective-permute-start | bytes 6291464 | tf_op jit(solution)/shard_map/ppermute | solution.py:20
  196.6 1.0 slice.15
  197.6 1.9 collective-permute-start.5
  199.6 4.6 %collective-permute-done.5 = f32[3,8192]{1,0:T(4,128)S(1)} collective-permute-done((f32[3,8192]{1,0:T(4,128)S(1)}, f32[3,8192]{1,0:T(4,128)S(1)}, u32[]{:S(2)}, u32[]{:S(2)}) %collective-permute-start.5) | collective-permute-done | bytes 98336 | tf_op jit(solution)/shard_map/ppermute | solution.py:20
  204.2 1.0 add_convert_fusion
  205.2 2.2 collective-permute-start.6
  207.4 17.9 %reduce-scatter.2.cloned.1.call-done = f32[22,1024]{1,0:T(8,128)} async-done(((f32[22,8192]{1,0:T(8,128)}), f32[22,1024]{1,0:T(8,128)}) %reduce-scatter.2.cloned.1.call-update) | async-done | bytes 90128 | tf_op jit(solution)/shard_map/reduce_scatter | solution.py:394
  225.2 1.6 copy.14
  226.9 16.7 %collective-permute-done.6 = bf16[3,8192]{1,0:T(4,128)(2,1)S(1)} collective-permute-done((bf16[3,8192]{1,0:T(4,128)(2,1)S(1)}, bf16[3,8192]{1,0:T(4,128)(2,1)S(1)}, u32[]{:S(2)}, u32[]{:S(2)}) %collective-permute-start.6) | collective-permute-done | bytes 49184 | tf_op jit(solution)/shard_map/ppermute | solution.py:20
  244.2 1.3 copy.17
  (17 shorter events, 3.0 us)
Async XLA Ops:
  7.2 218.1 %reduce-scatter.2.cloned.1.call-start = ((), (), s32[]{:S(2)}) async-start(), calls=%async_computation.1 | async-start | bytes 884736 | tf_op jit(solution)/shard_map/reduce_scatter | solution.py:394
  7.2 1.6 copy-start
  8.8 1.6 copy-start.1
  10.4 1.0 copy-start.2
  11.4 0.7 copy-start.3
  12.2 0.7 copy-start.4
  37.3 10.6 %collective-permute-start.1 = (f32[8,16,8,128]{3,2,1,0:T(8,128)S(1)}, f32[8,16,8,128]{3,2,1,0:T(8,128)S(1)}, u32[]{:S(2)}, u32[]{:S(2)}) collective-permute-start(f32[8,16,8,128]{3,2,1,0:T(8,128)S(1)} %get-tuple-element.11), channel_id=1, source_target_pairs={{1,0},{2,1},{3,2},{4,3},{5,4},{6,5},{7,6},{9,8},{10,9},{11,10},{12... | collective-permute-start | bytes 1572872 | tf_op jit(solution)/shard_map/ppermute | solution.py:20
  48.0 10.5 %collective-permute-start.2 = (f32[8,16,8,128]{3,2,1,0:T(8,128)S(1)}, f32[8,16,8,128]{3,2,1,0:T(8,128)S(1)}, u32[]{:S(2)}, u32[]{:S(2)}) collective-permute-start(f32[8,16,8,128]{3,2,1,0:T(8,128)S(1)} %multiply_add_fusion.1), channel_id=1, source_target_pairs={{1,0},{2,1},{3,2},{4,3},{5,4},{6,5},{7,6},{9,8},{10,9},{11,10},{12... | collective-permute-start | bytes 1572872 | tf_op jit(solution)/shard_map/ppermute | solution.py:20
  58.6 10.5 %collective-permute-start.3 = (f32[8,16,8,128]{3,2,1,0:T(8,128)S(1)}, f32[8,16,8,128]{3,2,1,0:T(8,128)S(1)}, u32[]{:S(2)}, u32[]{:S(2)}) collective-permute-start(f32[8,16,8,128]{3,2,1,0:T(8,128)S(1)} %multiply_add_fusion), channel_id=1, source_target_pairs={{1,0},{2,1},{3,2},{4,3},{5,4},{6,5},{7,6},{9,8},{10,9},{11,10},{12... | collective-permute-start | bytes 1572872 | tf_op jit(solution)/shard_map/ppermute | solution.py:20
  61.5 5.0 %collective-permute-start = (bf16[3,8192]{1,0:T(4,128)(2,1)S(1)}, bf16[3,8192]{1,0:T(4,128)(2,1)S(1)}, u32[]{:S(2)}, u32[]{:S(2)}) collective-permute-start(bf16[3,8192]{1,0:T(4,128)(2,1)S(1)} %slice_bitcast_fusion), channel_id=1, source_target_pairs={{0,1},{1,2},{2,3},{3,4},{4,5},{5,6},{6,7},{8,9},{9,10},{10,11},{11... | collective-permute-start | bytes 147464 | tf_op jit(solution)/shard_map/ppermute | solution.py:20
  66.4 2.7 %copy-start.6 = (bf16[3,8192]{1,0:T(4,128)(2,1)}, bf16[3,8192]{1,0:T(4,128)(2,1)S(1)}, u32[]{:S(2)}) copy-start(bf16[3,8192]{1,0:T(4,128)(2,1)S(1)} %collective-permute-done.hist_ref) | copy-start | bytes 147460
  69.1 0.8 copy-start.5
  193.6 50.0 %collective-permute-start.4 = (bf16[128,8192]{1,0:T(8,128)(2,1)}, bf16[128,8192]{1,0:T(8,128)(2,1)S(1)}, u32[]{:S(2)}, u32[]{:S(2)}) collective-permute-start(bf16[128,8192]{1,0:T(8,128)(2,1)} %get-tuple-element.13), channel_id=1, source_target_pairs={{8,0},{16,8},{24,16},{9,1},{17,9},{25,17},{10,2},{18,10},{26,18},{... | collective-permute-start | bytes 6291464 | tf_op jit(solution)/shard_map/ppermute | solution.py:20
  197.6 6.6 %collective-permute-start.5 = (f32[3,8192]{1,0:T(4,128)S(1)}, f32[3,8192]{1,0:T(4,128)S(1)}, u32[]{:S(2)}, u32[]{:S(2)}) collective-permute-start(f32[3,8192]{1,0:T(4,128)S(1)} %slice.15), channel_id=1, source_target_pairs={{1,0},{2,1},{3,2},{4,3},{5,4},{6,5},{7,6},{9,8},{10,9},{11,10},{12... | collective-permute-start | bytes 294920 | tf_op jit(solution)/shard_map/ppermute | solution.py:20
  205.2 38.3 %collective-permute-start.6 = (bf16[3,8192]{1,0:T(4,128)(2,1)S(1)}, bf16[3,8192]{1,0:T(4,128)(2,1)S(1)}, u32[]{:S(2)}, u32[]{:S(2)}) collective-permute-start(bf16[3,8192]{1,0:T(4,128)(2,1)S(1)} %add_convert_fusion), channel_id=1, source_target_pairs={{8,0},{16,8},{24,16},{9,1},{17,9},{25,17},{10,2},{18,10},{26,18},{... | collective-permute-start | bytes 147464 | tf_op jit(solution)/shard_map/ppermute | solution.py:20
Sparse Core Ops, SparseCore 0:
  199.7 25.4 reduce-scatter.1

commit v2 on v0

v2 whole, which is shorter than its diff:
```python
import functools

import jax
import jax.numpy as jnp
from jax import lax
from jax.experimental import pallas as pl
from jax.experimental.pallas import tpu as pltpu
from jax.sharding import PartitionSpec as P

LANES = 128
LOG2E = 1.4426950408889634
LN2 = 0.6931471805599453
RESET_STEP = 1e4
PAST = 8
CHUNK = 8
WIDE = 16
MIB = 1 << 20
HEAD_VMEM = 60 * MIB
MAIN_VMEM = 60 * MIB
REACH = 3


def shift_to(x, axis, by):
    length = lax.axis_size(axis)
    pairs = [(i, i + by) for i in range(length) if 0 <= i + by < length]
    return lax.ppermute(x, axis, pairs)


def at_chunk(i, size):
    return pl.multiple_of(i * size, size)


def fill_keep(offset, len_ref, keep_t):
    rows, lanes = keep_t.shape
    place = lax.broadcasted_iota(jnp.int32, (rows, lanes), 0) + (offset - PAST)

    def mark(d, carry):
        start, keep = carry
        return start + len_ref[0, d], jnp.where(place == start, 0.0, keep)

    _, keep = lax.fori_loop(
        0, len_ref.shape[1], mark, (jnp.int32(0), jnp.ones((rows, lanes), jnp.float32)))
    keep_t[...] = keep


def fill_maps(maps_ref, maps_t):
    count, rows = maps_ref.shape
    turned = maps_ref[...].T
    for n in range(count):
        maps_t[n * rows:(n + 1) * rows, :] = jnp.broadcast_to(turned[:, n:n + 1], (rows, LANES))


def spread(ref, row, group):
    return ref[pl.ds(row, group, stride=0), :]


def gather_positions(src_ref, dst, group, first=0):
    rows = src_ref.shape[0]

    def move(i, _):
        t = at_chunk(i, WIDE)
        wide = src_ref[pl.ds(t, WIDE), :].astype(jnp.float32)
        dst[pl.ds(first + t, WIDE)] = wide.reshape(WIDE, group, LANES)
        return 0

    lax.fori_loop(0, rows // WIDE, move, 0)


def scatter_positions(src, dst_ref, group):
    rows = dst_ref.shape[0]

    def move(i, _):
        t = at_chunk(i, WIDE)
        wide = src[pl.ds(t, WIDE)].reshape(WIDE, group * LANES)
        dst_ref[pl.ds(t, WIDE), :] = wide.astype(dst_ref.dtype)
        return 0

    lax.fori_loop(0, rows // WIDE, move, 0)


def head_kernel(group, unroll, place_ref, len_ref, maps_ref, dt_ref, gy_ref, alog_ref, head_ref,
                keep_t, maps_t, step_t, gy_t, a2_s):
    rows = dt_ref.shape[0]
    states = alog_ref.shape[0]

    fill_keep(place_ref[0] * rows, len_ref, keep_t)
    fill_maps(maps_ref, maps_t)
    gather_positions(gy_ref, gy_t, group)
    gather_positions(dt_ref, step_t, group)
    a2_s[...] = (-LOG2E * jnp.exp(alog_ref[...])).reshape(states, group, LANES)

    def steps(i, total):
        t = at_chunk(i, CHUNK)
        step = jnp.log1p(jnp.exp(step_t[pl.ds(t, CHUNK)]))
        for k in range(CHUNK):
            one = step[k] + (1.0 - spread(keep_t, PAST + t + k, group)) * RESET_STEP
            step_t[t + k] = one
            total = total + one
        return total

    zero = jnp.zeros((group, LANES), jnp.float32)
    total = lax.fori_loop(0, rows // CHUNK, steps, zero)

    def token(i, cars):
        t = rows - 1 - i
        gy = gy_t[t]
        step = step_t[t]
        out = []
        for n in range(states):
            decay = jnp.exp2(step * a2_s[n])
            out.append(decay * (spread(maps_t, n * rows + t, group) * gy + cars[n]))
        return tuple(out)

    cars = lax.fori_loop(0, rows, token, (zero,) * states, unroll=unroll)
    for n in range(states):
        head_ref[n] = cars[n]
    head_ref[states] = total


def head_call(group, block, place, lengths, maps, dt, gy, alog):
    rows = dt.shape[0]
    states = alog.shape[0]
    width = group * LANES
    smem = pl.BlockSpec(memory_space=pltpu.SMEM)
    col = lambda i: (0, block)
    f32 = jnp.float32
    return pl.pallas_call(
        functools.partial(head_kernel, group, 8),
        grid=(1,),
        out_shape=jax.ShapeDtypeStruct((states + 1, group, LANES), f32),
        in_specs=[smem, smem, pl.BlockSpec((states, rows), lambda i: (1, 0)),
                  pl.BlockSpec((rows, width), col),
                  pl.BlockSpec((rows, width), col), pl.BlockSpec((states, width), col)],
        out_specs=pl.BlockSpec((states + 1, group, LANES), lambda i: (0, 0, 0)),
        scratch_shapes=[
            pltpu.VMEM((rows + 3 * PAST, LANES), f32),
            pltpu.VMEM((states * rows + 8, LANES), f32),
            pltpu.VMEM((rows, group, LANES), f32),
            pltpu.VMEM((rows, group, LANES), f32),
            pltpu.VMEM((states, group, LANES), f32),
        ],
        compiler_params=pltpu.CompilerParams(
            dimension_semantics=("arbitrary",), vmem_limit_bytes=HEAD_VMEM),
        cost_estimate=pl.CostEstimate(
            flops=rows * states * width * 1000, transcendentals=0,
            bytes_accessed=width * rows * states * 4),
        name="head",
    )(place, lengths, maps, dt, gy, alog)


def main_kernel(group, part, shards, place_ref, len_ref, maps_ref, x_ref, hist_ref, dt_ref, gy_ref,
                start_ref, alog_ref, cw_ref, cb_ref, sk_ref, next_ref, next2_ref, next3_ref, *rest):
    rest = rest[-24:]
    (gx_ref, gdt_ref, edge_ref, gp_ref, gm_ref,
     keep_t, maps_t, x_t, sig_t, gy_t, a2_s, small_s, start_s, gin_s,
     step_t, du_t, u_t, slope_t, w_t, v_t, gc_t, h_s, acc_s, gp_s) = rest
    rows = x_ref.shape[0]
    states = alog_ref.shape[0]
    f32 = jnp.float32
    zero = jnp.zeros((group, LANES), f32)

    fill_keep(place_ref[0] * rows, len_ref, keep_t)
    fill_maps(maps_ref, maps_t)
    gather_positions(x_ref, x_t, group, 3)
    gather_positions(gy_ref, gy_t, group)
    gather_positions(dt_ref, step_t, group)
    a2_s[...] = (-LOG2E * jnp.exp(alog_ref[...])).reshape(states, group, LANES)
    start_s[...] = start_ref[...].reshape(states, group, LANES)
    x_t[0:3] = hist_ref[...].astype(f32).reshape(3, group, LANES)
    small_s[0:4] = cw_ref[...].reshape(4, group, LANES)
    small_s[4:5] = cb_ref[...].reshape(1, group, LANES)
    small_s[5:6] = sk_ref[...].reshape(1, group, LANES)
    gc_t[0:3] = jnp.zeros((3, group, LANES), f32)
    gc_t[rows + 3:rows + 6] = jnp.zeros((3, group, LANES), f32)

    def keep_at(t):
        return spread(keep_t, PAST + t, group)

    def rows_of(i, _):
        t = at_chunk(i, CHUNK)
        for k in range(CHUNK):
            keep = keep_at(t + k)
            conv = keep_at(t + k - 2) * (small_s[0] * x_t[t + k])
            conv = keep_at(t + k - 1) * (small_s[1] * x_t[t + k + 1] + conv)
            conv = keep * (small_s[2] * x_t[t + k + 2] + conv)
            conv = small_s[4] + small_s[3] * x_t[t + k + 3] + conv
            sig = 1.0 / (1.0 + jnp.exp(-conv))
            u = conv * sig
            e = jnp.exp(step_t[t + k])
            step = jnp.log1p(e)
            step_t[t + k] = step + (1.0 - keep) * RESET_STEP
            du_t[t + k] = step * u
            u_t[t + k] = u
            sig_t[t + k] = e / (1.0 + e)
            slope_t[t + k] = sig * (1.0 + conv * (1.0 - sig))
            w_t[t + k] = step
        return 0

    lax.fori_loop(0, rows // CHUNK, rows_of, 0)

    last = shards - 1 - place_ref[0]
    for n in range(states):
        arrived = jnp.where(last >= 3, next3_ref[0, n], 0.0)
        for d, ref in ((2, next2_ref), (1, next_ref)):
            arrived = ref[0, n] + jnp.exp2(ref[0, states] * a2_s[n]) * arrived
            arrived = jnp.where(last >= d, arrived, 0.0)
        gin_s[n] = arrived

    def fold(p):
        out = p[0:8]
        for k in range(1, group // 8):
            out = out + p[k * 8:(k + 1) * 8]
        return out

    for lo in range(0, states, part):
        hi = lo + part

        for n in range(lo, hi):
            h_s[0, n - lo] = start_s[n]

        def forward(t, hs):
            step = step_t[t]
            du = du_t[t]
            out = []
            for n in range(lo, hi):
                decay = jnp.exp2(step * a2_s[n])
                h = decay * hs[n - lo] + spread(maps_t, n * rows + t, group) * du
                h_s[t + 1, n - lo] = h
                out.append(h)
            return tuple(out)

        lax.fori_loop(0, rows, forward, tuple(start_s[n] for n in range(lo, hi)), unroll=8)

        def backward(i, carry):
            cars, rates = carry
            t = rows - 1 - i
            step = step_t[t]
            du = du_t[t]
            y = gy_t[t]
            new_cars, new_rates = [], []
            w = None if lo == 0 else gc_t[t + 3]
            v = None if lo == 0 else v_t[t]
            for n in range(lo, hi):
                m = n - lo
                g = spread(maps_t, (states + n) * rows + t, group) * y + cars[m]
                acc_s[n, t] = fold(g * du)
                acc_s[states + n, t] = fold(h_s[t + 1, m] * y)
                bg = spread(maps_t, n * rows + t, group) * g
                w = bg if w is None else w + bg
                car = jnp.exp2(step * a2_s[n]) * g
                aq = a2_s[n] * (car * h_s[t, m])
                v = aq if v is None else v + aq
                new_cars.append(car)
                new_rates.append(rates[m] + step * aq)
            gc_t[t + 3] = w
            v_t[t] = v
            return tuple(new_cars), tuple(new_rates)

        _, rates = lax.fori_loop(
            0, rows, backward,
            (tuple(gin_s[n] for n in range(lo, hi)), (zero,) * part), unroll=4)
        for n in range(lo, hi):
            gp_s[n] = rates[n - lo] * LN2

    def finish(i, carry):
        taps = list(carry)
        t = at_chunk(rows // CHUNK - 1 - i, CHUNK)
        for k in range(CHUNK - 1, -1, -1):
            y = gy_t[t + k]
            u = u_t[t + k]
            w = gc_t[t + k + 3]
            grad_u = small_s[5] * y + w_t[t + k] * w
            v_t[t + k] = (u * w + LN2 * v_t[t + k]) * sig_t[t + k]
            gc = grad_u * slope_t[t + k]
            gc_t[t + k + 3] = gc
            x = small_s[0] * gc_t[t + k + 6] * keep_at(t + k + 3)
            x = (small_s[1] * gc_t[t + k + 5] + x) * keep_at(t + k + 2)
            x = (small_s[2] * gc_t[t + k + 4] + x) * keep_at(t + k + 1)
            w_t[t + k] = small_s[3] * gc + x
            e1 = keep_at(t + k) * gc
            e2 = keep_at(t + k - 1) * e1
            e3 = keep_at(t + k - 2) * e2
            taps[0] += e3 * x_t[t + k]
            taps[1] += e2 * x_t[t + k + 1]
            taps[2] += e1 * x_t[t + k + 2]
            taps[3] += gc * x_t[t + k + 3]
            taps[4] += y * u
            taps[5] += gc
        return tuple(taps)

    taps = lax.fori_loop(0, rows // CHUNK, finish, (zero,) * 6)
    for k in range(6):
        gp_s[states + k] = taps[k]
    for k in range(3):
        x = small_s[0] * gc_t[k + 3] * keep_at(k)
        x = (small_s[1] * gc_t[k + 2] + x) * keep_at(k - 1)
        x = (small_s[2] * gc_t[k + 1] + x) * keep_at(k - 2)
        small_s[6 + k] = x
    scatter_positions(w_t, gx_ref, group)
    scatter_positions(v_t, gdt_ref, group)
    edge_ref[0:3, :] = small_s[6:9].reshape(3, group * LANES)
    edge_ref[3:6, :] = w_t[rows - 3:rows].reshape(3, group * LANES)
    gp_ref[...] = gp_s[...].reshape(states + 6, group * LANES)

    def reduce_state(n, _):
        for tb in range(rows // 8):
            total = acc_s[n, tb * 8:tb * 8 + 8]
            maps_t[tb * 8:tb * 8 + 8, :] = jnp.sum(total, axis=1)
        flat = maps_t[0:rows, :].T
        gm_ref[pl.ds(n, 1), :] = jnp.sum(flat, axis=0, keepdims=True)
        return 0

    lax.fori_loop(0, 2 * states, reduce_state, 0)


def main_call(group, part, shards, block, place, lengths, maps, x, hist, dt, gy, start, alog, cw,
              cb, sk, heads, gdt):
    rows, channels = x.shape
    states = alog.shape[0]
    width = group * LANES
    smem = pl.BlockSpec(memory_space=pltpu.SMEM)
    col = lambda i, p: (0, block)
    f32 = jnp.float32
    table = pltpu.VMEM((rows, group, LANES), f32)
    vectors = pltpu.VMEM((states, group, LANES), f32)

    def later(d):
        return pl.BlockSpec((1, states + 1, group, LANES),
                            lambda i, p: (jnp.minimum(p[0] + d, shards - 1), 0, 0, 0))

    operands = [place, lengths, maps, x, hist, dt, gy, start, alog, cw, cb, sk, heads, heads, heads]
    in_specs = [smem, pl.BlockSpec((2 * states, rows), lambda i, p: (0, 0)),
                pl.BlockSpec((rows, width), col),
                pl.BlockSpec((3, width), col),
                pl.BlockSpec((rows, width), col),
                pl.BlockSpec((rows, width), col),
                pl.BlockSpec((states, width), col),
                pl.BlockSpec((states, width), col),
                pl.BlockSpec((4, width), col),
                pl.BlockSpec((1, width), col),
                pl.BlockSpec((1, width), col),
                later(1), later(2), later(3)]
    aliases = {}
    if gdt is not None:
        aliases = {len(operands): 1}
        operands.append(gdt)
        in_specs.append(pl.BlockSpec(memory_space=pl.ANY))
    return pl.pallas_call(
        functools.partial(main_kernel, group, part, shards),
        out_shape=(
            jax.ShapeDtypeStruct((rows, width), jnp.bfloat16),
            jax.ShapeDtypeStruct((rows, channels), jnp.bfloat16),
            jax.ShapeDtypeStruct((6, width), f32),
            jax.ShapeDtypeStruct((states + 6, width), f32),
            jax.ShapeDtypeStruct((2 * states, rows), f32),
        ),
        grid_spec=pltpu.PrefetchScalarGridSpec(
            num_scalar_prefetch=1,
            grid=(1,),
            in_specs=in_specs,
            out_specs=(pl.BlockSpec((rows, width), lambda i, p: (0, 0)),
                       pl.BlockSpec((rows, width), col),
                       pl.BlockSpec((6, width), lambda i, p: (0, 0)),
                       pl.BlockSpec((states + 6, width), lambda i, p: (0, 0)),
                       pl.BlockSpec((2 * states, rows), lambda i, p: (0, 0))),
            scratch_shapes=[
                pltpu.VMEM((rows + 3 * PAST, LANES), f32),
                pltpu.VMEM((2 * states * rows + 8, LANES), f32),
                pltpu.VMEM((rows + 3, group, LANES), f32),
                table, table,
                vectors,
                pltpu.VMEM((9, group, LANES), f32),
                vectors, vectors,
                table, table, table, table, table, table,
                pltpu.VMEM((rows + 6, group, LANES), f32),
                pltpu.VMEM((rows + 1, part, group, LANES), f32),
                pltpu.VMEM((2 * states, rows, 8, LANES), f32),
                pltpu.VMEM((states + 6, group, LANES), f32),
            ]),
        input_output_aliases=aliases,
        compiler_params=pltpu.CompilerParams(
            dimension_semantics=("arbitrary",), vmem_limit_bytes=MAIN_VMEM),
        cost_estimate=pl.CostEstimate(
            flops=rows * states * width * 5000, transcendentals=0,
            bytes_accessed=width * rows * states * 18),
        name="main",
    )(*operands)


def on_device(inner_x, dt_raw, grad_out, state_maps, saved_states, a_log, conv_weight, conv_bias,
              skip_gain, doc_lengths):
    rows = inner_x.shape[1]
    channels = inner_x.shape[2]
    states = a_log.shape[1]
    shards = lax.axis_size("ctx")
    sections = lax.axis_size("pipe")
    group = 16
    width = group * LANES
    blocks = channels // width
    me = lax.axis_index("ctx").astype(jnp.int32)
    place = me.reshape(1)
    maps = state_maps[0].reshape(2 * states, rows)
    x, dt, gy = inner_x[0], dt_raw[0], grad_out[0]
    hist = shift_to(x[rows - 3:], "ctx", 1)

    def after(value, *earlier):
        return lax.optimization_barrier((value,) + earlier)[0]

    own, heads = [], []
    for b in range(blocks):
        here = after(place, hist) if b == min(2, blocks - 1) else place
        own.append(head_call(group, b, here, doc_lengths, maps, dt, gy, a_log[0]))
        heads.append(lax.all_gather(own[-1], "ctx"))
    ready = after(place, *own)

    gdt = None
    maps_sum = 0.0
    arrived, edges, shares = [], [], []
    for b in range(blocks):
        here = after(ready, *arrived[:-1], *shares[:-1]) if b == blocks - 1 else ready
        gx, gdt, edge, gp, gm = main_call(
            group, 8, shards, b, here, doc_lengths, maps, x, hist, dt, gy, saved_states[0, 0],
            a_log[0], conv_weight[0], conv_bias, skip_gain, heads[b], gdt)
        arrived.append(shift_to(gx, "pipe", -1))
        if b > 0:
            gp = after(gp, shares[b - 1])
        shares.append(lax.psum(gp, "ctx"))
        edges.append(edge)
        maps_sum = maps_sum + gm
    if blocks > 1:
        edges[-1] = after(edges[-1], arrived[-2])

    edge = jnp.concatenate(edges, 1)
    mine = shift_to(edge[3:], "pipe", -1)
    pairs = [(s * shards + k, (s - 1) * shards + k - 1)
             for s in range(1, sections) for k in range(1, shards)]
    spilled = lax.ppermute(edge[:3], ("pipe", "ctx"), pairs)
    tail = (mine + spilled).astype(jnp.bfloat16)
    upstream = jnp.concatenate(arrived, 1)
    upstream = lax.dynamic_update_slice(upstream, tail, (rows - 3, 0))
    share = channels // shards
    params = lax.dynamic_slice_in_dim(jnp.concatenate(shares, 1), me * share, share, 1)
    return upstream[None], gdt[None], maps_sum.reshape(1, 2, states, rows), params[None]


def solution(mesh):
    in_specs = (
        P("pipe", "ctx", None),
        P("pipe", "ctx", None),
        P("pipe", "ctx", None),
        P("pipe", None, None, "ctx"),
        P("pipe", "ctx", None, None),
        P("pipe", None, None),
        P("pipe", None, None),
        P("pipe", None),
        P("pipe", None),
        P("pipe", None),
    )
    out_specs = (
        P("pipe", "ctx", None),
        P("pipe", "ctx", None),
        P("pipe", None, None, "ctx"),
        P("pipe", None, "ctx"),
    )
    return jax.shard_map(
        on_device, mesh=mesh, in_specs=in_specs, out_specs=out_specs, check_vma=False
    )
```

time: 1440 us -> 349 us (0.24)
  other arithmetic: 983 us -> 2.78 us
  local copies, waits for them, and re-layouts: 306 us -> 6.28 us
  Pallas kernels: 0 us -> 134 us
  waiting for transfers between devices: 41.2 us -> 165 us
  loops' own time: 64 us -> 0 us
    reduce_sum x146 -> x0, other arithmetic: 595 us -> none  [the longest x64 325 us: backward_block(): grads_c[t] = jnp.sum(afters[t] * y_blk[t][None, :], axis=1)]
    add x67 -> x1, other arithmetic: 234 us -> 1.33 us  [on_device(): maps_sum = maps_sum + gm]
    pallas_call x0 -> x8, Pallas kernels: none -> 134 us  [the longest x4 107 us: main_call(): pl.pallas_call(functools.partial(main_kernel, group, part, shards), out_s...]
    dynamic_slice x176 -> x0, local copies, waits for them, and re-layouts: 124 us -> none  [the longest x128 85.2 us: cut(): return lax.dynamic_slice_in_dim(array, index * block, block, 0)]
    mul x35 -> x0, other arithmetic: 122 us -> none  [the longest x16 61 us: backward_block(): state = decay * state + (step_b[t] * act_b[t])[None, :] * b_blk[t][:, None]]
    psum x0 -> x4, waiting for transfers between devices: none -> 119 us  [on_device(): shares.append(lax.psum(gp, 'ctx'))]
    another operation x4 -> x0, loops' own time: 64 us -> none  [the longest x1 42.3 us: on_device(): lax.scan(backward_block, (incoming, zeros_state), jnp.arange(blocks), rev...]
    slice x52 -> x2, local copies, waits for them, and re-layouts: 59.9 us -> 1 us  [the longest x1 0.94 us: on_device(): hist = shift_to(x[rows - 3:], 'ctx', 1)]
  transfers between devices with their start and end apart: 6 -> 15, of which waited for: 2 -> 6; matrix products, arithmetic and copies ran while one was open for 22% -> 2% of each run, Pallas kernels for 0% -> 37%
where the time goes in v2:
time: 349 us; the launch traced here: 344 us
  waiting for transfers between devices  165 us (47%)
  Pallas kernels  134 us (38%)
  starting transfers between devices  21.8 us (6%)
  between operations  14.4 us (4%)
  local copies, waits for them, and re-layouts  6.28 us (2%)
    psum x4, waiting for transfers between devices, on_device(): shares.append(lax.psum(gp, 'ctx'))  119 us
    pallas_call x4, Pallas kernels, main_call(): pl.pallas_call(functools.partial(main_kernel, group, part, shards), out_s...  107 us
    all_gather x4, waiting for transfers between devices, on_device(): heads.append(lax.all_gather(own[-1], 'ctx'))  44.6 us
    pallas_call x4, Pallas kernels, head_call(): pl.pallas_call(functools.partial(head_kernel, group, 8), grid=(1,), out_s...  26.8 us
    ppermute x6, starting transfers between devices, shift_to(): return lax.ppermute(x, axis, pairs)  17.4 us
  transfers between devices with their start and end apart: 15, of which 6 were waited for; matrix products, arithmetic and copies ran while one was open for 2% of the time, Pallas kernels for 37%

profile of v2, /device:TPU:13, one launch (start us, length us, event | category | flops | bytes accessed | tf_op | source)
XLA Modules:
  0.0 344.0 jit_solution(15573362506475288046)
XLA Ops:
  7.2 6.7 %head.4 = f32[17,16,128]{2,1,0:T(8,128)} custom-call(s32[1]{0:T(128)} %bitcast.place_ref, s32[1,8]{1,0:T(1,128)} %len_ref.15, f32[32,128]{1,0:T(8,128)} %bitcast.69, bf16[128,8192]{1,0:T(8,128)(2,1)} %bitcast.25, bf16[128,8192]{1,0:T(8,128)(2,1)} %bitcast.33, f32[16,8192]{1,0:T(8,128)} %bitcast.57), custom_call_target="tpu_custom_call" | custom-call | flops 4194304000 | bytes 16777216 | tf_op jit(solution)/shard_map/head/pallas_call | solution.py:127
  14.9 3.8 %collective-permute-start = (bf16[3,8192]{1,0:T(4,128)(2,1)S(1)}, bf16[3,8192]{1,0:T(4,128)(2,1)S(1)}, u32[]{:S(2)}, u32[]{:S(2)}) collective-permute-start(bf16[3,8192]{1,0:T(4,128)(2,1)S(1)} %slice_bitcast_fusion), channel_id=1, source_target_pairs={{0,1},{1,2},{2,3},{3,4},{4,5},{5,6},{6,7},{8,9},{9,10},{10,11},{11... | collective-permute-start | bytes 147464 | tf_op jit(solution)/shard_map/ppermute | solution.py:26
  18.7 6.7 %head.5 = f32[17,16,128]{2,1,0:T(8,128)} custom-call(s32[1]{0:T(128)} %bitcast.place_ref, s32[1,8]{1,0:T(1,128)} %len_ref.15, f32[32,128]{1,0:T(8,128)} %bitcast.70, bf16[128,8192]{1,0:T(8,128)(2,1)} %bitcast.26, bf16[128,8192]{1,0:T(8,128)(2,1)} %bitcast.34, f32[16,8192]{1,0:T(8,128)} %bitcast.58), custom_call_target="tpu_custom_call" | custom-call | flops 4194304000 | bytes 16777216 | tf_op jit(solution)/shard_map/head/pallas_call | solution.py:127
  25.5 6.7 %head.7 = f32[17,16,128]{2,1,0:T(8,128)} custom-call(s32[1]{0:T(128)} %bitcast.place_ref, s32[1,8]{1,0:T(1,128)} %len_ref.15, f32[32,128]{1,0:T(8,128)} %bitcast.71, bf16[128,8192]{1,0:T(8,128)(2,1)} %bitcast.27, bf16[128,8192]{1,0:T(8,128)(2,1)} %bitcast.35, f32[16,8192]{1,0:T(8,128)} %bitcast.59), custom_call_target="tpu_custom_call" | custom-call | flops 4194304000 | bytes 16777216 | tf_op jit(solution)/shard_map/head/pallas_call | solution.py:127
  32.2 6.7 %head.6 = f32[17,16,128]{2,1,0:T(8,128)} custom-call(s32[1]{0:T(128)} %bitcast.place_ref, s32[1,8]{1,0:T(1,128)} %len_ref.15, f32[32,128]{1,0:T(8,128)} %bitcast.72, bf16[128,8192]{1,0:T(8,128)(2,1)} %bitcast.28, bf16[128,8192]{1,0:T(8,128)(2,1)} %bitcast.36, f32[16,8192]{1,0:T(8,128)} %bitcast.60), custom_call_target="tpu_custom_call" | custom-call | flops 4194304000 | bytes 16777216 | tf_op jit(solution)/shard_map/head/pallas_call | solution.py:127
  38.9 26.7 %main.4 = (bf16[128,2048]{1,0:T(8,128)(2,1)}, bf16[128,8192]{1,0:T(8,128)(2,1)}, f32[6,2048]{1,0:T(8,128)}, f32[22,2048]{1,0:T(8,128)}, f32[32,128]{1,0:T(8,128)}) custom-call(s32[1]{0:T(128)} %bitcast.place_ref, s32[1,8]{1,0:T(1,128)} %len_ref.15, f32[32,128]{1,0:T(8,128)} %bitcast.73, bf16[128,8192]{1,0:T(8,128)(2,1)} %bitcast.21, ...), custom_call_target="tpu_custom_call" | custom-call | flops 20971520000 | bytes 75497472 | tf_op jit(solution)/shard_map/main/pallas_call | solution.py:348
  66.3 26.8 %main.5 = (bf16[128,2048]{1,0:T(8,128)(2,1)}, bf16[128,8192]{1,0:T(8,128)(2,1)}, f32[6,2048]{1,0:T(8,128)}, f32[22,2048]{1,0:T(8,128)}, f32[32,128]{1,0:T(8,128)}) custom-call(s32[1]{0:T(128)} %bitcast.place_ref, s32[1,8]{1,0:T(1,128)} %len_ref.15, f32[32,128]{1,0:T(8,128)} %bitcast.74, ...), custom_call_target="tpu_custom_call", output_to_operand_aliasing={{1}: (15, {})} | custom-call | flops 20971520000 | bytes 75497472 | tf_op jit(solution)/shard_map/main/pallas_call | solution.py:348
  93.1 24.6 %all-reduce.5.cloned.1.call-done = f32[22,2048]{1,0:T(8,128)} async-done(((f32[22,2048]{1,0:T(8,128)}), f32[22,2048]{1,0:T(8,128)}) %all-reduce.5.cloned.1.call-update) | async-done | bytes 180240 | tf_op jit(solution)/shard_map/psum | solution.py:427
  118.4 3.1 collective-permute-start.2
  121.5 2.2 collective-permute-start.1
  124.5 19.0 %all-gather.13.cloned.1.call-done = f32[136,16,128]{2,1,0:T(8,128)} async-done(((f32[17,16,128]{2,1,0:T(8,128)}), f32[136,16,128]{2,1,0:T(8,128)}) %all-gather.13.cloned.1.call-update) | async-done | bytes 1114128 | tf_op jit(solution)/shard_map/all_gather | solution.py:413
  143.5 26.7 %main.6 = (bf16[128,2048]{1,0:T(8,128)(2,1)}, bf16[128,8192]{1,0:T(8,128)(2,1)}, f32[6,2048]{1,0:T(8,128)}, f32[22,2048]{1,0:T(8,128)}, f32[32,128]{1,0:T(8,128)}) custom-call(s32[1]{0:T(128)} %bitcast.place_ref, s32[1,8]{1,0:T(1,128)} %len_ref.15, f32[32,128]{1,0:T(8,128)} %bitcast.75, ...), custom_call_target="tpu_custom_call", output_to_operand_aliasing={{1}: (15, {})} | custom-call | flops 20971520000 | bytes 75497472 | tf_op jit(solution)/shard_map/main/pallas_call | solution.py:348
  170.3 3.1 collective-permute-start.3
  174.2 23.1 %all-reduce.7.cloned.1.call-done = f32[22,2048]{1,0:T(8,128)} async-done(((f32[22,2048]{1,0:T(8,128)}), f32[22,2048]{1,0:T(8,128)}) %all-reduce.7.cloned.1.call-update) | async-done | bytes 180240 | tf_op jit(solution)/shard_map/psum | solution.py:427
  197.4 25.6 %all-gather.15.cloned.1.call-done = f32[136,16,128]{2,1,0:T(8,128)} async-done(((f32[17,16,128]{2,1,0:T(8,128)}), f32[136,16,128]{2,1,0:T(8,128)}) %all-gather.15.cloned.1.call-update) | async-done | bytes 1114128 | tf_op jit(solution)/shard_map/all_gather | solution.py:413
  223.0 26.8 %main.7 = (bf16[128,2048]{1,0:T(8,128)(2,1)}, bf16[128,8192]{1,0:T(8,128)(2,1)}, f32[6,2048]{1,0:T(8,128)}, f32[22,2048]{1,0:T(8,128)}, f32[32,128]{1,0:T(8,128)}) custom-call(s32[1]{0:T(128)} %bitcast.place_ref, s32[1,8]{1,0:T(1,128)} %len_ref.15, f32[32,128]{1,0:T(8,128)} %bitcast.76, ...), custom_call_target="tpu_custom_call", output_to_operand_aliasing={{1}: (15, {})} | custom-call | flops 20971520000 | bytes 75497472 | tf_op jit(solution)/shard_map/main/pallas_call | solution.py:348
  249.8 27.1 %all-reduce.9.cloned.1.call-done = f32[22,2048]{1,0:T(8,128)} async-done(((f32[22,2048]{1,0:T(8,128)}), f32[22,2048]{1,0:T(8,128)}) %all-reduce.9.cloned.1.call-update) | async-done | bytes 180240 | tf_op jit(solution)/shard_map/psum | solution.py:427
  276.9 3.1 collective-permute-start.4
  280.0 1.3 add_add_fusion
  282.3 2.2 collective-permute-start.5
  284.5 4.1 %collective-permute-start.6 = (f32[3,8192]{1,0:T(4,128)S(1)}, f32[3,8192]{1,0:T(4,128)S(1)}, u32[]{:S(2)}, u32[]{:S(2)}) collective-permute-start(f32[3,8192]{1,0:T(4,128)S(1)} %get-tuple-element.58), channel_id=1, source_target_pairs={{9,0},{10,1},{11,2},{12,3},{13,4},{14,5},{15,6},{17,8},{18,9},{19,... | collective-permute-start | bytes 294920 | tf_op jit(solution)/shard_map/ppermute | solution.py:437
  288.6 44.4 %all-reduce.11.cloned.1.call-done = f32[22,2048]{1,0:T(8,128)} async-done(((f32[22,2048]{1,0:T(8,128)}), f32[22,2048]{1,0:T(8,128)}) %all-reduce.11.cloned.1.call-update) | async-done | bytes 180240 | tf_op jit(solution)/shard_map/psum | solution.py:427
  333.8 1.4 maximum_bitcast_fusion
  335.8 1.3 copy-done
  (54 shorter events, 6.5 us)
Async XLA Ops:
  7.2 31.7 %all-gather.9.cloned.1.call-start = ((), (), s32[]{:S(2)}) async-start(), calls=%async_computation.4 | async-start | bytes 1253376 | tf_op jit(solution)/shard_map/all_gather | solution.py:413
  13.9 52.3 %all-gather.11.cloned.1.call-start = ((), (), s32[]{:S(2)}) async-start(), calls=%async_computation.5 | async-start | bytes 1253376 | tf_op jit(solution)/shard_map/all_gather | solution.py:413
  14.9 17.2 %collective-permute-start = (bf16[3,8192]{1,0:T(4,128)(2,1)S(1)}, bf16[3,8192]{1,0:T(4,128)(2,1)S(1)}, u32[]{:S(2)}, u32[]{:S(2)}) collective-permute-start(bf16[3,8192]{1,0:T(4,128)(2,1)S(1)} %slice_bitcast_fusion), channel_id=1, source_target_pairs={{0,1},{1,2},{2,3},{3,4},{4,5},{5,6},{6,7},{8,9},{9,10},{10,11},{11... | collective-permute-start | bytes 147464 | tf_op jit(solution)/shard_map/ppermute | solution.py:26
  25.4 92.3 %all-reduce.5.cloned.1.call-start = ((), (), s32[]{:S(2)}) async-start(), calls=%async_computation | async-start | bytes 393216 | tf_op jit(solution)/shard_map/psum | solution.py:427
  32.2 6.7 %copy-start.9 = (bf16[3,8192]{1,0:T(4,128)(2,1)}, bf16[3,8192]{1,0:T(4,128)(2,1)S(1)}, u32[]{:S(2)}) copy-start(bf16[3,8192]{1,0:T(4,128)(2,1)S(1)} %collective-permute-done.hist_ref) | copy-start | bytes 147460
  65.6 77.9 %all-gather.13.cloned.1.call-start = ((), (), s32[]{:S(2)}) async-start(), calls=%async_computation.6 | async-start | bytes 1253376 | tf_op jit(solution)/shard_map/all_gather | solution.py:413
  66.2 131.1 %all-reduce.7.cloned.1.call-start = ((), (), s32[]{:S(2)}) async-start(), calls=%async_computation.1 | async-start | bytes 393216 | tf_op jit(solution)/shard_map/psum | solution.py:427
  66.3 55.2 %copy-start.8 = (bf16[128,2048]{1,0:T(8,128)(2,1)S(1)}, bf16[128,2048]{1,0:T(8,128)(2,1)}, u32[]{:S(2)}) copy-start(bf16[128,2048]{1,0:T(8,128)(2,1)} %get-tuple-element.33) | copy-start | bytes 1572868
  66.3 57.4 %copy-start.4 = (f32[6,2048]{1,0:T(8,128)S(1)}, f32[6,2048]{1,0:T(8,128)}, u32[]{:S(2)}) copy-start(f32[6,2048]{1,0:T(8,128)} %get-tuple-element.44) | copy-start | bytes 147460
  117.7 105.3 %all-gather.15.cloned.1.call-start = ((), (), s32[]{:S(2)}) async-start(), calls=%async_computation.7 | async-start | bytes 1253376 | tf_op jit(solution)/shard_map/all_gather | solution.py:413
  118.3 158.6 %all-reduce.9.cloned.1.call-start = ((), (), s32[]{:S(2)}) async-start(), calls=%async_computation.2 | async-start | bytes 393216 | tf_op jit(solution)/shard_map/psum | solution.py:427
  118.4 79.0 %collective-permute-start.2 = (bf16[128,2048]{1,0:T(8,128)(2,1)}, bf16[128,2048]{1,0:T(8,128)(2,1)S(1)}, u32[]{:S(2)}, u32[]{:S(2)}) collective-permute-start(bf16[128,2048]{1,0:T(8,128)(2,1)} %get-tuple-element.35), channel_id=1, source_target_pairs={{8,0},{16,8},{24,16},{9,1},{17,9},{25,17},{10,2},{18,10},{26,18},{... | collective-permute-start | bytes 1572872 | tf_op jit(solution)/shard_map/ppermute | solution.py:26
  121.5 75.9 %collective-permute-start.1 = (bf16[128,2048]{1,0:T(8,128)(2,1)S(1)}, bf16[128,2048]{1,0:T(8,128)(2,1)S(1)}, u32[]{:S(2)}, u32[]{:S(2)}) collective-permute-start(bf16[128,2048]{1,0:T(8,128)(2,1)S(1)} %copy-done.8), channel_id=1, source_target_pairs={{8,0},{16,8},{24,16},{9,1},{17,9},{25,17},{10,2},{18,10},{26,18},{... | collective-permute-start | bytes 1572872 | tf_op jit(solution)/shard_map/ppermute | solution.py:26
  170.3 111.1 %collective-permute-start.3 = (bf16[128,2048]{1,0:T(8,128)(2,1)}, bf16[128,2048]{1,0:T(8,128)(2,1)S(1)}, u32[]{:S(2)}, u32[]{:S(2)}) collective-permute-start(bf16[128,2048]{1,0:T(8,128)(2,1)} %get-tuple-element.37), channel_id=1, source_target_pairs={{8,0},{16,8},{24,16},{9,1},{17,9},{25,17},{10,2},{18,10},{26,18},{... | collective-permute-start | bytes 1572872 | tf_op jit(solution)/shard_map/ppermute | solution.py:26
  197.3 135.6 %all-reduce.11.cloned.1.call-start = ((), (), s32[]{:S(2)}) async-start(), calls=%async_computation.3 | async-start | bytes 393216 | tf_op jit(solution)/shard_map/psum | solution.py:427
  223.0 57.0 %copy-start.5 = (f32[32,128]{1,0:T(8,128)S(1)}, f32[32,128]{1,0:T(8,128)}, u32[]{:S(2)}) copy-start(f32[32,128]{1,0:T(8,128)} %get-tuple-element.50) | copy-start | bytes 49156
  223.0 57.0 %copy-start.6 = (f32[32,128]{1,0:T(8,128)S(1)}, f32[32,128]{1,0:T(8,128)}, u32[]{:S(2)}) copy-start(f32[32,128]{1,0:T(8,128)} %get-tuple-element.51) | copy-start | bytes 49156
  223.0 57.0 %copy-start.7 = (f32[32,128]{1,0:T(8,128)S(1)}, f32[32,128]{1,0:T(8,128)}, u32[]{:S(2)}) copy-start(f32[32,128]{1,0:T(8,128)} %get-tuple-element.52) | copy-start | bytes 49156
  223.0 110.0 %copy-start.2 = (f32[22,2048]{1,0:T(8,128)S(1)}, f32[22,2048]{1,0:T(8,128)}, u32[]{:S(2)}) copy-start(f32[22,2048]{1,0:T(8,128)} %all-reduce.5.cloned.1.call-done) | copy-start | bytes 540676
  223.0 110.0 %copy-start.3 = (f32[22,2048]{1,0:T(8,128)S(1)}, f32[22,2048]{1,0:T(8,128)}, u32[]{:S(2)}) copy-start(f32[22,2048]{1,0:T(8,128)} %all-reduce.7.cloned.1.call-done) | copy-start | bytes 540676
  276.9 56.9 %collective-permute-start.4 = (bf16[128,2048]{1,0:T(8,128)(2,1)}, bf16[128,2048]{1,0:T(8,128)(2,1)}, u32[]{:S(2)}, u32[]{:S(2)}) collective-permute-start(bf16[128,2048]{1,0:T(8,128)(2,1)} %get-tuple-element.43), channel_id=1, source_target_pairs={{8,0},{16,8},{24,16},{9,1},{17,9},{25,17},{10,2},{18,10},{26,18},{... | collective-permute-start | bytes 1572872 | tf_op jit(solution)/shard_map/ppermute | solution.py:26
  281.4 52.4 %copy-start.1 = (bf16[128,2048]{1,0:T(8,128)(2,1)}, bf16[128,2048]{1,0:T(8,128)(2,1)S(1)}, u32[]{:S(2)}) copy-start(bf16[128,2048]{1,0:T(8,128)(2,1)S(1)} %collective-permute-done.3) | copy-start | bytes 1572868
  282.3 51.4 %collective-permute-start.5 = (f32[3,8192]{1,0:T(4,128)S(1)}, f32[3,8192]{1,0:T(4,128)S(1)}, u32[]{:S(2)}, u32[]{:S(2)}) collective-permute-start(f32[3,8192]{1,0:T(4,128)S(1)} %get-tuple-element.59), channel_id=1, source_target_pairs={{8,0},{16,8},{24,16},{9,1},{17,9},{25,17},{10,2},{18,10},{26,18},{... | collective-permute-start | bytes 294920 | tf_op jit(solution)/shard_map/ppermute | solution.py:26
  284.5 49.2 %collective-permute-start.6 = (f32[3,8192]{1,0:T(4,128)S(1)}, f32[3,8192]{1,0:T(4,128)S(1)}, u32[]{:S(2)}, u32[]{:S(2)}) collective-permute-start(f32[3,8192]{1,0:T(4,128)S(1)} %get-tuple-element.58), channel_id=1, source_target_pairs={{9,0},{10,1},{11,2},{12,3},{13,4},{14,5},{15,6},{17,8},{18,9},{19,... | collective-permute-start | bytes 294920 | tf_op jit(solution)/shard_map/ppermute | solution.py:437
  (1 other events, 1.3 us)
Sparse Core Ops, SparseCore 0:
  14.1 23.9 all-gather.8
  39.7 22.0 all-gather.10
  65.8 51.9 all-reduce.4
  119.3 24.1 all-gather.12
  145.8 51.4 all-reduce.6
  198.8 24.1 all-gather.14
  225.3 51.5 all-reduce.8
  279.3 53.6 all-reduce.10

commit v3 on v2

--- a/solution.py
+++ b/solution.py
@@ -26,6 +26,10 @@
     return lax.ppermute(x, axis, pairs)
 
 
+def after(value, *earlier):
+    return lax.optimization_barrier((value,) + earlier)[0]
+
+
 def at_chunk(i, size):
     return pl.multiple_of(i * size, size)
 
@@ -83,8 +87,11 @@
     rows = dt_ref.shape[0]
     states = alog_ref.shape[0]
 
-    fill_keep(place_ref[0] * rows, len_ref, keep_t)
-    fill_maps(maps_ref, maps_t)
+    @pl.when(pl.program_id(0) == 0)
+    def _():
+        fill_keep(place_ref[0] * rows, len_ref, keep_t)
+        fill_maps(maps_ref, maps_t)
+
     gather_positions(gy_ref, gy_t, group)
     gather_positions(dt_ref, step_t, group)
     a2_s[...] = (-LOG2E * jnp.exp(alog_ref[...])).reshape(states, group, LANES)
@@ -113,25 +120,25 @@
 
     cars = lax.fori_loop(0, rows, token, (zero,) * states, unroll=unroll)
     for n in range(states):
-        head_ref[n] = cars[n]
-    head_ref[states] = total
-
-
-def head_call(group, block, place, lengths, maps, dt, gy, alog):
+        head_ref[0, n] = cars[n]
+    head_ref[0, states] = total
+
+
+def head_call(group, block, blocks, place, lengths, maps, dt, gy, alog):
     rows = dt.shape[0]
     states = alog.shape[0]
     width = group * LANES
     smem = pl.BlockSpec(memory_space=pltpu.SMEM)
-    col = lambda i: (0, block)
+    col = lambda i: (0, block + i)
     f32 = jnp.float32
     return pl.pallas_call(
         functools.partial(head_kernel, group, 8),
-        grid=(1,),
-        out_shape=jax.ShapeDtypeStruct((states + 1, group, LANES), f32),
+        grid=(blocks,),
+        out_shape=jax.ShapeDtypeStruct((blocks, states + 1, group, LANES), f32),
         in_specs=[smem, smem, pl.BlockSpec((states, rows), lambda i: (1, 0)),
                   pl.BlockSpec((rows, width), col),
                   pl.BlockSpec((rows, width), col), pl.BlockSpec((states, width), col)],
-        out_specs=pl.BlockSpec((states + 1, group, LANES), lambda i: (0, 0, 0)),
+        out_specs=pl.BlockSpec((1, states + 1, group, LANES), lambda i: (i, 0, 0, 0)),
         scratch_shapes=[
             pltpu.VMEM((rows + 3 * PAST, LANES), f32),
             pltpu.VMEM((states * rows + 8, LANES), f32),
@@ -142,16 +149,17 @@
         compiler_params=pltpu.CompilerParams(
             dimension_semantics=("arbitrary",), vmem_limit_bytes=HEAD_VMEM),
         cost_estimate=pl.CostEstimate(
-            flops=rows * states * width * 1000, transcendentals=0,
-            bytes_accessed=width * rows * states * 4),
+            flops=blocks * rows * states * width * 1000, transcendentals=0,
+            bytes_accessed=blocks * width * rows * states * 4),
         name="head",
     )(place, lengths, maps, dt, gy, alog)
 
 
 def main_kernel(group, part, shards, place_ref, len_ref, maps_ref, x_ref, hist_ref, dt_ref, gy_ref,
                 start_ref, alog_ref, cw_ref, cb_ref, sk_ref, next_ref, next2_ref, next3_ref, *rest):
-    rest = rest[-24:]
-    (gx_ref, gdt_ref, edge_ref, gp_ref, gm_ref,
+    maps_before = rest[-26] if len(rest) > 25 else None
+    rest = rest[-25:]
+    (gx_ref, gdt_ref, mine_ref, spill_ref, gp_ref, gm_ref,
      keep_t, maps_t, x_t, sig_t, gy_t, a2_s, small_s, start_s, gin_s,
      step_t, du_t, u_t, slope_t, w_t, v_t, gc_t, h_s, acc_s, gp_s) = rest
     rows = x_ref.shape[0]
@@ -298,23 +306,39 @@
         small_s[6 + k] = x
     scatter_positions(w_t, gx_ref, group)
     scatter_positions(v_t, gdt_ref, group)
-    edge_ref[0:3, :] = small_s[6:9].reshape(3, group * LANES)
-    edge_ref[3:6, :] = w_t[rows - 3:rows].reshape(3, group * LANES)
+    mine_ref[...] = w_t[rows - 3:rows].reshape(3, group * LANES)
+    spill_ref[...] = small_s[6:9].reshape(3, group * LANES)
     gp_ref[...] = gp_s[...].reshape(states + 6, group * LANES)
 
-    def reduce_state(n, _):
+    sub = lax.broadcasted_iota(jnp.int32, (8, LANES), 0)
+
+    def pair_up(parts, shift):
+        low = (sub & shift) == 0
+        return [jnp.where(low, a, b) + pltpu.roll(jnp.where(low, b, a), shift, 0)
+                for a, b in zip(parts[::2], parts[1::2])]
+
+    def add_sublanes(n, _):
         for tb in range(rows // 8):
-            total = acc_s[n, tb * 8:tb * 8 + 8]
-            maps_t[tb * 8:tb * 8 + 8, :] = jnp.sum(total, axis=1)
-        flat = maps_t[0:rows, :].T
-        gm_ref[pl.ds(n, 1), :] = jnp.sum(flat, axis=0, keepdims=True)
+            parts = [acc_s[n, tb * 8 + k] for k in range(8)]
+            for shift in (1, 2, 4):
+                parts = pair_up(parts, shift)
+            maps_t[pl.ds(n * rows + tb * 8, 8), :] = parts[0]
         return 0
 
-    lax.fori_loop(0, 2 * states, reduce_state, 0)
+    def add_lanes(n, _):
+        flat = maps_t[pl.ds(at_chunk(n, rows), rows), :].T
+        total = jnp.sum(flat, axis=0, keepdims=True)
+        if maps_before is not None:
+            total = total + maps_before[pl.ds(n, 1), :]
+        gm_ref[pl.ds(n, 1), :] = total
+        return 0
+
+    lax.fori_loop(0, 2 * states, add_sublanes, 0)
+    lax.fori_loop(0, 2 * states, add_lanes, 0, unroll=4)
 
 
 def main_call(group, part, shards, block, place, lengths, maps, x, hist, dt, gy, start, alog, cw,
-              cb, sk, heads, gdt):
+              cb, sk, heads, carried):
     rows, channels = x.shape
     states = alog.shape[0]
     width = group * LANES
@@ -341,17 +365,19 @@
                 pl.BlockSpec((1, width), col),
                 later(1), later(2), later(3)]
     aliases = {}
-    if gdt is not None:
-        aliases = {len(operands): 1}
-        operands.append(gdt)
-        in_specs.append(pl.BlockSpec(memory_space=pl.ANY))
+    if carried is not None:
+        aliases = {len(operands) + k: k + 1 for k in range(len(carried))}
+        operands += carried
+        in_specs += [pl.BlockSpec(memory_space=pl.ANY)] * (len(carried) - 1)
+        in_specs.append(pl.BlockSpec((2 * states, rows), lambda i, p: (0, 0)))
     return pl.pallas_call(
         functools.partial(main_kernel, group, part, shards),
         out_shape=(
             jax.ShapeDtypeStruct((rows, width), jnp.bfloat16),
             jax.ShapeDtypeStruct((rows, channels), jnp.bfloat16),
-            jax.ShapeDtypeStruct((6, width), f32),
-            jax.ShapeDtypeStruct((states + 6, width), f32),
+            jax.ShapeDtypeStruct((3, channels), f32),
+            jax.ShapeDtypeStruct((3, channels), f32),
+            jax.ShapeDtypeStruct((states + 6, channels), f32),
             jax.ShapeDtypeStruct((2 * states, rows), f32),
         ),
         grid_spec=pltpu.PrefetchScalarGridSpec(
@@ -360,8 +386,9 @@
             in_specs=in_specs,
             out_specs=(pl.BlockSpec((rows, width), lambda i, p: (0, 0)),
                        pl.BlockSpec((rows, width), col),
-                       pl.BlockSpec((6, width), lambda i, p: (0, 0)),
-                       pl.BlockSpec((states + 6, width), lambda i, p: (0, 0)),
+                       pl.BlockSpec((3, width), col),
+                       pl.BlockSpec((3, width), col),
+                       pl.BlockSpec((states + 6, width), col),
                        pl.BlockSpec((2 * states, rows), lambda i, p: (0, 0))),
             scratch_shapes=[
                 pltpu.VMEM((rows + 3 * PAST, LANES), f32),
@@ -387,6 +414,33 @@
     )(*operands)
 
 
+def join_kernel(count, *refs):
+    out_ref = refs[-1]
+    width = refs[0].shape[1]
+    for b in range(count):
+        out_ref[:, b * width:(b + 1) * width] = refs[b][...]
+
+
+def join_edge_kernel(count, *refs):
+    join_kernel(count, *refs[:count], refs[-1])
+    rows = refs[0].shape[0]
+    tail = refs[count][...] + refs[count + 1][...]
+    refs[-1][rows - 3:rows, :] = tail.astype(jnp.bfloat16)
+
+
+def join_call(blocks, mine=None, spilled=None):
+    count = len(blocks)
+    rows, width = blocks[0].shape
+    edges = [] if mine is None else [mine, spilled]
+    body = join_kernel if mine is None else join_edge_kernel
+    return pl.pallas_call(
+        functools.partial(body, count),
+        out_shape=jax.ShapeDtypeStruct((rows, count * width), blocks[0].dtype),
+        compiler_params=pltpu.CompilerParams(vmem_limit_bytes=16 * MIB),
+        name="join",
+    )(*blocks, *edges)
+
+
 def on_device(inner_x, dt_raw, grad_out, state_maps, saved_states, a_log, conv_weight, conv_bias,
               skip_gain, doc_lengths):
     rows = inner_x.shape[1]
@@ -406,41 +460,34 @@
     def after(value, *earlier):
         return lax.optimization_barrier((value,) + earlier)[0]
 
-    own, heads = [], []
+    first = head_call(group, 0, 1, place, doc_lengths, maps, dt, gy, a_log[0])
+    heads = [lax.all_gather(first[0], "ctx")]
+    ready = place
+    if blocks > 1:
+        others = head_call(group, 1, blocks - 1, after(place, first), doc_lengths, maps, dt, gy,
+                           a_log[0])
+        heads += [lax.all_gather(others[b], "ctx") for b in range(blocks - 1)]
+        ready = after(place, others)
+
+    carried = None
+    arrived = []
     for b in range(blocks):
-        here = after(place, hist) if b == min(2, blocks - 1) else place
-        own.append(head_call(group, b, here, doc_lengths, maps, dt, gy, a_log[0]))
-        heads.append(lax.all_gather(own[-1], "ctx"))
-    ready = after(place, *own)
-
-    gdt = None
-    maps_sum = 0.0
-    arrived, edges, shares = [], [], []
-    for b in range(blocks):
-        here = after(ready, *arrived[:-1], *shares[:-1]) if b == blocks - 1 else ready
-        gx, gdt, edge, gp, gm = main_call(
+        here = after(ready, *arrived[:-1]) if b == blocks - 1 else ready
+        gx, *carried = main_call(
             group, 8, shards, b, here, doc_lengths, maps, x, hist, dt, gy, saved_states[0, 0],
-            a_log[0], conv_weight[0], conv_bias, skip_gain, heads[b], gdt)
+            a_log[0], conv_weight[0], conv_bias, skip_gain, heads[b], carried)
         arrived.append(shift_to(gx, "pipe", -1))
-        if b > 0:
-            gp = after(gp, shares[b - 1])
-        shares.append(lax.psum(gp, "ctx"))
-        edges.append(edge)
-        maps_sum = maps_sum + gm
+    gdt, mine, spill, params, grad_maps = carried
     if blocks > 1:
-        edges[-1] = after(edges[-1], arrived[-2])
-
-    edge = jnp.concatenate(edges, 1)
-    mine = shift_to(edge[3:], "pipe", -1)
+        mine, spill, params, _ = lax.optimization_barrier((mine, spill, params, arrived[-2]))
+
+    shares = lax.psum_scatter(params, "ctx", scatter_dimension=1, tiled=True)
+    mine = shift_to(mine, "pipe", -1)
     pairs = [(s * shards + k, (s - 1) * shards + k - 1)
              for s in range(1, sections) for k in range(1, shards)]
-    spilled = lax.ppermute(edge[:3], ("pipe", "ctx"), pairs)
-    tail = (mine + spilled).astype(jnp.bfloat16)
-    upstream = jnp.concatenate(arrived, 1)
-    upstream = lax.dynamic_update_slice(upstream, tail, (rows - 3, 0))
-    share = channels // shards
-    params = lax.dynamic_slice_in_dim(jnp.concatenate(shares, 1), me * share, share, 1)
-    return upstream[None], gdt[None], maps_sum.reshape(1, 2, states, rows), params[None]
+    spilled = lax.ppermute(spill, ("pipe", "ctx"), pairs)
+    upstream = join_call(arrived, mine, spilled)
+    return upstream[None], gdt[None], grad_maps.reshape(1, 2, states, rows), shares[None]
 
 
 def solution(mesh):

time: 349 us -> 186 us (0.53)
  the two profiles are of different devices: /device:TPU:13 before, /device:TPU:0 now
where the time goes in v3:
time: 186 us
  Pallas kernels  119 us (64%)
  waiting for transfers between devices  38 us (20%)
  between operations  13.9 us (7%)
  starting transfers between devices  10.3 us (6%)
  local copies, waits for them, and re-layouts  4.41 us (2%)
    pallas_call x4, Pallas kernels, main_call(): pl.pallas_call(functools.partial(main_kernel, group, part, shards), out_s...  95.8 us
    pallas_call x2, Pallas kernels, head_call(): pl.pallas_call(functools.partial(head_kernel, group, 8), grid=(blocks,),...  22.1 us
    ppermute x6, waiting for transfers between devices, shift_to(): return lax.ppermute(x, axis, pairs)  19.9 us
    reduce_scatter x1, waiting for transfers between devices, on_device(): shares = lax.psum_scatter(params, 'ctx', scatter_dimension=1, tiled=True)  13.1 us
    ppermute x6, starting transfers between devices, shift_to(): return lax.ppermute(x, axis, pairs)  8.78 us
  transfers between devices with their start and end apart: 12, of which 5 were waited for; matrix products, arithmetic and copies ran while one was open for 1% of the time, Pallas kernels for 61%

profile of v3, /device:TPU:0, one launch (start us, length us, event | category | flops | bytes accessed | tf_op | source)
XLA Modules:
  0.0 186.0 jit_solution(14097462424458487461)
XLA Ops:
  7.2 6.7 %head.2 = f32[1,17,16,128]{3,2,1,0:T(8,128)} custom-call(s32[1]{0:T(128)} %bitcast.place_ref, s32[1,8]{1,0:T(1,128)} %len_ref.11, f32[32,128]{1,0:T(8,128)} %bitcast.46, bf16[128,8192]{1,0:T(8,128)(2,1)} %bitcast.20, bf16[128,8192]{1,0:T(8,128)(2,1)} %bitcast.26, f32[16,8192]{1,0:T(8,128)} %bitcast.36), custom_call_target="tpu_custom_call" | custom-call | flops 4194304000 | bytes 16777216 | tf_op jit(solution)/shard_map/head/pallas_call | solution.py:134
  13.9 0.0 all-gather.7.cloned.1.call-start
  14.0 15.4 %head.3 = f32[3,17,16,128]{3,2,1,0:T(8,128)} custom-call(s32[1]{0:T(128)} %bitcast.place_ref, s32[1,8]{1,0:T(1,128)} %len_ref.11, f32[32,128]{1,0:T(8,128)} %bitcast.47, bf16[128,8192]{1,0:T(8,128)(2,1)} %bitcast.21, bf16[128,8192]{1,0:T(8,128)(2,1)} %bitcast.27, f32[16,8192]{1,0:T(8,128)} %bitcast.37), custom_call_target="tpu_custom_call" | custom-call | flops 12582912000 | bytes 50331648 | tf_op jit(solution)/shard_map/head/pallas_call | solution.py:134
  29.4 1.8 fusion
  31.3 0.7 all-gather.9.cloned.1.call-update
  32.0 0.9 slice_bitcast_fusion
  33.0 2.4 %collective-permute-start = (bf16[3,8192]{1,0:T(4,128)(2,1)S(1)}, bf16[3,8192]{1,0:T(4,128)(2,1)S(1)}, u32[]{:S(2)}, u32[]{:S(2)}) collective-permute-start(bf16[3,8192]{1,0:T(4,128)(2,1)S(1)} %slice_bitcast_fusion), channel_id=1, source_target_pairs={{0,1},{1,2},{2,3},{3,4},{4,5},{5,6},{6,7},{8,9},{9,10},{10,11},{11... | collective-permute-start | bytes 147464 | tf_op jit(solution)/shard_map/ppermute | solution.py:26
  35.4 0.8 collective-permute-done.hist_ref
  36.2 3.0 %all-gather.5.cloned.1.call-done.next_ref.next2_ref.next3_ref = f32[8,17,16,128]{3,2,1,0:T(8,128)} async-done(((f32[1,17,16,128]{3,2,1,0:T(8,128)}), f32[8,17,16,128]{3,2,1,0:T(8,128)}) %all-gather.5.cloned.1.call-update) | async-done | bytes 1114128 | tf_op jit(solution)/shard_map/all_gather | solution.py:464
  39.2 23.9 %main.4 = (bf16[128,2048]{1,0:T(8,128)(2,1)}, bf16[128,8192]{1,0:T(8,128)(2,1)}, f32[3,8192]{1,0:T(4,128)}, f32[3,8192]{1,0:T(4,128)}, f32[22,8192]{1,0:T(8,128)}, /*index=5*/f32[32,128]{1,0:T(8,128)}) custom-call(s32[1]{0:T(128)} %bitcast.place_ref, s32[1,8]{1,0:T(1,128)} %len_ref.11, f32[32,128]{1,0:T(8,128)} %bitcast.48, bf16[128,8192]{1,0:T(8,128)(2,1)} %bitcast.16, ...), custom_call_target="tpu_custom_call" | custom-call | flops 20971520000 | bytes 75497472 | tf_op jit(solution)/shard_map/main/pallas_call | solution.py:373
  63.1 1.3 collective-permute-start.1
  64.5 24.0 %main.5 = (bf16[128,2048]{1,0:T(8,128)(2,1)}, bf16[128,8192]{1,0:T(8,128)(2,1)}, f32[3,8192]{1,0:T(4,128)}, f32[3,8192]{1,0:T(4,128)}, f32[22,8192]{1,0:T(8,128)}, /*index=5*/f32[32,128]{1,0:T(8,128)}) custom-call(s32[1]{0:T(128)} %bitcast.place_ref, ...), custom_call_target="tpu_custom_call", output_to_operand_aliasing={{1}: (15, {}), {2}: (16, {}), {3}: (17, {}), {4}: (18, {}),... | custom-call | flops 20971520000 | bytes 75497472 | tf_op jit(solution)/shard_map/main/pallas_call | solution.py:373
  88.4 1.3 collective-permute-start.2
  89.7 24.0 %main.6 = (bf16[128,2048]{1,0:T(8,128)(2,1)}, bf16[128,8192]{1,0:T(8,128)(2,1)}, f32[3,8192]{1,0:T(4,128)}, f32[3,8192]{1,0:T(4,128)}, f32[22,8192]{1,0:T(8,128)}, /*index=5*/f32[32,128]{1,0:T(8,128)}) custom-call(s32[1]{0:T(128)} %bitcast.place_ref, ...), custom_call_target="tpu_custom_call", output_to_operand_aliasing={{1}: (15, {}), {2}: (16, {}), {3}: (17, {}), {4}: (18, {}),... | custom-call | flops 20971520000 | bytes 75497472 | tf_op jit(solution)/shard_map/main/pallas_call | solution.py:373
  113.7 1.3 collective-permute-start.3
  115.1 24.0 %main.7 = (bf16[128,2048]{1,0:T(8,128)(2,1)}, bf16[128,8192]{1,0:T(8,128)(2,1)}, f32[3,8192]{1,0:T(4,128)}, f32[3,8192]{1,0:T(4,128)}, f32[22,8192]{1,0:T(8,128)}, /*index=5*/f32[32,128]{1,0:T(8,128)}) custom-call(s32[1]{0:T(128)} %bitcast.place_ref, ...), custom_call_target="tpu_custom_call", output_to_operand_aliasing={{1}: (15, {}), {2}: (16, {}), {3}: (17, {}), {4}: (18, {}),... | custom-call | flops 20971520000 | bytes 75497472 | tf_op jit(solution)/shard_map/main/pallas_call | solution.py:373
  139.1 1.3 collective-permute-start.4
  140.4 1.3 collective-permute-start.5
  141.7 1.3 collective-permute-start.6
  143.0 19.1 %collective-permute-done.5.refs_4_ = f32[3,8192]{1,0:T(4,128)S(1)} collective-permute-done((f32[3,8192]{1,0:T(4,128)}, f32[3,8192]{1,0:T(4,128)S(1)}, u32[]{:S(2)}, u32[]{:S(2)}) %collective-permute-start.5) | collective-permute-done | bytes 98336 | tf_op jit(solution)/shard_map/ppermute | solution.py:26
  162.1 1.2 collective-permute-done.6.refs_5_
  163.2 1.5 join.1
  164.7 13.1 %reduce-scatter.2.cloned.1.call-done = f32[22,1024]{1,0:T(8,128)} async-done(((f32[22,8192]{1,0:T(8,128)}), f32[22,1024]{1,0:T(8,128)}) %reduce-scatter.2.cloned.1.call-update) | async-done | bytes 90128 | tf_op jit(solution)/shard_map/reduce_scatter | solution.py:484
  177.8 1.6 copy.30
  (17 shorter events, 0.3 us)
Async XLA Ops:
  7.2 32.0 %all-gather.5.cloned.1.call-start = ((), (), s32[]{:S(2)}) async-start(), calls=%async_computation.1 | async-start | bytes 1253376 | tf_op jit(solution)/shard_map/all_gather | solution.py:464
  13.9 50.5 %all-gather.7.cloned.1.call-start = ((), (), s32[]{:S(2)}) async-start(), calls=%async_computation.2 | async-start | bytes 1253376 | tf_op jit(solution)/shard_map/all_gather | solution.py:469
  31.2 58.5 %all-gather.9.cloned.1.call-start = ((), (), s32[]{:S(2)}) async-start(), calls=%async_computation.3 | async-start | bytes 1253376 | tf_op jit(solution)/shard_map/all_gather | solution.py:469
  32.0 83.1 %all-gather.11.cloned.1.call-start = ((), (), s32[]{:S(2)}) async-start(), calls=%async_computation.4 | async-start | bytes 1253376 | tf_op jit(solution)/shard_map/all_gather | solution.py:469
  33.0 3.2 %collective-permute-start = (bf16[3,8192]{1,0:T(4,128)(2,1)S(1)}, bf16[3,8192]{1,0:T(4,128)(2,1)S(1)}, u32[]{:S(2)}, u32[]{:S(2)}) collective-permute-start(bf16[3,8192]{1,0:T(4,128)(2,1)S(1)} %slice_bitcast_fusion), channel_id=1, source_target_pairs={{0,1},{1,2},{2,3},{3,4},{4,5},{5,6},{6,7},{8,9},{9,10},{10,11},{11... | collective-permute-start | bytes 147464 | tf_op jit(solution)/shard_map/ppermute | solution.py:26
  35.3 142.5 %reduce-scatter.2.cloned.1.call-start = ((), (), s32[]{:S(2)}) async-start(), calls=%async_computation.5 | async-start | bytes 884736 | tf_op jit(solution)/shard_map/reduce_scatter | solution.py:484
  36.2 3.0 %copy-start = (bf16[3,8192]{1,0:T(4,128)(2,1)}, bf16[3,8192]{1,0:T(4,128)(2,1)S(1)}, u32[]{:S(2)}) copy-start(bf16[3,8192]{1,0:T(4,128)(2,1)S(1)} %collective-permute-done.hist_ref) | copy-start | bytes 147460
  63.1 51.9 %collective-permute-start.1 = (bf16[128,2048]{1,0:T(8,128)(2,1)}, bf16[128,2048]{1,0:T(8,128)(2,1)S(1)}, u32[]{:S(2)}, u32[]{:S(2)}) collective-permute-start(bf16[128,2048]{1,0:T(8,128)(2,1)} %get-tuple-element.36), channel_id=1, source_target_pairs={{8,0},{16,8},{24,16},{9,1},{17,9},{25,17},{10,2},{18,10},{26,18},{... | collective-permute-start | bytes 1572872 | tf_op jit(solution)/shard_map/ppermute | solution.py:26
  88.4 26.6 %collective-permute-start.2 = (bf16[128,2048]{1,0:T(8,128)(2,1)}, bf16[128,2048]{1,0:T(8,128)(2,1)S(1)}, u32[]{:S(2)}, u32[]{:S(2)}) collective-permute-start(bf16[128,2048]{1,0:T(8,128)(2,1)} %get-tuple-element.42), channel_id=1, source_target_pairs={{8,0},{16,8},{24,16},{9,1},{17,9},{25,17},{10,2},{18,10},{26,18},{... | collective-permute-start | bytes 1572872 | tf_op jit(solution)/shard_map/ppermute | solution.py:26
  113.7 25.3 %collective-permute-start.3 = (bf16[128,2048]{1,0:T(8,128)(2,1)}, bf16[128,2048]{1,0:T(8,128)(2,1)S(1)}, u32[]{:S(2)}, u32[]{:S(2)}) collective-permute-start(bf16[128,2048]{1,0:T(8,128)(2,1)} %get-tuple-element.48), channel_id=1, source_target_pairs={{8,0},{16,8},{24,16},{9,1},{17,9},{25,17},{10,2},{18,10},{26,18},{... | collective-permute-start | bytes 1572872 | tf_op jit(solution)/shard_map/ppermute | solution.py:26
  139.1 24.2 %collective-permute-start.4 = (bf16[128,2048]{1,0:T(8,128)(2,1)}, bf16[128,2048]{1,0:T(8,128)(2,1)S(1)}, u32[]{:S(2)}, u32[]{:S(2)}) collective-permute-start(bf16[128,2048]{1,0:T(8,128)(2,1)} %get-tuple-element.55), channel_id=1, source_target_pairs={{8,0},{16,8},{24,16},{9,1},{17,9},{25,17},{10,2},{18,10},{26,18},{... | collective-permute-start | bytes 1572872 | tf_op jit(solution)/shard_map/ppermute | solution.py:26
  140.4 21.7 %collective-permute-start.5 = (f32[3,8192]{1,0:T(4,128)}, f32[3,8192]{1,0:T(4,128)S(1)}, u32[]{:S(2)}, u32[]{:S(2)}) collective-permute-start(f32[3,8192]{1,0:T(4,128)} %get-tuple-element.59), channel_id=1, source_target_pairs={{8,0},{16,8},{24,16},{9,1},{17,9},{25,17},{10,2},{18,10},{26,18},{... | collective-permute-start | bytes 294920 | tf_op jit(solution)/shard_map/ppermute | solution.py:26
  141.7 21.6 %collective-permute-start.6 = (f32[3,8192]{1,0:T(4,128)}, f32[3,8192]{1,0:T(4,128)S(1)}, u32[]{:S(2)}, u32[]{:S(2)}) collective-permute-start(f32[3,8192]{1,0:T(4,128)} %get-tuple-element.60), channel_id=1, source_target_pairs={{9,0},{10,1},{11,2},{12,3},{13,4},{14,5},{15,6},{17,8},{18,9},{19,... | collective-permute-start | bytes 294920 | tf_op jit(solution)/shard_map/ppermute | solution.py:488
Sparse Core Ops, SparseCore 0:
  14.1 25.1 all-gather.4
  40.8 22.0 all-gather.6
  64.6 22.0 all-gather.8
  88.2 22.0 all-gather.10
  139.2 38.5 reduce-scatter.1

commit v4 on v3

--- a/solution.py
+++ b/solution.py
@@ -155,7 +155,7 @@
     )(place, lengths, maps, dt, gy, alog)
 
 
-def main_kernel(group, part, shards, place_ref, len_ref, maps_ref, x_ref, hist_ref, dt_ref, gy_ref,
+def main_kernel(group, part, many, place_ref, len_ref, maps_ref, x_ref, hist_ref, dt_ref, gy_ref,
                 start_ref, alog_ref, cw_ref, cb_ref, sk_ref, next_ref, next2_ref, next3_ref, *rest):
     maps_before = rest[-26] if len(rest) > 25 else None
     rest = rest[-25:]
@@ -167,8 +167,13 @@
     f32 = jnp.float32
     zero = jnp.zeros((group, LANES), f32)
 
-    fill_keep(place_ref[0] * rows, len_ref, keep_t)
-    fill_maps(maps_ref, maps_t)
+    first = pl.program_id(0) == 0
+
+    @pl.when(first)
+    def _():
+        fill_keep(place_ref[0] * rows, len_ref, keep_t)
+        fill_maps(maps_ref, maps_t)
+
     gather_positions(x_ref, x_t, group, 3)
     gather_positions(gy_ref, gy_t, group)
     gather_positions(dt_ref, step_t, group)
@@ -206,12 +211,10 @@
 
     lax.fori_loop(0, rows // CHUNK, rows_of, 0)
 
-    last = shards - 1 - place_ref[0]
     for n in range(states):
-        arrived = jnp.where(last >= 3, next3_ref[0, n], 0.0)
-        for d, ref in ((2, next2_ref), (1, next_ref)):
+        arrived = next3_ref[0, n]
+        for ref in (next2_ref, next_ref):
             arrived = ref[0, n] + jnp.exp2(ref[0, states] * a2_s[n]) * arrived
-            arrived = jnp.where(last >= d, arrived, 0.0)
         gin_s[n] = arrived
 
     def fold(p):
@@ -220,55 +223,71 @@
             out = out + p[k * 8:(k + 1) * 8]
         return out
 
-    for lo in range(0, states, part):
-        hi = lo + part
-
-        for n in range(lo, hi):
-            h_s[0, n - lo] = start_s[n]
-
-        def forward(t, hs):
-            step = step_t[t]
-            du = du_t[t]
-            out = []
+    def assign(ref, n, t, value):
+        ref[n, t] = value
+
+    def add(ref, n, t, value):
+        ref[n, t] += value
+
+    def scans(put):
+        for lo in range(0, states, part):
+            hi = lo + part
+
             for n in range(lo, hi):
-                decay = jnp.exp2(step * a2_s[n])
-                h = decay * hs[n - lo] + spread(maps_t, n * rows + t, group) * du
-                h_s[t + 1, n - lo] = h
-                out.append(h)
-            return tuple(out)
-
-        lax.fori_loop(0, rows, forward, tuple(start_s[n] for n in range(lo, hi)), unroll=8)
-
-        def backward(i, carry):
-            cars, rates = carry
-            t = rows - 1 - i
-            step = step_t[t]
-            du = du_t[t]
-            y = gy_t[t]
-            new_cars, new_rates = [], []
-            w = None if lo == 0 else gc_t[t + 3]
-            v = None if lo == 0 else v_t[t]
+                h_s[0, n - lo] = start_s[n]
+
+            def forward(t, hs):
+                step = step_t[t]
+                du = du_t[t]
+                out = []
+                for n in range(lo, hi):
+                    decay = jnp.exp2(step * a2_s[n])
+                    h = decay * hs[n - lo] + spread(maps_t, n * rows + t, group) * du
+                    h_s[t + 1, n - lo] = h
+                    out.append(h)
+                return tuple(out)
+
+            lax.fori_loop(0, rows, forward, tuple(start_s[n] for n in range(lo, hi)), unroll=8)
+
+            def backward(i, carry):
+                cars, rates = carry
+                t = rows - 1 - i
+                step = step_t[t]
+                du = du_t[t]
+                y = gy_t[t]
+                new_cars, new_rates = [], []
+                w = None if lo == 0 else gc_t[t + 3]
+                v = None if lo == 0 else v_t[t]
+                for n in range(lo, hi):
+                    m = n - lo
+                    g = spread(maps_t, (states + n) * rows + t, group) * y + cars[m]
+                    put(acc_s, n, t, fold(g * du))
+                    put(acc_s, states + n, t, fold(h_s[t + 1, m] * y))
+                    bg = spread(maps_t, n * rows + t, group) * g
+                    w = bg if w is None else w + bg
+                    car = jnp.exp2(step * a2_s[n]) * g
+                    aq = a2_s[n] * (car * h_s[t, m])
+                    v = aq if v is None else v + aq
+                    new_cars.append(car)
+                    new_rates.append(rates[m] + step * aq)
+                gc_t[t + 3] = w
+                v_t[t] = v
+                return tuple(new_cars), tuple(new_rates)
+
+            _, rates = lax.fori_loop(
+                0, rows, backward,
+                (tuple(gin_s[n] for n in range(lo, hi)), (zero,) * part), unroll=4)
             for n in range(lo, hi):
-                m = n - lo
-                g = spread(maps_t, (states + n) * rows + t, group) * y + cars[m]
-                acc_s[n, t] = fold(g * du)
-                acc_s[states + n, t] = fold(h_s[t + 1, m] * y)
-                bg = spread(maps_t, n * rows + t, group) * g
-                w = bg if w is None else w + bg
-                car = jnp.exp2(step * a2_s[n]) * g
-                aq = a2_s[n] * (car * h_s[t, m])
-                v = aq if v is None else v + aq
-                new_cars.append(car)
-                new_rates.append(rates[m] + step * aq)
-            gc_t[t + 3] = w
-            v_t[t] = v
-            return tuple(new_cars), tuple(new_rates)
-
-        _, rates = lax.fori_loop(
-            0, rows, backward,
-            (tuple(gin_s[n] for n in range(lo, hi)), (zero,) * part), unroll=4)
-        for n in range(lo, hi):
-            gp_s[n] = rates[n - lo] * LN2
+                gp_s[n] = rates[n - lo] * LN2
+
+    @pl.when(first)
+    def _():
+        scans(assign)
+
+    if many:
+        @pl.when(jnp.logical_not(first))
+        def _():
+            scans(add)
 
     def finish(i, carry):
         taps = list(carry)
@@ -308,7 +327,12 @@
     scatter_positions(v_t, gdt_ref, group)
     mine_ref[...] = w_t[rows - 3:rows].reshape(3, group * LANES)
     spill_ref[...] = small_s[6:9].reshape(3, group * LANES)
-    gp_ref[...] = gp_s[...].reshape(states + 6, group * LANES)
+    for k in range(states + 6, gp_s.shape[0]):
+        gp_s[k] = zero
+    wide = gp_s[...].reshape(gp_s.shape[0], group * LANES)
+    share = gp_ref.shape[2]
+    for k in range(gp_ref.shape[0]):
+        gp_ref[k] = wide[:, k * share:(k + 1) * share]
 
     sub = lax.broadcasted_iota(jnp.int32, (8, LANES), 0)
 
@@ -333,27 +357,27 @@
         gm_ref[pl.ds(n, 1), :] = total
         return 0
 
-    lax.fori_loop(0, 2 * states, add_sublanes, 0)
-    lax.fori_loop(0, 2 * states, add_lanes, 0, unroll=4)
-
-
-def main_call(group, part, shards, block, place, lengths, maps, x, hist, dt, gy, start, alog, cw,
-              cb, sk, heads, carried):
+    @pl.when(pl.program_id(0) == pl.num_programs(0) - 1)
+    def _():
+        lax.fori_loop(0, 2 * states, add_sublanes, 0)
+        lax.fori_loop(0, 2 * states, add_lanes, 0, unroll=4)
+
+
+def main_call(group, part, shards, block, blocks, place, lengths, maps, x, hist, dt, gy, start,
+              alog, cw, cb, sk, heads, carried):
     rows, channels = x.shape
     states = alog.shape[0]
     width = group * LANES
+    share = channels // shards
+    params = -(-(states + 6) // 8) * 8
     smem = pl.BlockSpec(memory_space=pltpu.SMEM)
-    col = lambda i, p: (0, block)
+    col = lambda i: (0, block + i)
+    whole = lambda i: (0, 0)
     f32 = jnp.float32
     table = pltpu.VMEM((rows, group, LANES), f32)
     vectors = pltpu.VMEM((states, group, LANES), f32)
-
-    def later(d):
-        return pl.BlockSpec((1, states + 1, group, LANES),
-                            lambda i, p: (jnp.minimum(p[0] + d, shards - 1), 0, 0, 0))
-
-    operands = [place, lengths, maps, x, hist, dt, gy, start, alog, cw, cb, sk, heads, heads, heads]
-    in_specs = [smem, pl.BlockSpec((2 * states, rows), lambda i, p: (0, 0)),
+    operands = [place, lengths, maps, x, hist, dt, gy, start, alog, cw, cb, sk, *heads]
+    in_specs = [smem, smem, pl.BlockSpec((2 * states, rows), whole),
                 pl.BlockSpec((rows, width), col),
                 pl.BlockSpec((3, width), col),
                 pl.BlockSpec((rows, width), col),
@@ -362,83 +386,74 @@
                 pl.BlockSpec((states, width), col),
                 pl.BlockSpec((4, width), col),
                 pl.BlockSpec((1, width), col),
-                pl.BlockSpec((1, width), col),
-                later(1), later(2), later(3)]
+                pl.BlockSpec((1, width), col)]
+    in_specs += [pl.BlockSpec((1, states + 1, group, LANES), lambda i: (i, 0, 0, 0))] * REACH
     aliases = {}
     if carried is not None:
         aliases = {len(operands) + k: k + 1 for k in range(len(carried))}
         operands += carried
         in_specs += [pl.BlockSpec(memory_space=pl.ANY)] * (len(carried) - 1)
-        in_specs.append(pl.BlockSpec((2 * states, rows), lambda i, p: (0, 0)))
+        in_specs.append(pl.BlockSpec((2 * states, rows), whole))
     return pl.pallas_call(
-        functools.partial(main_kernel, group, part, shards),
+        functools.partial(main_kernel, group, part, blocks > 1),
+        grid=(blocks,),
         out_shape=(
-            jax.ShapeDtypeStruct((rows, width), jnp.bfloat16),
+            jax.ShapeDtypeStruct((rows, blocks * width), jnp.bfloat16),
             jax.ShapeDtypeStruct((rows, channels), jnp.bfloat16),
             jax.ShapeDtypeStruct((3, channels), f32),
             jax.ShapeDtypeStruct((3, channels), f32),
-            jax.ShapeDtypeStruct((states + 6, channels), f32),
+            jax.ShapeDtypeStruct((shards, params, share), f32),
             jax.ShapeDtypeStruct((2 * states, rows), f32),
         ),
-        grid_spec=pltpu.PrefetchScalarGridSpec(
-            num_scalar_prefetch=1,
-            grid=(1,),
-            in_specs=in_specs,
-            out_specs=(pl.BlockSpec((rows, width), lambda i, p: (0, 0)),
-                       pl.BlockSpec((rows, width), col),
-                       pl.BlockSpec((3, width), col),
-                       pl.BlockSpec((3, width), col),
-                       pl.BlockSpec((states + 6, width), col),
-                       pl.BlockSpec((2 * states, rows), lambda i, p: (0, 0))),
-            scratch_shapes=[
-                pltpu.VMEM((rows + 3 * PAST, LANES), f32),
-                pltpu.VMEM((2 * states * rows + 8, LANES), f32),
-                pltpu.VMEM((rows + 3, group, LANES), f32),
-                table, table,
-                vectors,
-                pltpu.VMEM((9, group, LANES), f32),
-                vectors, vectors,
-                table, table, table, table, table, table,
-                pltpu.VMEM((rows + 6, group, LANES), f32),
-                pltpu.VMEM((rows + 1, part, group, LANES), f32),
-                pltpu.VMEM((2 * states, rows, 8, LANES), f32),
-                pltpu.VMEM((states + 6, group, LANES), f32),
-            ]),
+        in_specs=in_specs,
+        out_specs=(pl.BlockSpec((rows, width), lambda i: (0, i)),
+                   pl.BlockSpec((rows, width), col),
+                   pl.BlockSpec((3, width), col),
+                   pl.BlockSpec((3, width), col),
+                   pl.BlockSpec((width // share, params, share), lambda i: (block + i, 0, 0)),
+                   pl.BlockSpec((2 * states, rows), whole)),
+        scratch_shapes=[
+            pltpu.VMEM((rows + 3 * PAST, LANES), f32),
+            pltpu.VMEM((2 * states * rows + 8, LANES), f32),
+            pltpu.VMEM((rows + 3, group, LANES), f32),
+            table, table,
+            vectors,
+            pltpu.VMEM((9, group, LANES), f32),
+            vectors, vectors,
+            table, table, table, table, table, table,
+            pltpu.VMEM((rows + 6, group, LANES), f32),
+            pltpu.VMEM((rows + 1, part, group, LANES), f32),
+            pltpu.VMEM((2 * states, rows, 8, LANES), f32),
+            pltpu.VMEM((params, group, LANES), f32),
+        ],
         input_output_aliases=aliases,
         compiler_params=pltpu.CompilerParams(
             dimension_semantics=("arbitrary",), vmem_limit_bytes=MAIN_VMEM),
         cost_estimate=pl.CostEstimate(
-            flops=rows * states * width * 5000, transcendentals=0,
-            bytes_accessed=width * rows * states * 18),
+            flops=blocks * rows * states * width * 5000, transcendentals=0,
+            bytes_accessed=blocks * width * rows * states * 18),
         name="main",
     )(*operands)
 
 
 def join_kernel(count, *refs):
     out_ref = refs[-1]
-    width = refs[0].shape[1]
+    rows, width = refs[0].shape
     for b in range(count):
         out_ref[:, b * width:(b + 1) * width] = refs[b][...]
-
-
-def join_edge_kernel(count, *refs):
-    join_kernel(count, *refs[:count], refs[-1])
-    rows = refs[0].shape[0]
     tail = refs[count][...] + refs[count + 1][...]
-    refs[-1][rows - 3:rows, :] = tail.astype(jnp.bfloat16)
-
-
-def join_call(blocks, mine=None, spilled=None):
+    out_ref[rows - 3:rows, :] = tail.astype(out_ref.dtype)
+
+
+def join_call(blocks, mine, spilled):
     count = len(blocks)
     rows, width = blocks[0].shape
-    edges = [] if mine is None else [mine, spilled]
-    body = join_kernel if mine is None else join_edge_kernel
     return pl.pallas_call(
-        functools.partial(body, count),
+        functools.partial(join_kernel, count),
         out_shape=jax.ShapeDtypeStruct((rows, count * width), blocks[0].dtype),
         compiler_params=pltpu.CompilerParams(vmem_limit_bytes=16 * MIB),
         name="join",
-    )(*blocks, *edges)
+    )(*blocks, mine, spilled)
 
 
 def on_device(inner_x, dt_raw, grad_out, state_maps, saved_states, a_log, conv_weight, conv_bias,
@@ -460,32 +475,30 @@
     def after(value, *earlier):
         return lax.optimization_barrier((value,) + earlier)[0]
 
-    first = head_call(group, 0, 1, place, doc_lengths, maps, dt, gy, a_log[0])
-    heads = [lax.all_gather(first[0], "ctx")]
-    ready = place
-    if blocks > 1:
-        others = head_call(group, 1, blocks - 1, after(place, first), doc_lengths, maps, dt, gy,
-                           a_log[0])
-        heads += [lax.all_gather(others[b], "ctx") for b in range(blocks - 1)]
-        ready = after(place, others)
+    calls = 2
+    many = blocks // calls
+    here, heads = place, []
+    for c in range(calls):
+        own = head_call(group, c * many, many, here, doc_lengths, maps, dt, gy, a_log[0])
+        heads.append([shift_to(own, "ctx", -d) for d in range(1, REACH + 1)])
+        here = after(place, own)
 
     carried = None
     arrived = []
-    for b in range(blocks):
-        here = after(ready, *arrived[:-1]) if b == blocks - 1 else ready
+    for c in range(calls):
         gx, *carried = main_call(
-            group, 8, shards, b, here, doc_lengths, maps, x, hist, dt, gy, saved_states[0, 0],
-            a_log[0], conv_weight[0], conv_bias, skip_gain, heads[b], carried)
+            group, 8, shards, c * many, many, here, doc_lengths, maps, x, hist, dt, gy,
+            saved_states[0, 0], a_log[0], conv_weight[0], conv_bias, skip_gain, heads[c], carried)
         arrived.append(shift_to(gx, "pipe", -1))
     gdt, mine, spill, params, grad_maps = carried
-    if blocks > 1:
-        mine, spill, params, _ = lax.optimization_barrier((mine, spill, params, arrived[-2]))
-
-    shares = lax.psum_scatter(params, "ctx", scatter_dimension=1, tiled=True)
+    mine, spill, params, _ = lax.optimization_barrier((mine, spill, params, arrived[-2]))
+
     mine = shift_to(mine, "pipe", -1)
     pairs = [(s * shards + k, (s - 1) * shards + k - 1)
              for s in range(1, sections) for k in range(1, shards)]
     spilled = lax.ppermute(spill, ("pipe", "ctx"), pairs)
+    shares = lax.all_to_all(params, "ctx", 0, 0, tiled=True)
+    shares = jnp.sum(shares, axis=0)[:states + 6]
     upstream = join_call(arrived, mine, spilled)
     return upstream[None], gdt[None], grad_maps.reshape(1, 2, states, rows), shares[None]
 

time: 186 us -> 170 us (0.914)
  the two profiles are of different devices: /device:TPU:0 before, /device:TPU:13 now
where the time goes in v4:
time: 170 us; the launch traced here: 167 us
  Pallas kernels  107 us (63%)
  starting transfers between devices  30.6 us (18%)
  waiting for transfers between devices  25.1 us (15%)
  local copies, waits for them, and re-layouts  3.27 us (2%)
    pallas_call x2, Pallas kernels, main_call(): pl.pallas_call(functools.partial(main_kernel, group, part, blocks > 1), g...  83.9 us
    ppermute x10, waiting for transfers between devices, shift_to(): return lax.ppermute(x, axis, pairs)  24.9 us
    ppermute x10, starting transfers between devices, shift_to(): return lax.ppermute(x, axis, pairs)  22.7 us
    pallas_call x2, Pallas kernels, head_call(): pl.pallas_call(functools.partial(head_kernel, group, 8), grid=(blocks,),...  22 us
    all_to_all x1, starting transfers between devices, on_device(): shares = lax.all_to_all(params, 'ctx', 0, 0, tiled=True)  5.96 us
  transfers between devices with their start and end apart: 12, of which 3 were waited for; matrix products, arithmetic and copies ran while one was open for 1% of the time, Pallas kernels for 58%

profile of v4, /device:TPU:13, one launch (start us, length us, event | category | flops | bytes accessed | tf_op | source)
XLA Modules:
  0.0 167.3 jit_solution(1586891509366173407)
XLA Ops:
  0.6 11.0 %head.2 = f32[2,17,16,128]{3,2,1,0:T(8,128)} custom-call(s32[1]{0:T(128)} %bitcast.place_ref, s32[1,8]{1,0:T(1,128)} %len_ref.7, f32[32,128]{1,0:T(8,128)} %bitcast.34, bf16[128,8192]{1,0:T(8,128)(2,1)} %bitcast.18, bf16[128,8192]{1,0:T(8,128)(2,1)} %bitcast.22, f32[16,8192]{1,0:T(8,128)} %bitcast.28), custom_call_target="tpu_custom_call" | custom-call | flops 8388608000 | bytes 33554432 | tf_op jit(solution)/shard_map/head/pallas_call | solution.py:134
  11.6 2.6 %collective-permute-start.3 = (f32[2,17,16,128]{3,2,1,0:T(8,128)}, f32[2,17,16,128]{3,2,1,0:T(8,128)S(1)}, u32[]{:S(2)}, u32[]{:S(2)}) collective-permute-start(f32[2,17,16,128]{3,2,1,0:T(8,128)} %head.2), channel_id=1, source_target_pairs={{3,0},{4,1},{5,2},{6,3},{7,4},{11,8},{12,9},{13,10},{14,11},{15,12... | collective-permute-start | bytes 835592 | tf_op jit(solution)/shard_map/ppermute | solution.py:26
  14.3 1.9 %collective-permute-start.2 = (f32[2,17,16,128]{3,2,1,0:T(8,128)}, f32[2,17,16,128]{3,2,1,0:T(8,128)S(1)}, u32[]{:S(2)}, u32[]{:S(2)}) collective-permute-start(f32[2,17,16,128]{3,2,1,0:T(8,128)} %head.2), channel_id=1, source_target_pairs={{2,0},{3,1},{4,2},{5,3},{6,4},{7,5},{10,8},{11,9},{12,10},{13,11},... | collective-permute-start | bytes 835592 | tf_op jit(solution)/shard_map/ppermute | solution.py:26
  16.2 1.9 %collective-permute-start.1 = (f32[2,17,16,128]{3,2,1,0:T(8,128)}, f32[2,17,16,128]{3,2,1,0:T(8,128)S(1)}, u32[]{:S(2)}, u32[]{:S(2)}) collective-permute-start(f32[2,17,16,128]{3,2,1,0:T(8,128)} %head.2), channel_id=1, source_target_pairs={{1,0},{2,1},{3,2},{4,3},{5,4},{6,5},{7,6},{9,8},{10,9},{11,10},{12... | collective-permute-start | bytes 835592 | tf_op jit(solution)/shard_map/ppermute | solution.py:26
  18.1 0.9 slice_bitcast_fusion
  19.1 3.6 %collective-permute-start = (bf16[3,8192]{1,0:T(4,128)(2,1)S(1)}, bf16[3,8192]{1,0:T(4,128)(2,1)S(1)}, u32[]{:S(2)}, u32[]{:S(2)}) collective-permute-start(bf16[3,8192]{1,0:T(4,128)(2,1)S(1)} %slice_bitcast_fusion), channel_id=1, source_target_pairs={{0,1},{1,2},{2,3},{3,4},{4,5},{5,6},{6,7},{8,9},{9,10},{10,11},{11... | collective-permute-start | bytes 147464 | tf_op jit(solution)/shard_map/ppermute | solution.py:26
  22.7 11.0 %head.3 = f32[2,17,16,128]{3,2,1,0:T(8,128)} custom-call(s32[1]{0:T(128)} %bitcast.place_ref, s32[1,8]{1,0:T(1,128)} %len_ref.7, f32[32,128]{1,0:T(8,128)} %bitcast.35, bf16[128,8192]{1,0:T(8,128)(2,1)} %bitcast.19, bf16[128,8192]{1,0:T(8,128)(2,1)} %bitcast.23, f32[16,8192]{1,0:T(8,128)} %bitcast.29), custom_call_target="tpu_custom_call" | custom-call | flops 8388608000 | bytes 33554432 | tf_op jit(solution)/shard_map/head/pallas_call | solution.py:134
  33.7 1.9 %collective-permute-start.7 = (f32[2,17,16,128]{3,2,1,0:T(8,128)}, f32[2,17,16,128]{3,2,1,0:T(8,128)S(1)}, u32[]{:S(2)}, u32[]{:S(2)}) collective-permute-start(f32[2,17,16,128]{3,2,1,0:T(8,128)} %head.3), channel_id=1, source_target_pairs={{3,0},{4,1},{5,2},{6,3},{7,4},{11,8},{12,9},{13,10},{14,11},{15,12... | collective-permute-start | bytes 835592 | tf_op jit(solution)/shard_map/ppermute | solution.py:26
  35.6 1.9 %collective-permute-start.6 = (f32[2,17,16,128]{3,2,1,0:T(8,128)}, f32[2,17,16,128]{3,2,1,0:T(8,128)S(1)}, u32[]{:S(2)}, u32[]{:S(2)}) collective-permute-start(f32[2,17,16,128]{3,2,1,0:T(8,128)} %head.3), channel_id=1, source_target_pairs={{2,0},{3,1},{4,2},{5,3},{6,4},{7,5},{10,8},{11,9},{12,10},{13,11},... | collective-permute-start | bytes 835592 | tf_op jit(solution)/shard_map/ppermute | solution.py:26
  37.6 1.9 %collective-permute-start.5 = (f32[2,17,16,128]{3,2,1,0:T(8,128)}, f32[2,17,16,128]{3,2,1,0:T(8,128)S(1)}, u32[]{:S(2)}, u32[]{:S(2)}) collective-permute-start(f32[2,17,16,128]{3,2,1,0:T(8,128)} %head.3), channel_id=1, source_target_pairs={{1,0},{2,1},{3,2},{4,3},{5,4},{6,5},{7,6},{9,8},{10,9},{11,10},{12... | collective-permute-start | bytes 835592 | tf_op jit(solution)/shard_map/ppermute | solution.py:26
  39.6 0.7 copy-done.3
  40.3 42.1 %main.2 = (bf16[128,4096]{1,0:T(8,128)(2,1)}, bf16[128,8192]{1,0:T(8,128)(2,1)}, f32[3,8192]{1,0:T(4,128)}, f32[3,8192]{1,0:T(4,128)}, f32[8,24,1024]{2,1,0:T(8,128)}, /*index=5*/f32[32,128]{1,0:T(8,128)}) custom-call(s32[1]{0:T(128)} %bitcast.place_ref, s32[1,8]{1,0:T(1,128)} %len_ref.7, f32[32,128]{1,0:T(8,128)} %bitcast.36, bf16[128,8192]{1,0:T(8,128)(2,1)} %bitcast.16, ...), custom_call_target="tpu_custom_call" | custom-call | flops 41943040000 | bytes 150994944 | tf_op jit(solution)/shard_map/main/pallas_call | solution.py:397
  82.4 3.1 %collective-permute-start.4 = (bf16[128,4096]{1,0:T(8,128)(2,1)}, bf16[128,4096]{1,0:T(8,128)(2,1)S(1)}, u32[]{:S(2)}, u32[]{:S(2)}) collective-permute-start(bf16[128,4096]{1,0:T(8,128)(2,1)} %get-tuple-element.23), channel_id=1, source_target_pairs={{8,0},{16,8},{24,16},{9,1},{17,9},{25,17},{10,2},{18,10},{26,18},{... | collective-permute-start | bytes 3145736 | tf_op jit(solution)/shard_map/ppermute | solution.py:26
  85.5 0.7 copy-done
  86.4 41.8 %main.3 = (bf16[128,4096]{1,0:T(8,128)(2,1)}, bf16[128,8192]{1,0:T(8,128)(2,1)}, f32[3,8192]{1,0:T(4,128)}, f32[3,8192]{1,0:T(4,128)}, f32[8,24,1024]{2,1,0:T(8,128)}, /*index=5*/f32[32,128]{1,0:T(8,128)}) custom-call(s32[1]{0:T(128)} %bitcast.place_ref, ...), custom_call_target="tpu_custom_call", output_to_operand_aliasing={{1}: (15, {}), {2}: (16, {}), {3}: (17, {}), {4}: (18, {}),... | custom-call | flops 41943040000 | bytes 150994944 | tf_op jit(solution)/shard_map/main/pallas_call | solution.py:397
  128.2 6.0 %all-to-all-start = ((f32[8,24,1024]{2,1,0:T(8,128)}), f32[8,24,1024]{2,1,0:T(8,128)S(1)}, u32[]{:S(2)}, u32[]{:S(2)}) async-start(f32[8,24,1024]{2,1,0:T(8,128)} %get-tuple-element.37), calls=%async_computation | async-start | bytes 1572864 | tf_op jit(solution)/shard_map/all_to_all | solution.py:500
  134.2 1.9 %collective-permute-start.8 = (bf16[128,4096]{1,0:T(8,128)(2,1)}, bf16[128,4096]{1,0:T(8,128)(2,1)S(1)}, u32[]{:S(2)}, u32[]{:S(2)}) collective-permute-start(bf16[128,4096]{1,0:T(8,128)(2,1)} %get-tuple-element.29), channel_id=1, source_target_pairs={{8,0},{16,8},{24,16},{9,1},{17,9},{25,17},{10,2},{18,10},{26,18},{... | collective-permute-start | bytes 3145736 | tf_op jit(solution)/shard_map/ppermute | solution.py:26
  136.1 1.9 %collective-permute-start.9 = (f32[3,8192]{1,0:T(4,128)}, f32[3,8192]{1,0:T(4,128)S(1)}, u32[]{:S(2)}, u32[]{:S(2)}) collective-permute-start(f32[3,8192]{1,0:T(4,128)} %get-tuple-element.33), channel_id=1, source_target_pairs={{8,0},{16,8},{24,16},{9,1},{17,9},{25,17},{10,2},{18,10},{26,18},{... | collective-permute-start | bytes 294920 | tf_op jit(solution)/shard_map/ppermute | solution.py:26
  138.1 1.9 %collective-permute-start.10 = (f32[3,8192]{1,0:T(4,128)}, f32[3,8192]{1,0:T(4,128)S(1)}, u32[]{:S(2)}, u32[]{:S(2)}) collective-permute-start(f32[3,8192]{1,0:T(4,128)} %get-tuple-element.34), channel_id=1, source_target_pairs={{9,0},{10,1},{11,2},{12,3},{13,4},{14,5},{15,6},{17,8},{18,9},{19,... | collective-permute-start | bytes 294920 | tf_op jit(solution)/shard_map/ppermute | solution.py:499
  140.0 22.1 %collective-permute-done.8.refs_1_ = bf16[128,4096]{1,0:T(8,128)(2,1)S(1)} collective-permute-done((bf16[128,4096]{1,0:T(8,128)(2,1)}, bf16[128,4096]{1,0:T(8,128)(2,1)S(1)}, u32[]{:S(2)}, u32[]{:S(2)}) %collective-permute-start.8) | collective-permute-done | bytes 1048608 | tf_op jit(solution)/shard_map/ppermute | solution.py:26
  162.1 2.8 %collective-permute-done.9.refs_2_ = f32[3,8192]{1,0:T(4,128)S(1)} collective-permute-done((f32[3,8192]{1,0:T(4,128)}, f32[3,8192]{1,0:T(4,128)S(1)}, u32[]{:S(2)}, u32[]{:S(2)}) %collective-permute-start.9) | collective-permute-done | bytes 98336 | tf_op jit(solution)/shard_map/ppermute | solution.py:26
  164.9 0.1 collective-permute-done.10.refs_3_
  165.0 1.5 join.1
  166.6 0.7 broadcast_in_dim.11
  (22 shorter events, 0.4 us)
Async XLA Ops:
  11.6 25.9 %collective-permute-start.3 = (f32[2,17,16,128]{3,2,1,0:T(8,128)}, f32[2,17,16,128]{3,2,1,0:T(8,128)S(1)}, u32[]{:S(2)}, u32[]{:S(2)}) collective-permute-start(f32[2,17,16,128]{3,2,1,0:T(8,128)} %head.2), channel_id=1, source_target_pairs={{3,0},{4,1},{5,2},{6,3},{7,4},{11,8},{12,9},{13,10},{14,11},{15,12... | collective-permute-start | bytes 835592 | tf_op jit(solution)/shard_map/ppermute | solution.py:26
  14.3 25.3 %collective-permute-start.2 = (f32[2,17,16,128]{3,2,1,0:T(8,128)}, f32[2,17,16,128]{3,2,1,0:T(8,128)S(1)}, u32[]{:S(2)}, u32[]{:S(2)}) collective-permute-start(f32[2,17,16,128]{3,2,1,0:T(8,128)} %head.2), channel_id=1, source_target_pairs={{2,0},{3,1},{4,2},{5,3},{6,4},{7,5},{10,8},{11,9},{12,10},{13,11},... | collective-permute-start | bytes 835592 | tf_op jit(solution)/shard_map/ppermute | solution.py:26
  16.2 23.4 %collective-permute-start.1 = (f32[2,17,16,128]{3,2,1,0:T(8,128)}, f32[2,17,16,128]{3,2,1,0:T(8,128)S(1)}, u32[]{:S(2)}, u32[]{:S(2)}) collective-permute-start(f32[2,17,16,128]{3,2,1,0:T(8,128)} %head.2), channel_id=1, source_target_pairs={{1,0},{2,1},{3,2},{4,3},{5,4},{6,5},{7,6},{9,8},{10,9},{11,10},{12... | collective-permute-start | bytes 835592 | tf_op jit(solution)/shard_map/ppermute | solution.py:26
  19.1 16.6 %collective-permute-start = (bf16[3,8192]{1,0:T(4,128)(2,1)S(1)}, bf16[3,8192]{1,0:T(4,128)(2,1)S(1)}, u32[]{:S(2)}, u32[]{:S(2)}) collective-permute-start(bf16[3,8192]{1,0:T(4,128)(2,1)S(1)} %slice_bitcast_fusion), channel_id=1, source_target_pairs={{0,1},{1,2},{2,3},{3,4},{4,5},{5,6},{6,7},{8,9},{9,10},{10,11},{11... | collective-permute-start | bytes 147464 | tf_op jit(solution)/shard_map/ppermute | solution.py:26
  33.7 51.8 %collective-permute-start.7 = (f32[2,17,16,128]{3,2,1,0:T(8,128)}, f32[2,17,16,128]{3,2,1,0:T(8,128)S(1)}, u32[]{:S(2)}, u32[]{:S(2)}) collective-permute-start(f32[2,17,16,128]{3,2,1,0:T(8,128)} %head.3), channel_id=1, source_target_pairs={{3,0},{4,1},{5,2},{6,3},{7,4},{11,8},{12,9},{13,10},{14,11},{15,12... | collective-permute-start | bytes 835592 | tf_op jit(solution)/shard_map/ppermute | solution.py:26
  35.6 3.9 %copy-start.6 = (bf16[3,8192]{1,0:T(4,128)(2,1)}, bf16[3,8192]{1,0:T(4,128)(2,1)S(1)}, u32[]{:S(2)}) copy-start(bf16[3,8192]{1,0:T(4,128)(2,1)S(1)} %collective-permute-done.hist_ref) | copy-start | bytes 147460
  35.6 49.9 %collective-permute-start.6 = (f32[2,17,16,128]{3,2,1,0:T(8,128)}, f32[2,17,16,128]{3,2,1,0:T(8,128)S(1)}, u32[]{:S(2)}, u32[]{:S(2)}) collective-permute-start(f32[2,17,16,128]{3,2,1,0:T(8,128)} %head.3), channel_id=1, source_target_pairs={{2,0},{3,1},{4,2},{5,3},{6,4},{7,5},{10,8},{11,9},{12,10},{13,11},... | collective-permute-start | bytes 835592 | tf_op jit(solution)/shard_map/ppermute | solution.py:26
  37.6 2.0 %copy-start.2 = (f32[2,17,16,128]{3,2,1,0:T(8,128)}, f32[2,17,16,128]{3,2,1,0:T(8,128)S(1)}, u32[]{:S(2)}) copy-start(f32[2,17,16,128]{3,2,1,0:T(8,128)S(1)} %collective-permute-done.3.next3_ref) | copy-start | bytes 835588
  37.6 47.9 %collective-permute-start.5 = (f32[2,17,16,128]{3,2,1,0:T(8,128)}, f32[2,17,16,128]{3,2,1,0:T(8,128)S(1)}, u32[]{:S(2)}, u32[]{:S(2)}) collective-permute-start(f32[2,17,16,128]{3,2,1,0:T(8,128)} %head.3), channel_id=1, source_target_pairs={{1,0},{2,1},{3,2},{4,3},{5,4},{6,5},{7,6},{9,8},{10,9},{11,10},{12... | collective-permute-start | bytes 835592 | tf_op jit(solution)/shard_map/ppermute | solution.py:26
  39.5 0.7 copy-start.3
  39.5 0.8 copy-start.5
  82.4 45.8 %collective-permute-start.4 = (bf16[128,4096]{1,0:T(8,128)(2,1)}, bf16[128,4096]{1,0:T(8,128)(2,1)S(1)}, u32[]{:S(2)}, u32[]{:S(2)}) collective-permute-start(bf16[128,4096]{1,0:T(8,128)(2,1)} %get-tuple-element.23), channel_id=1, source_target_pairs={{8,0},{16,8},{24,16},{9,1},{17,9},{25,17},{10,2},{18,10},{26,18},{... | collective-permute-start | bytes 3145736 | tf_op jit(solution)/shard_map/ppermute | solution.py:26
  85.5 0.7 copy-start
  85.5 0.8 copy-start.1
  85.5 0.9 copy-start.4
  128.2 38.3 %all-to-all-start = ((f32[8,24,1024]{2,1,0:T(8,128)}), f32[8,24,1024]{2,1,0:T(8,128)S(1)}, u32[]{:S(2)}, u32[]{:S(2)}) async-start(f32[8,24,1024]{2,1,0:T(8,128)} %get-tuple-element.37), calls=%async_computation | async-start | bytes 1572864 | tf_op jit(solution)/shard_map/all_to_all | solution.py:500
  134.2 27.9 %collective-permute-start.8 = (bf16[128,4096]{1,0:T(8,128)(2,1)}, bf16[128,4096]{1,0:T(8,128)(2,1)S(1)}, u32[]{:S(2)}, u32[]{:S(2)}) collective-permute-start(bf16[128,4096]{1,0:T(8,128)(2,1)} %get-tuple-element.29), channel_id=1, source_target_pairs={{8,0},{16,8},{24,16},{9,1},{17,9},{25,17},{10,2},{18,10},{26,18},{... | collective-permute-start | bytes 3145736 | tf_op jit(solution)/shard_map/ppermute | solution.py:26
  136.1 28.8 %collective-permute-start.9 = (f32[3,8192]{1,0:T(4,128)}, f32[3,8192]{1,0:T(4,128)S(1)}, u32[]{:S(2)}, u32[]{:S(2)}) collective-permute-start(f32[3,8192]{1,0:T(4,128)} %get-tuple-element.33), channel_id=1, source_target_pairs={{8,0},{16,8},{24,16},{9,1},{17,9},{25,17},{10,2},{18,10},{26,18},{... | collective-permute-start | bytes 294920 | tf_op jit(solution)/shard_map/ppermute | solution.py:26
  138.1 27.0 %collective-permute-start.10 = (f32[3,8192]{1,0:T(4,128)}, f32[3,8192]{1,0:T(4,128)S(1)}, u32[]{:S(2)}, u32[]{:S(2)}) collective-permute-start(f32[3,8192]{1,0:T(4,128)} %get-tuple-element.34), channel_id=1, source_target_pairs={{9,0},{10,1},{11,2},{12,3},{13,4},{14,5},{15,6},{17,8},{18,9},{19,... | collective-permute-start | bytes 294920 | tf_op jit(solution)/shard_map/ppermute | solution.py:499

commit v5 on v4

--- a/solution.py
+++ b/solution.py
@@ -55,7 +55,8 @@
 
 
 def spread(ref, row, group):
-    return ref[pl.ds(row, group, stride=0), :]
+    one = ref[pl.ds(row, 8, stride=0), :]
+    return jnp.concatenate([one] * (group // 8), axis=0)
 
 
 def gather_positions(src_ref, dst, group, first=0):
@@ -157,11 +158,11 @@
 
 def main_kernel(group, part, many, place_ref, len_ref, maps_ref, x_ref, hist_ref, dt_ref, gy_ref,
                 start_ref, alog_ref, cw_ref, cb_ref, sk_ref, next_ref, next2_ref, next3_ref, *rest):
-    maps_before = rest[-26] if len(rest) > 25 else None
-    rest = rest[-25:]
+    maps_before = rest[-28] if len(rest) > 27 else None
+    rest = rest[-27:]
     (gx_ref, gdt_ref, mine_ref, spill_ref, gp_ref, gm_ref,
      keep_t, maps_t, x_t, sig_t, gy_t, a2_s, small_s, start_s, gin_s,
-     step_t, du_t, u_t, slope_t, w_t, v_t, gc_t, h_s, acc_s, gp_s) = rest
+     step_t, du_t, u_t, slope_t, w_t, v_t, gc_t, h_s, accb_s, accc_s, gp_s, dec_s) = rest
     rows = x_ref.shape[0]
     states = alog_ref.shape[0]
     f32 = jnp.float32
@@ -175,7 +176,8 @@
         fill_maps(maps_ref, maps_t)
 
     gather_positions(x_ref, x_t, group, 3)
-    gather_positions(gy_ref, gy_t, group)
+    gather_positions(gy_ref, gy_t, group, 1)
+    gy_t[0:1] = jnp.zeros((1, group, LANES), f32)
     gather_positions(dt_ref, step_t, group)
     a2_s[...] = (-LOG2E * jnp.exp(alog_ref[...])).reshape(states, group, LANES)
     start_s[...] = start_ref[...].reshape(states, group, LANES)
@@ -233,9 +235,6 @@
         for lo in range(0, states, part):
             hi = lo + part
 
-            for n in range(lo, hi):
-                h_s[0, n - lo] = start_s[n]
-
             def forward(t, hs):
                 step = step_t[t]
                 du = du_t[t]
@@ -243,30 +242,36 @@
                 for n in range(lo, hi):
                     decay = jnp.exp2(step * a2_s[n])
                     h = decay * hs[n - lo] + spread(maps_t, n * rows + t, group) * du
-                    h_s[t + 1, n - lo] = h
+                    h_s[t, n - lo] = hs[n - lo]
+                    dec_s[t, n - lo] = decay
                     out.append(h)
                 return tuple(out)
 
-            lax.fori_loop(0, rows, forward, tuple(start_s[n] for n in range(lo, hi)), unroll=8)
+            final = lax.fori_loop(
+                0, rows, forward, tuple(start_s[n] for n in range(lo, hi)), unroll=16)
+            for n in range(lo, hi):
+                put(accc_s, n, rows, fold(final[n - lo] * gy_t[rows]))
 
             def backward(i, carry):
                 cars, rates = carry
                 t = rows - 1 - i
                 step = step_t[t]
                 du = du_t[t]
-                y = gy_t[t]
+                y = gy_t[t + 1]
+                y_before = gy_t[t]
                 new_cars, new_rates = [], []
                 w = None if lo == 0 else gc_t[t + 3]
                 v = None if lo == 0 else v_t[t]
                 for n in range(lo, hi):
                     m = n - lo
                     g = spread(maps_t, (states + n) * rows + t, group) * y + cars[m]
-                    put(acc_s, n, t, fold(g * du))
-                    put(acc_s, states + n, t, fold(h_s[t + 1, m] * y))
+                    put(accb_s, n, t, fold(g * du))
+                    h = h_s[t, m]
+                    put(accc_s, n, t, fold(h * y_before))
                     bg = spread(maps_t, n * rows + t, group) * g
                     w = bg if w is None else w + bg
-                    car = jnp.exp2(step * a2_s[n]) * g
-                    aq = a2_s[n] * (car * h_s[t, m])
+                    car = dec_s[t, m] * g
+                    aq = a2_s[n] * (car * h)
                     v = aq if v is None else v + aq
                     new_cars.append(car)
                     new_rates.append(rates[m] + step * aq)
@@ -276,7 +281,7 @@
 
             _, rates = lax.fori_loop(
                 0, rows, backward,
-                (tuple(gin_s[n] for n in range(lo, hi)), (zero,) * part), unroll=4)
+                (tuple(gin_s[n] for n in range(lo, hi)), (zero,) * part), unroll=8)
             for n in range(lo, hi):
                 gp_s[n] = rates[n - lo] * LN2
 
@@ -293,7 +298,7 @@
         taps = list(carry)
         t = at_chunk(rows // CHUNK - 1 - i, CHUNK)
         for k in range(CHUNK - 1, -1, -1):
-            y = gy_t[t + k]
+            y = gy_t[t + k + 1]
             u = u_t[t + k]
             w = gc_t[t + k + 3]
             grad_u = small_s[5] * y + w_t[t + k] * w
@@ -341,13 +346,16 @@
         return [jnp.where(low, a, b) + pltpu.roll(jnp.where(low, b, a), shift, 0)
                 for a, b in zip(parts[::2], parts[1::2])]
 
-    def add_sublanes(n, _):
-        for tb in range(rows // 8):
-            parts = [acc_s[n, tb * 8 + k] for k in range(8)]
-            for shift in (1, 2, 4):
-                parts = pair_up(parts, shift)
-            maps_t[pl.ds(n * rows + tb * 8, 8), :] = parts[0]
-        return 0
+    def add_sublanes(ref, ahead, base):
+        def add_state(n, _):
+            for tb in range(rows // 8):
+                parts = [ref[n, tb * 8 + k + ahead] for k in range(8)]
+                for shift in (1, 2, 4):
+                    parts = pair_up(parts, shift)
+                maps_t[pl.ds((base + n) * rows + tb * 8, 8), :] = parts[0]
+            return 0
+
+        lax.fori_loop(0, states, add_state, 0)
 
     def add_lanes(n, _):
         flat = maps_t[pl.ds(at_chunk(n, rows), rows), :].T
@@ -359,7 +367,8 @@
 
     @pl.when(pl.program_id(0) == pl.num_programs(0) - 1)
     def _():
-        lax.fori_loop(0, 2 * states, add_sublanes, 0)
+        add_sublanes(accb_s, 0, 0)
+        add_sublanes(accc_s, 1, states)
         lax.fori_loop(0, 2 * states, add_lanes, 0, unroll=4)
 
 
@@ -416,15 +425,18 @@
             pltpu.VMEM((rows + 3 * PAST, LANES), f32),
             pltpu.VMEM((2 * states * rows + 8, LANES), f32),
             pltpu.VMEM((rows + 3, group, LANES), f32),
-            table, table,
+            table,
+            pltpu.VMEM((rows + 1, group, LANES), f32),
             vectors,
             pltpu.VMEM((9, group, LANES), f32),
             vectors, vectors,
             table, table, table, table, table, table,
             pltpu.VMEM((rows + 6, group, LANES), f32),
-            pltpu.VMEM((rows + 1, part, group, LANES), f32),
-            pltpu.VMEM((2 * states, rows, 8, LANES), f32),
+            pltpu.VMEM((rows, part, group, LANES), f32),
+            pltpu.VMEM((states, rows, 8, LANES), f32),
+            pltpu.VMEM((states, rows + 1, 8, LANES), f32),
             pltpu.VMEM((params, group, LANES), f32),
+            pltpu.VMEM((rows, part, group, LANES), f32),
         ],
         input_output_aliases=aliases,
         compiler_params=pltpu.CompilerParams(
@@ -487,7 +499,7 @@
     arrived = []
     for c in range(calls):
         gx, *carried = main_call(
-            group, 8, shards, c * many, many, here, doc_lengths, maps, x, hist, dt, gy,
+            group, 4, shards, c * many, many, here, doc_lengths, maps, x, hist, dt, gy,
             saved_states[0, 0], a_log[0], conv_weight[0], conv_bias, skip_gain, heads[c], carried)
         arrived.append(shift_to(gx, "pipe", -1))
     gdt, mine, spill, params, grad_maps = carried
@@ -497,7 +509,13 @@
     pairs = [(s * shards + k, (s - 1) * shards + k - 1)
              for s in range(1, sections) for k in range(1, shards)]
     spilled = lax.ppermute(spill, ("pipe", "ctx"), pairs)
-    shares = lax.all_to_all(params, "ctx", 0, 0, tiled=True)
+    sides = params.reshape((shards // 2, 2) + params.shape[1:])
+    side = me % 2
+    given = lax.dynamic_index_in_dim(sides, 1 - side, 1, keepdims=False)
+    got = lax.ppermute(given, "ctx", [(k, k ^ 1) for k in range(shards)])
+    half = lax.dynamic_index_in_dim(sides, side, 1, keepdims=False) + got
+    groups = [list(range(k, shards, 2)) for k in range(2)]
+    shares = lax.all_to_all(half, "ctx", 0, 0, tiled=True, axis_index_groups=groups)
     shares = jnp.sum(shares, axis=0)[:states + 6]
     upstream = join_call(arrived, mine, spilled)
     return upstream[None], gdt[None], grad_maps.reshape(1, 2, states, rows), shares[None]

time: 170 us -> 162 us (0.953)
  waiting for transfers between devices: 25.1 us -> 16.8 us
  Pallas kernels: 107 us -> 103 us
  other arithmetic: 0.04 us -> 1.82 us
    ppermute x10, waiting for transfers between devices: 24.9 us -> 16.4 us  [shift_to(): return lax.ppermute(x, axis, pairs)]
    pallas_call x2, Pallas kernels: 83.9 us -> 79.9 us  [main_call(): pl.pallas_call(functools.partial(main_kernel, group, part, blocks > 1), g...]
    add x0 -> x1, other arithmetic: none -> 1.8 us  [on_device(): half = lax.dynamic_index_in_dim(sides, side, 1, keepdims=False) + got]
  transfers between devices with their start and end apart: 12 -> 13, of which waited for: 3 -> 3; matrix products, arithmetic and copies ran while one was open for 1% -> 2% of each run, Pallas kernels for 58% -> 58%
where the time goes in v5:
time: 162 us; the launch traced here: 159 us
  Pallas kernels  103 us (64%)
  starting transfers between devices  31.1 us (19%)
  waiting for transfers between devices  16.8 us (10%)
  local copies, waits for them, and re-layouts  4.37 us (3%)
  other arithmetic  1.82 us (1%)
    pallas_call x2, Pallas kernels, main_call(): pl.pallas_call(functools.partial(main_kernel, group, part, blocks > 1), g...  79.9 us
    ppermute x10, starting transfers between devices, shift_to(): return lax.ppermute(x, axis, pairs)  22.8 us
    pallas_call x2, Pallas kernels, head_call(): pl.pallas_call(functools.partial(head_kernel, group, 8), grid=(blocks,),...  22 us
    ppermute x10, waiting for transfers between devices, shift_to(): return lax.ppermute(x, axis, pairs)  16.4 us
    all_to_all x1, starting transfers between devices, on_device(): lax.all_to_all(half, 'ctx', 0, 0, tiled=True, axis_index_groups=groups)  5.46 us
  transfers between devices with their start and end apart: 13, of which 3 were waited for; matrix products, arithmetic and copies ran while one was open for 2% of the time, Pallas kernels for 58%

profile of v5, /device:TPU:13, one launch (start us, length us, event | category | flops | bytes accessed | tf_op | source)
XLA Modules:
  0.0 158.5 jit_solution(18031304101807948884)
XLA Ops:
  0.6 11.0 %head.2 = f32[2,17,16,128]{3,2,1,0:T(8,128)} custom-call(s32[1]{0:T(128)} %bitcast.place_ref, s32[1,8]{1,0:T(1,128)} %len_ref.7, f32[32,128]{1,0:T(8,128)} %bitcast.41, bf16[128,8192]{1,0:T(8,128)(2,1)} %bitcast.25, bf16[128,8192]{1,0:T(8,128)(2,1)} %bitcast.29, f32[16,8192]{1,0:T(8,128)} %bitcast.35), custom_call_target="tpu_custom_call" | custom-call | flops 8388608000 | bytes 33554432 | tf_op jit(solution)/shard_map/head/pallas_call | solution.py:135
  11.6 2.6 %collective-permute-start.1 = (f32[2,17,16,128]{3,2,1,0:T(8,128)}, f32[2,17,16,128]{3,2,1,0:T(8,128)S(1)}, u32[]{:S(2)}, u32[]{:S(2)}) collective-permute-start(f32[2,17,16,128]{3,2,1,0:T(8,128)} %head.2), channel_id=1, source_target_pairs={{1,0},{2,1},{3,2},{4,3},{5,4},{6,5},{7,6},{9,8},{10,9},{11,10},{12... | collective-permute-start | bytes 835592 | tf_op jit(solution)/shard_map/ppermute | solution.py:26
  14.2 2.1 %collective-permute-start.2 = (f32[2,17,16,128]{3,2,1,0:T(8,128)}, f32[2,17,16,128]{3,2,1,0:T(8,128)S(1)}, u32[]{:S(2)}, u32[]{:S(2)}) collective-permute-start(f32[2,17,16,128]{3,2,1,0:T(8,128)} %head.2), channel_id=1, source_target_pairs={{2,0},{3,1},{4,2},{5,3},{6,4},{7,5},{10,8},{11,9},{12,10},{13,11},... | collective-permute-start | bytes 835592 | tf_op jit(solution)/shard_map/ppermute | solution.py:26
  16.3 1.9 %collective-permute-start.3 = (f32[2,17,16,128]{3,2,1,0:T(8,128)}, f32[2,17,16,128]{3,2,1,0:T(8,128)S(1)}, u32[]{:S(2)}, u32[]{:S(2)}) collective-permute-start(f32[2,17,16,128]{3,2,1,0:T(8,128)} %head.2), channel_id=1, source_target_pairs={{3,0},{4,1},{5,2},{6,3},{7,4},{11,8},{12,9},{13,10},{14,11},{15,12... | collective-permute-start | bytes 835592 | tf_op jit(solution)/shard_map/ppermute | solution.py:26
  18.2 0.9 slice_bitcast_fusion
  19.2 3.4 %collective-permute-start = (bf16[3,8192]{1,0:T(4,128)(2,1)S(1)}, bf16[3,8192]{1,0:T(4,128)(2,1)S(1)}, u32[]{:S(2)}, u32[]{:S(2)}) collective-permute-start(bf16[3,8192]{1,0:T(4,128)(2,1)S(1)} %slice_bitcast_fusion), channel_id=1, source_target_pairs={{0,1},{1,2},{2,3},{3,4},{4,5},{5,6},{6,7},{8,9},{9,10},{10,11},{11... | collective-permute-start | bytes 147464 | tf_op jit(solution)/shard_map/ppermute | solution.py:26
  22.5 11.0 %head.3 = f32[2,17,16,128]{3,2,1,0:T(8,128)} custom-call(s32[1]{0:T(128)} %bitcast.place_ref, s32[1,8]{1,0:T(1,128)} %len_ref.7, f32[32,128]{1,0:T(8,128)} %bitcast.42, bf16[128,8192]{1,0:T(8,128)(2,1)} %bitcast.26, bf16[128,8192]{1,0:T(8,128)(2,1)} %bitcast.30, f32[16,8192]{1,0:T(8,128)} %bitcast.36), custom_call_target="tpu_custom_call" | custom-call | flops 8388608000 | bytes 33554432 | tf_op jit(solution)/shard_map/head/pallas_call | solution.py:135
  33.5 1.9 %collective-permute-start.5 = (f32[2,17,16,128]{3,2,1,0:T(8,128)}, f32[2,17,16,128]{3,2,1,0:T(8,128)S(1)}, u32[]{:S(2)}, u32[]{:S(2)}) collective-permute-start(f32[2,17,16,128]{3,2,1,0:T(8,128)} %head.3), channel_id=1, source_target_pairs={{1,0},{2,1},{3,2},{4,3},{5,4},{6,5},{7,6},{9,8},{10,9},{11,10},{12... | collective-permute-start | bytes 835592 | tf_op jit(solution)/shard_map/ppermute | solution.py:26
  35.5 1.9 %collective-permute-start.6 = (f32[2,17,16,128]{3,2,1,0:T(8,128)}, f32[2,17,16,128]{3,2,1,0:T(8,128)S(1)}, u32[]{:S(2)}, u32[]{:S(2)}) collective-permute-start(f32[2,17,16,128]{3,2,1,0:T(8,128)} %head.3), channel_id=1, source_target_pairs={{2,0},{3,1},{4,2},{5,3},{6,4},{7,5},{10,8},{11,9},{12,10},{13,11},... | collective-permute-start | bytes 835592 | tf_op jit(solution)/shard_map/ppermute | solution.py:26
  37.4 1.9 %collective-permute-start.7 = (f32[2,17,16,128]{3,2,1,0:T(8,128)}, f32[2,17,16,128]{3,2,1,0:T(8,128)S(1)}, u32[]{:S(2)}, u32[]{:S(2)}) collective-permute-start(f32[2,17,16,128]{3,2,1,0:T(8,128)} %head.3), channel_id=1, source_target_pairs={{3,0},{4,1},{5,2},{6,3},{7,4},{11,8},{12,9},{13,10},{14,11},{15,12... | collective-permute-start | bytes 835592 | tf_op jit(solution)/shard_map/ppermute | solution.py:26
  39.4 0.7 copy-done.2
  40.2 40.1 %main.2 = (bf16[128,4096]{1,0:T(8,128)(2,1)}, bf16[128,8192]{1,0:T(8,128)(2,1)}, f32[3,8192]{1,0:T(4,128)}, f32[3,8192]{1,0:T(4,128)}, f32[8,24,1024]{2,1,0:T(8,128)}, /*index=5*/f32[32,128]{1,0:T(8,128)}) custom-call(s32[1]{0:T(128)} %bitcast.place_ref, s32[1,8]{1,0:T(1,128)} %len_ref.7, f32[32,128]{1,0:T(8,128)} %bitcast.43, bf16[128,8192]{1,0:T(8,128)(2,1)} %bitcast.23, ...), custom_call_target="tpu_custom_call" | custom-call | flops 41943040000 | bytes 150994944 | tf_op jit(solution)/shard_map/main/pallas_call | solution.py:406
  80.3 3.1 %collective-permute-start.4 = (bf16[128,4096]{1,0:T(8,128)(2,1)}, bf16[128,4096]{1,0:T(8,128)(2,1)S(1)}, u32[]{:S(2)}, u32[]{:S(2)}) collective-permute-start(bf16[128,4096]{1,0:T(8,128)(2,1)} %get-tuple-element.23), channel_id=1, source_target_pairs={{8,0},{16,8},{24,16},{9,1},{17,9},{25,17},{10,2},{18,10},{26,18},{... | collective-permute-start | bytes 3145736 | tf_op jit(solution)/shard_map/ppermute | solution.py:26
  84.3 39.8 %main.3 = (bf16[128,4096]{1,0:T(8,128)(2,1)}, bf16[128,8192]{1,0:T(8,128)(2,1)}, f32[3,8192]{1,0:T(4,128)}, f32[3,8192]{1,0:T(4,128)}, f32[8,24,1024]{2,1,0:T(8,128)}, /*index=5*/f32[32,128]{1,0:T(8,128)}) custom-call(s32[1]{0:T(128)} %bitcast.place_ref, ...), custom_call_target="tpu_custom_call", output_to_operand_aliasing={{1}: (15, {}), {2}: (16, {}), {3}: (17, {}), {4}: (18, {}),... | custom-call | flops 41943040000 | bytes 150994944 | tf_op jit(solution)/shard_map/main/pallas_call | solution.py:406
  124.1 1.1 dynamic-slice_bitcast_fusion
  125.3 2.2 %collective-permute-start.8 = (bf16[128,4096]{1,0:T(8,128)(2,1)}, bf16[128,4096]{1,0:T(8,128)(2,1)S(1)}, u32[]{:S(2)}, u32[]{:S(2)}) collective-permute-start(bf16[128,4096]{1,0:T(8,128)(2,1)} %get-tuple-element.29), channel_id=1, source_target_pairs={{8,0},{16,8},{24,16},{9,1},{17,9},{25,17},{10,2},{18,10},{26,18},{... | collective-permute-start | bytes 3145736 | tf_op jit(solution)/shard_map/ppermute | solution.py:26
  127.5 1.8 %bitcast_add_fusion = f32[4,24,1024]{2,1,0:T(8,128)} fusion(f32[4,24,1024]{2,1,0:T(8,128)S(1)} %collective-permute-done.11, f32[4,2,24,1024]{3,2,1,0:T(8,128)} %bitcast.21, s32[]{:T(128)S(6)} %select_n.15), kind=kLoop, calls=%fused_computation | loop fusion | flops 98304 | bytes 1179652 | tf_op jit(solution)/shard_map/add | solution.py:516
  129.3 5.5 %all-to-all-start = ((f32[4,24,1024]{2,1,0:T(8,128)}), f32[4,24,1024]{2,1,0:T(8,128)S(1)}, u32[]{:S(2)}, u32[]{:S(2)}) async-start(f32[4,24,1024]{2,1,0:T(8,128)} %bitcast_add_fusion), calls=%async_computation | async-start | bytes 786432 | tf_op jit(solution)/shard_map/all_to_all | solution.py:518
  134.8 1.9 %collective-permute-start.9 = (f32[3,8192]{1,0:T(4,128)S(1)}, f32[3,8192]{1,0:T(4,128)S(1)}, u32[]{:S(2)}, u32[]{:S(2)}) collective-permute-start(f32[3,8192]{1,0:T(4,128)S(1)} %copy-done.6), channel_id=1, source_target_pairs={{8,0},{16,8},{24,16},{9,1},{17,9},{25,17},{10,2},{18,10},{26,18},{... | collective-permute-start | bytes 294920 | tf_op jit(solution)/shard_map/ppermute | solution.py:26
  136.7 2.8 %collective-permute-start.10 = (f32[3,8192]{1,0:T(4,128)S(1)}, f32[3,8192]{1,0:T(4,128)S(1)}, u32[]{:S(2)}, u32[]{:S(2)}) collective-permute-start(f32[3,8192]{1,0:T(4,128)S(1)} %copy-done.7), channel_id=1, source_target_pairs={{9,0},{10,1},{11,2},{12,3},{13,4},{14,5},{15,6},{17,8},{18,9},{19,... | collective-permute-start | bytes 294920 | tf_op jit(solution)/shard_map/ppermute | solution.py:511
  139.5 13.6 %collective-permute-done.8.refs_1_ = bf16[128,4096]{1,0:T(8,128)(2,1)S(1)} collective-permute-done((bf16[128,4096]{1,0:T(8,128)(2,1)}, bf16[128,4096]{1,0:T(8,128)(2,1)S(1)}, u32[]{:S(2)}, u32[]{:S(2)}) %collective-permute-start.8) | collective-permute-done | bytes 1048608 | tf_op jit(solution)/shard_map/ppermute | solution.py:26
  153.1 2.8 %collective-permute-done.9.refs_2_ = f32[3,8192]{1,0:T(4,128)S(1)} collective-permute-done((f32[3,8192]{1,0:T(4,128)S(1)}, f32[3,8192]{1,0:T(4,128)S(1)}, u32[]{:S(2)}, u32[]{:S(2)}) %collective-permute-start.9) | collective-permute-done | bytes 98336 | tf_op jit(solution)/shard_map/ppermute | solution.py:26
  156.3 1.5 join.1
  157.8 0.7 broadcast_in_dim.11
  (30 shorter events, 1.5 us)
Async XLA Ops:
  11.6 25.8 %collective-permute-start.1 = (f32[2,17,16,128]{3,2,1,0:T(8,128)}, f32[2,17,16,128]{3,2,1,0:T(8,128)S(1)}, u32[]{:S(2)}, u32[]{:S(2)}) collective-permute-start(f32[2,17,16,128]{3,2,1,0:T(8,128)} %head.2), channel_id=1, source_target_pairs={{1,0},{2,1},{3,2},{4,3},{5,4},{6,5},{7,6},{9,8},{10,9},{11,10},{12... | collective-permute-start | bytes 835592 | tf_op jit(solution)/shard_map/ppermute | solution.py:26
  14.2 25.2 %collective-permute-start.2 = (f32[2,17,16,128]{3,2,1,0:T(8,128)}, f32[2,17,16,128]{3,2,1,0:T(8,128)S(1)}, u32[]{:S(2)}, u32[]{:S(2)}) collective-permute-start(f32[2,17,16,128]{3,2,1,0:T(8,128)} %head.2), channel_id=1, source_target_pairs={{2,0},{3,1},{4,2},{5,3},{6,4},{7,5},{10,8},{11,9},{12,10},{13,11},... | collective-permute-start | bytes 835592 | tf_op jit(solution)/shard_map/ppermute | solution.py:26
  16.3 23.1 %collective-permute-start.3 = (f32[2,17,16,128]{3,2,1,0:T(8,128)}, f32[2,17,16,128]{3,2,1,0:T(8,128)S(1)}, u32[]{:S(2)}, u32[]{:S(2)}) collective-permute-start(f32[2,17,16,128]{3,2,1,0:T(8,128)} %head.2), channel_id=1, source_target_pairs={{3,0},{4,1},{5,2},{6,3},{7,4},{11,8},{12,9},{13,10},{14,11},{15,12... | collective-permute-start | bytes 835592 | tf_op jit(solution)/shard_map/ppermute | solution.py:26
  19.2 16.3 %collective-permute-start = (bf16[3,8192]{1,0:T(4,128)(2,1)S(1)}, bf16[3,8192]{1,0:T(4,128)(2,1)S(1)}, u32[]{:S(2)}, u32[]{:S(2)}) collective-permute-start(bf16[3,8192]{1,0:T(4,128)(2,1)S(1)} %slice_bitcast_fusion), channel_id=1, source_target_pairs={{0,1},{1,2},{2,3},{3,4},{4,5},{5,6},{6,7},{8,9},{9,10},{10,11},{11... | collective-permute-start | bytes 147464 | tf_op jit(solution)/shard_map/ppermute | solution.py:26
  33.5 49.8 %collective-permute-start.5 = (f32[2,17,16,128]{3,2,1,0:T(8,128)}, f32[2,17,16,128]{3,2,1,0:T(8,128)S(1)}, u32[]{:S(2)}, u32[]{:S(2)}) collective-permute-start(f32[2,17,16,128]{3,2,1,0:T(8,128)} %head.3), channel_id=1, source_target_pairs={{1,0},{2,1},{3,2},{4,3},{5,4},{6,5},{7,6},{9,8},{10,9},{11,10},{12... | collective-permute-start | bytes 835592 | tf_op jit(solution)/shard_map/ppermute | solution.py:26
  35.5 3.9 %copy-start.8 = (bf16[3,8192]{1,0:T(4,128)(2,1)}, bf16[3,8192]{1,0:T(4,128)(2,1)S(1)}, u32[]{:S(2)}) copy-start(bf16[3,8192]{1,0:T(4,128)(2,1)S(1)} %collective-permute-done.hist_ref) | copy-start | bytes 147460
  35.5 47.9 %collective-permute-start.6 = (f32[2,17,16,128]{3,2,1,0:T(8,128)}, f32[2,17,16,128]{3,2,1,0:T(8,128)S(1)}, u32[]{:S(2)}, u32[]{:S(2)}) collective-permute-start(f32[2,17,16,128]{3,2,1,0:T(8,128)} %head.3), channel_id=1, source_target_pairs={{2,0},{3,1},{4,2},{5,3},{6,4},{7,5},{10,8},{11,9},{12,10},{13,11},... | collective-permute-start | bytes 835592 | tf_op jit(solution)/shard_map/ppermute | solution.py:26
  37.4 2.0 %copy-start.1 = (f32[2,17,16,128]{3,2,1,0:T(8,128)}, f32[2,17,16,128]{3,2,1,0:T(8,128)S(1)}, u32[]{:S(2)}) copy-start(f32[2,17,16,128]{3,2,1,0:T(8,128)S(1)} %collective-permute-done.1.next_ref) | copy-start | bytes 835588
  37.4 46.0 %collective-permute-start.7 = (f32[2,17,16,128]{3,2,1,0:T(8,128)}, f32[2,17,16,128]{3,2,1,0:T(8,128)S(1)}, u32[]{:S(2)}, u32[]{:S(2)}) collective-permute-start(f32[2,17,16,128]{3,2,1,0:T(8,128)} %head.3), channel_id=1, source_target_pairs={{3,0},{4,1},{5,2},{6,3},{7,4},{11,8},{12,9},{13,10},{14,11},{15,12... | collective-permute-start | bytes 835592 | tf_op jit(solution)/shard_map/ppermute | solution.py:26
  39.4 0.7 copy-start.2
  39.4 0.8 copy-start.3
  80.3 43.8 %collective-permute-start.4 = (bf16[128,4096]{1,0:T(8,128)(2,1)}, bf16[128,4096]{1,0:T(8,128)(2,1)S(1)}, u32[]{:S(2)}, u32[]{:S(2)}) collective-permute-start(bf16[128,4096]{1,0:T(8,128)(2,1)} %get-tuple-element.23), channel_id=1, source_target_pairs={{8,0},{16,8},{24,16},{9,1},{17,9},{25,17},{10,2},{18,10},{26,18},{... | collective-permute-start | bytes 3145736 | tf_op jit(solution)/shard_map/ppermute | solution.py:26
  83.4 0.7 copy-start
  83.4 0.8 copy-start.4
  83.4 0.9 copy-start.5
  124.1 10.7 %copy-start.6 = (f32[3,8192]{1,0:T(4,128)S(1)}, f32[3,8192]{1,0:T(4,128)}, u32[]{:S(2)}) copy-start(f32[3,8192]{1,0:T(4,128)} %get-tuple-element.33) | copy-start | bytes 294916
  124.1 12.6 %copy-start.7 = (f32[3,8192]{1,0:T(4,128)S(1)}, f32[3,8192]{1,0:T(4,128)}, u32[]{:S(2)}) copy-start(f32[3,8192]{1,0:T(4,128)} %get-tuple-element.34) | copy-start | bytes 294916
  125.2 2.3 %collective-permute-start.11 = (f32[4,24,1024]{2,1,0:T(8,128)S(1)}, f32[4,24,1024]{2,1,0:T(8,128)S(1)}, u32[]{:S(2)}, u32[]{:S(2)}) collective-permute-start(f32[4,24,1024]{2,1,0:T(8,128)S(1)} %dynamic-slice_bitcast_fusion), channel_id=1, source_target_pairs={{0,1},{1,0},{2,3},{3,2},{4,5},{5,4},{6,7},{7,6},{8,9},{9,8},{10,11... | collective-permute-start | bytes 1179656 | tf_op jit(solution)/shard_map/ppermute | solution.py:515
  125.3 27.7 %collective-permute-start.8 = (bf16[128,4096]{1,0:T(8,128)(2,1)}, bf16[128,4096]{1,0:T(8,128)(2,1)S(1)}, u32[]{:S(2)}, u32[]{:S(2)}) collective-permute-start(bf16[128,4096]{1,0:T(8,128)(2,1)} %get-tuple-element.29), channel_id=1, source_target_pairs={{8,0},{16,8},{24,16},{9,1},{17,9},{25,17},{10,2},{18,10},{26,18},{... | collective-permute-start | bytes 3145736 | tf_op jit(solution)/shard_map/ppermute | solution.py:26
  129.3 28.5 %all-to-all-start = ((f32[4,24,1024]{2,1,0:T(8,128)}), f32[4,24,1024]{2,1,0:T(8,128)S(1)}, u32[]{:S(2)}, u32[]{:S(2)}) async-start(f32[4,24,1024]{2,1,0:T(8,128)} %bitcast_add_fusion), calls=%async_computation | async-start | bytes 786432 | tf_op jit(solution)/shard_map/all_to_all | solution.py:518
  134.8 21.1 %collective-permute-start.9 = (f32[3,8192]{1,0:T(4,128)S(1)}, f32[3,8192]{1,0:T(4,128)S(1)}, u32[]{:S(2)}, u32[]{:S(2)}) collective-permute-start(f32[3,8192]{1,0:T(4,128)S(1)} %copy-done.6), channel_id=1, source_target_pairs={{8,0},{16,8},{24,16},{9,1},{17,9},{25,17},{10,2},{18,10},{26,18},{... | collective-permute-start | bytes 294920 | tf_op jit(solution)/shard_map/ppermute | solution.py:26
  136.7 19.6 %collective-permute-start.10 = (f32[3,8192]{1,0:T(4,128)S(1)}, f32[3,8192]{1,0:T(4,128)S(1)}, u32[]{:S(2)}, u32[]{:S(2)}) collective-permute-start(f32[3,8192]{1,0:T(4,128)S(1)} %copy-done.7), channel_id=1, source_target_pairs={{9,0},{10,1},{11,2},{12,3},{13,4},{14,5},{15,6},{17,8},{18,9},{19,... | collective-permute-start | bytes 294920 | tf_op jit(solution)/shard_map/ppermute | solution.py:511

commit v6 on v5

--- a/solution.py
+++ b/solution.py
@@ -372,7 +372,7 @@
         lax.fori_loop(0, 2 * states, add_lanes, 0, unroll=4)
 
 
-def main_call(group, part, shards, block, blocks, place, lengths, maps, x, hist, dt, gy, start,
+def main_call(group, part, shards, block, blocks, skip, place, lengths, maps, x, hist, dt, gy, start,
               alog, cw, cb, sk, heads, carried):
     rows, channels = x.shape
     states = alog.shape[0]
@@ -396,7 +396,7 @@
                 pl.BlockSpec((4, width), col),
                 pl.BlockSpec((1, width), col),
                 pl.BlockSpec((1, width), col)]
-    in_specs += [pl.BlockSpec((1, states + 1, group, LANES), lambda i: (i, 0, 0, 0))] * REACH
+    in_specs += [pl.BlockSpec((1, states + 1, group, LANES), lambda i: (skip + i, 0, 0, 0))] * REACH
     aliases = {}
     if carried is not None:
         aliases = {len(operands) + k: k + 1 for k in range(len(carried))}
@@ -450,19 +450,21 @@
 
 def join_kernel(count, *refs):
     out_ref = refs[-1]
-    rows, width = refs[0].shape
-    for b in range(count):
-        out_ref[:, b * width:(b + 1) * width] = refs[b][...]
+    rows = out_ref.shape[0]
+    at = 0
+    for ref in refs[:count]:
+        out_ref[:, at:at + ref.shape[1]] = ref[...]
+        at += ref.shape[1]
     tail = refs[count][...] + refs[count + 1][...]
     out_ref[rows - 3:rows, :] = tail.astype(out_ref.dtype)
 
 
 def join_call(blocks, mine, spilled):
     count = len(blocks)
-    rows, width = blocks[0].shape
+    rows = blocks[0].shape[0]
     return pl.pallas_call(
         functools.partial(join_kernel, count),
-        out_shape=jax.ShapeDtypeStruct((rows, count * width), blocks[0].dtype),
+        out_shape=jax.ShapeDtypeStruct((rows, mine.shape[1]), blocks[0].dtype),
         compiler_params=pltpu.CompilerParams(vmem_limit_bytes=16 * MIB),
         name="join",
     )(*blocks, mine, spilled)
@@ -487,24 +489,25 @@
     def after(value, *earlier):
         return lax.optimization_barrier((value,) + earlier)[0]
 
-    calls = 2
-    many = blocks // calls
+    many = blocks // 2
     here, heads = place, []
-    for c in range(calls):
-        own = head_call(group, c * many, many, here, doc_lengths, maps, dt, gy, a_log[0])
+    for first in (0, many):
+        own = head_call(group, first, many, here, doc_lengths, maps, dt, gy, a_log[0])
         heads.append([shift_to(own, "ctx", -d) for d in range(1, REACH + 1)])
         here = after(place, own)
 
+    calls = [(0, many, 0, heads[0])] + [(many + b, 1, b, heads[1]) for b in range(many)]
     carried = None
     arrived = []
-    for c in range(calls):
+    for block, count, skip, arriving in calls:
         gx, *carried = main_call(
-            group, 4, shards, c * many, many, here, doc_lengths, maps, x, hist, dt, gy,
-            saved_states[0, 0], a_log[0], conv_weight[0], conv_bias, skip_gain, heads[c], carried)
+            group, 4, shards, block, count, skip, here, doc_lengths, maps, x, hist, dt, gy,
+            saved_states[0, 0], a_log[0], conv_weight[0], conv_bias, skip_gain, arriving, carried)
         arrived.append(shift_to(gx, "pipe", -1))
     gdt, mine, spill, params, grad_maps = carried
-    mine, spill, params, _ = lax.optimization_barrier((mine, spill, params, arrived[-2]))
-
+    mine, spill, params, *_ = lax.optimization_barrier((mine, spill, params, *arrived[:-1]))
+
+    mine, spill, _ = lax.optimization_barrier((mine, spill, arrived[-1]))
     mine = shift_to(mine, "pipe", -1)
     pairs = [(s * shards + k, (s - 1) * shards + k - 1)
              for s in range(1, sections) for k in range(1, shards)]

time: 162 us -> 164 us (1.012)
  waiting for transfers between devices: 16.8 us -> 10.7 us
  Pallas kernels: 103 us -> 109 us
  starting transfers between devices: 31.1 us -> 34.6 us
    ppermute x10 -> x11, waiting for transfers between devices: 16.4 us -> 5.63 us  [shift_to(): return lax.ppermute(x, axis, pairs)]
    pallas_call x2 -> x3, Pallas kernels: 79.9 us -> 86 us  [main_call(): pl.pallas_call(functools.partial(main_kernel, group, part, blocks > 1), g...]
    ppermute x1, waiting for transfers between devices: 0.4 us -> 5.02 us  [on_device(): spilled = lax.ppermute(spill, ('pipe', 'ctx'), pairs)]
    ppermute x10 -> x11, starting transfers between devices: 22.8 us -> 25.6 us  [shift_to(): return lax.ppermute(x, axis, pairs)]
  transfers between devices with their start and end apart: 13 -> 14, of which waited for: 3 -> 2; matrix products, arithmetic and copies ran while one was open for 2% -> 2% of each run, Pallas kernels for 58% -> 61%
where the time goes in v6:
time: 164 us; the launch traced here: 162 us
  Pallas kernels  109 us (66%)
  starting transfers between devices  34.6 us (21%)
  waiting for transfers between devices  10.7 us (7%)
  local copies, waits for them, and re-layouts  4.39 us (3%)
  other arithmetic  1.84 us (1%)
    pallas_call x3, Pallas kernels, main_call(): pl.pallas_call(functools.partial(main_kernel, group, part, blocks > 1), g...  86 us
    ppermute x11, starting transfers between devices, shift_to(): return lax.ppermute(x, axis, pairs)  25.6 us
    pallas_call x2, Pallas kernels, head_call(): pl.pallas_call(functools.partial(head_kernel, group, 8), grid=(blocks,),...  22 us
    all_to_all x1, starting transfers between devices, on_device(): lax.all_to_all(half, 'ctx', 0, 0, tiled=True, axis_index_groups=groups)  5.76 us
    ppermute x11, waiting for transfers between devices, shift_to(): return lax.ppermute(x, axis, pairs)  5.63 us
    ppermute x1, waiting for transfers between devices, on_device(): spilled = lax.ppermute(spill, ('pipe', 'ctx'), pairs)  5.02 us
  transfers between devices with their start and end apart: 14, of which 2 were waited for; matrix products, arithmetic and copies ran while one was open for 2% of the time, Pallas kernels for 61%

profile of v6, /device:TPU:13, one launch (start us, length us, event | category | flops | bytes accessed | tf_op | source)
XLA Modules:
  0.0 161.9 jit_solution(7677269150303179881)
XLA Ops:
  0.6 11.0 %head.2 = f32[2,17,16,128]{3,2,1,0:T(8,128)} custom-call(s32[1]{0:T(128)} %bitcast.place_ref, s32[1,8]{1,0:T(1,128)} %len_ref.9, f32[32,128]{1,0:T(8,128)} %bitcast.47, bf16[128,8192]{1,0:T(8,128)(2,1)} %bitcast.26, bf16[128,8192]{1,0:T(8,128)(2,1)} %bitcast.31, f32[16,8192]{1,0:T(8,128)} %bitcast.39), custom_call_target="tpu_custom_call" | custom-call | flops 8388608000 | bytes 33554432 | tf_op jit(solution)/shard_map/head/pallas_call | solution.py:135
  11.6 2.6 %collective-permute-start.1 = (f32[2,17,16,128]{3,2,1,0:T(8,128)}, f32[2,17,16,128]{3,2,1,0:T(8,128)S(1)}, u32[]{:S(2)}, u32[]{:S(2)}) collective-permute-start(f32[2,17,16,128]{3,2,1,0:T(8,128)} %head.2), channel_id=1, source_target_pairs={{1,0},{2,1},{3,2},{4,3},{5,4},{6,5},{7,6},{9,8},{10,9},{11,10},{12... | collective-permute-start | bytes 835592 | tf_op jit(solution)/shard_map/ppermute | solution.py:26
  14.2 2.1 %collective-permute-start.2 = (f32[2,17,16,128]{3,2,1,0:T(8,128)}, f32[2,17,16,128]{3,2,1,0:T(8,128)S(1)}, u32[]{:S(2)}, u32[]{:S(2)}) collective-permute-start(f32[2,17,16,128]{3,2,1,0:T(8,128)} %head.2), channel_id=1, source_target_pairs={{2,0},{3,1},{4,2},{5,3},{6,4},{7,5},{10,8},{11,9},{12,10},{13,11},... | collective-permute-start | bytes 835592 | tf_op jit(solution)/shard_map/ppermute | solution.py:26
  16.3 1.9 %collective-permute-start.3 = (f32[2,17,16,128]{3,2,1,0:T(8,128)}, f32[2,17,16,128]{3,2,1,0:T(8,128)S(1)}, u32[]{:S(2)}, u32[]{:S(2)}) collective-permute-start(f32[2,17,16,128]{3,2,1,0:T(8,128)} %head.2), channel_id=1, source_target_pairs={{3,0},{4,1},{5,2},{6,3},{7,4},{11,8},{12,9},{13,10},{14,11},{15,12... | collective-permute-start | bytes 835592 | tf_op jit(solution)/shard_map/ppermute | solution.py:26
  18.2 0.9 slice_bitcast_fusion
  19.2 3.4 %collective-permute-start = (bf16[3,8192]{1,0:T(4,128)(2,1)S(1)}, bf16[3,8192]{1,0:T(4,128)(2,1)S(1)}, u32[]{:S(2)}, u32[]{:S(2)}) collective-permute-start(bf16[3,8192]{1,0:T(4,128)(2,1)S(1)} %slice_bitcast_fusion), channel_id=1, source_target_pairs={{0,1},{1,2},{2,3},{3,4},{4,5},{5,6},{6,7},{8,9},{9,10},{10,11},{11... | collective-permute-start | bytes 147464 | tf_op jit(solution)/shard_map/ppermute | solution.py:26
  22.5 11.0 %head.3 = f32[2,17,16,128]{3,2,1,0:T(8,128)} custom-call(s32[1]{0:T(128)} %bitcast.place_ref, s32[1,8]{1,0:T(1,128)} %len_ref.9, f32[32,128]{1,0:T(8,128)} %bitcast.48, bf16[128,8192]{1,0:T(8,128)(2,1)} %bitcast.27, bf16[128,8192]{1,0:T(8,128)(2,1)} %bitcast.32, f32[16,8192]{1,0:T(8,128)} %bitcast.40), custom_call_target="tpu_custom_call" | custom-call | flops 8388608000 | bytes 33554432 | tf_op jit(solution)/shard_map/head/pallas_call | solution.py:135
  33.5 1.9 %collective-permute-start.5 = (f32[2,17,16,128]{3,2,1,0:T(8,128)}, f32[2,17,16,128]{3,2,1,0:T(8,128)S(1)}, u32[]{:S(2)}, u32[]{:S(2)}) collective-permute-start(f32[2,17,16,128]{3,2,1,0:T(8,128)} %head.3), channel_id=1, source_target_pairs={{1,0},{2,1},{3,2},{4,3},{5,4},{6,5},{7,6},{9,8},{10,9},{11,10},{12... | collective-permute-start | bytes 835592 | tf_op jit(solution)/shard_map/ppermute | solution.py:26
  35.5 1.9 %collective-permute-start.6 = (f32[2,17,16,128]{3,2,1,0:T(8,128)}, f32[2,17,16,128]{3,2,1,0:T(8,128)S(1)}, u32[]{:S(2)}, u32[]{:S(2)}) collective-permute-start(f32[2,17,16,128]{3,2,1,0:T(8,128)} %head.3), channel_id=1, source_target_pairs={{2,0},{3,1},{4,2},{5,3},{6,4},{7,5},{10,8},{11,9},{12,10},{13,11},... | collective-permute-start | bytes 835592 | tf_op jit(solution)/shard_map/ppermute | solution.py:26
  37.4 1.9 %collective-permute-start.7 = (f32[2,17,16,128]{3,2,1,0:T(8,128)}, f32[2,17,16,128]{3,2,1,0:T(8,128)S(1)}, u32[]{:S(2)}, u32[]{:S(2)}) collective-permute-start(f32[2,17,16,128]{3,2,1,0:T(8,128)} %head.3), channel_id=1, source_target_pairs={{3,0},{4,1},{5,2},{6,3},{7,4},{11,8},{12,9},{13,10},{14,11},{15,12... | collective-permute-start | bytes 835592 | tf_op jit(solution)/shard_map/ppermute | solution.py:26
  40.2 40.1 %main.3 = (bf16[128,4096]{1,0:T(8,128)(2,1)}, bf16[128,8192]{1,0:T(8,128)(2,1)}, f32[3,8192]{1,0:T(4,128)}, f32[3,8192]{1,0:T(4,128)}, f32[8,24,1024]{2,1,0:T(8,128)}, /*index=5*/f32[32,128]{1,0:T(8,128)}) custom-call(s32[1]{0:T(128)} %bitcast.place_ref, s32[1,8]{1,0:T(1,128)} %len_ref.9, f32[32,128]{1,0:T(8,128)} %bitcast.49, bf16[128,8192]{1,0:T(8,128)(2,1)} %bitcast.23, ...), custom_call_target="tpu_custom_call" | custom-call | flops 41943040000 | bytes 150994944 | tf_op jit(solution)/shard_map/main/pallas_call | solution.py:406
  80.3 3.1 %collective-permute-start.4 = (bf16[128,4096]{1,0:T(8,128)(2,1)}, bf16[128,4096]{1,0:T(8,128)(2,1)S(1)}, u32[]{:S(2)}, u32[]{:S(2)}) collective-permute-start(bf16[128,4096]{1,0:T(8,128)(2,1)} %get-tuple-element.31), channel_id=1, source_target_pairs={{8,0},{16,8},{24,16},{9,1},{17,9},{25,17},{10,2},{18,10},{26,18},{... | collective-permute-start | bytes 3145736 | tf_op jit(solution)/shard_map/ppermute | solution.py:26
  84.3 22.9 %main.4 = (bf16[128,2048]{1,0:T(8,128)(2,1)}, bf16[128,8192]{1,0:T(8,128)(2,1)}, f32[3,8192]{1,0:T(4,128)}, f32[3,8192]{1,0:T(4,128)}, f32[8,24,1024]{2,1,0:T(8,128)}, /*index=5*/f32[32,128]{1,0:T(8,128)}) custom-call(s32[1]{0:T(128)} %bitcast.place_ref, ...), custom_call_target="tpu_custom_call", output_to_operand_aliasing={{1}: (15, {}), {2}: (16, {}), {3}: (17, {}), {4}: (18, {}),... | custom-call | flops 20971520000 | bytes 75497472 | tf_op jit(solution)/shard_map/main/pallas_call | solution.py:406
  107.2 2.2 %collective-permute-start.8 = (bf16[128,2048]{1,0:T(8,128)(2,1)}, bf16[128,2048]{1,0:T(8,128)(2,1)S(1)}, u32[]{:S(2)}, u32[]{:S(2)}) collective-permute-start(bf16[128,2048]{1,0:T(8,128)(2,1)} %get-tuple-element.37), channel_id=1, source_target_pairs={{8,0},{16,8},{24,16},{9,1},{17,9},{25,17},{10,2},{18,10},{26,18},{... | collective-permute-start | bytes 1572872 | tf_op jit(solution)/shard_map/ppermute | solution.py:26
  109.4 23.0 %main.5 = (bf16[128,2048]{1,0:T(8,128)(2,1)}, bf16[128,8192]{1,0:T(8,128)(2,1)}, f32[3,8192]{1,0:T(4,128)}, f32[3,8192]{1,0:T(4,128)}, f32[8,24,1024]{2,1,0:T(8,128)}, /*index=5*/f32[32,128]{1,0:T(8,128)}) custom-call(s32[1]{0:T(128)} %bitcast.place_ref, ...), custom_call_target="tpu_custom_call", output_to_operand_aliasing={{1}: (15, {}), {2}: (16, {}), {3}: (17, {}), {4}: (18, {}),... | custom-call | flops 20971520000 | bytes 75497472 | tf_op jit(solution)/shard_map/main/pallas_call | solution.py:406
  132.4 1.1 dynamic-slice_bitcast_fusion
  133.6 1.9 %collective-permute-start.9 = (bf16[128,2048]{1,0:T(8,128)(2,1)}, bf16[128,2048]{1,0:T(8,128)(2,1)S(1)}, u32[]{:S(2)}, u32[]{:S(2)}) collective-permute-start(bf16[128,2048]{1,0:T(8,128)(2,1)} %get-tuple-element.43), channel_id=1, source_target_pairs={{8,0},{16,8},{24,16},{9,1},{17,9},{25,17},{10,2},{18,10},{26,18},{... | collective-permute-start | bytes 1572872 | tf_op jit(solution)/shard_map/ppermute | solution.py:26
  135.5 1.8 %bitcast_add_fusion = f32[4,24,1024]{2,1,0:T(8,128)} fusion(f32[4,24,1024]{2,1,0:T(8,128)S(1)} %collective-permute-done.12, f32[4,2,24,1024]{3,2,1,0:T(8,128)} %bitcast.21, s32[]{:T(128)S(6)} %select_n.15), kind=kLoop, calls=%fused_computation | loop fusion | flops 98304 | bytes 1179652 | tf_op jit(solution)/shard_map/add | solution.py:519
  137.3 5.8 %all-to-all-start = ((f32[4,24,1024]{2,1,0:T(8,128)}), f32[4,24,1024]{2,1,0:T(8,128)S(1)}, u32[]{:S(2)}, u32[]{:S(2)}) async-start(f32[4,24,1024]{2,1,0:T(8,128)} %bitcast_add_fusion), calls=%async_computation | async-start | bytes 786432 | tf_op jit(solution)/shard_map/all_to_all | solution.py:521
  143.1 5.6 %collective-permute-done.9.refs_2_ = bf16[128,2048]{1,0:T(8,128)(2,1)S(1)} collective-permute-done((bf16[128,2048]{1,0:T(8,128)(2,1)}, bf16[128,2048]{1,0:T(8,128)(2,1)S(1)}, u32[]{:S(2)}, u32[]{:S(2)}) %collective-permute-start.9) | collective-permute-done | bytes 524320 | tf_op jit(solution)/shard_map/ppermute | solution.py:26
  148.7 2.8 %collective-permute-start.10 = (f32[3,8192]{1,0:T(4,128)S(1)}, f32[3,8192]{1,0:T(4,128)S(1)}, u32[]{:S(2)}, u32[]{:S(2)}) collective-permute-start(f32[3,8192]{1,0:T(4,128)S(1)} %copy-done.6), channel_id=1, source_target_pairs={{8,0},{16,8},{24,16},{9,1},{17,9},{25,17},{10,2},{18,10},{26,18},{... | collective-permute-start | bytes 294920 | tf_op jit(solution)/shard_map/ppermute | solution.py:26
  151.5 3.1 %collective-permute-start.11 = (f32[3,8192]{1,0:T(4,128)S(1)}, f32[3,8192]{1,0:T(4,128)S(1)}, u32[]{:S(2)}, u32[]{:S(2)}) collective-permute-start(f32[3,8192]{1,0:T(4,128)S(1)} %copy-done.7), channel_id=1, source_target_pairs={{9,0},{10,1},{11,2},{12,3},{13,4},{14,5},{15,6},{17,8},{18,9},{19,... | collective-permute-start | bytes 294920 | tf_op jit(solution)/shard_map/ppermute | solution.py:514
  154.7 5.0 %collective-permute-done.11.refs_4_ = f32[3,8192]{1,0:T(4,128)S(1)} collective-permute-done((f32[3,8192]{1,0:T(4,128)S(1)}, f32[3,8192]{1,0:T(4,128)S(1)}, u32[]{:S(2)}, u32[]{:S(2)}) %collective-permute-start.11) | collective-permute-done | bytes 98336 | tf_op jit(solution)/shard_map/ppermute | solution.py:514
  159.7 1.5 join.1
  (33 shorter events, 2.5 us)
Async XLA Ops:
  11.6 25.8 %collective-permute-start.1 = (f32[2,17,16,128]{3,2,1,0:T(8,128)}, f32[2,17,16,128]{3,2,1,0:T(8,128)S(1)}, u32[]{:S(2)}, u32[]{:S(2)}) collective-permute-start(f32[2,17,16,128]{3,2,1,0:T(8,128)} %head.2), channel_id=1, source_target_pairs={{1,0},{2,1},{3,2},{4,3},{5,4},{6,5},{7,6},{9,8},{10,9},{11,10},{12... | collective-permute-start | bytes 835592 | tf_op jit(solution)/shard_map/ppermute | solution.py:26
  14.2 25.2 %collective-permute-start.2 = (f32[2,17,16,128]{3,2,1,0:T(8,128)}, f32[2,17,16,128]{3,2,1,0:T(8,128)S(1)}, u32[]{:S(2)}, u32[]{:S(2)}) collective-permute-start(f32[2,17,16,128]{3,2,1,0:T(8,128)} %head.2), channel_id=1, source_target_pairs={{2,0},{3,1},{4,2},{5,3},{6,4},{7,5},{10,8},{11,9},{12,10},{13,11},... | collective-permute-start | bytes 835592 | tf_op jit(solution)/shard_map/ppermute | solution.py:26
  16.3 23.1 %collective-permute-start.3 = (f32[2,17,16,128]{3,2,1,0:T(8,128)}, f32[2,17,16,128]{3,2,1,0:T(8,128)S(1)}, u32[]{:S(2)}, u32[]{:S(2)}) collective-permute-start(f32[2,17,16,128]{3,2,1,0:T(8,128)} %head.2), channel_id=1, source_target_pairs={{3,0},{4,1},{5,2},{6,3},{7,4},{11,8},{12,9},{13,10},{14,11},{15,12... | collective-permute-start | bytes 835592 | tf_op jit(solution)/shard_map/ppermute | solution.py:26
  19.2 16.3 %collective-permute-start = (bf16[3,8192]{1,0:T(4,128)(2,1)S(1)}, bf16[3,8192]{1,0:T(4,128)(2,1)S(1)}, u32[]{:S(2)}, u32[]{:S(2)}) collective-permute-start(bf16[3,8192]{1,0:T(4,128)(2,1)S(1)} %slice_bitcast_fusion), channel_id=1, source_target_pairs={{0,1},{1,2},{2,3},{3,4},{4,5},{5,6},{6,7},{8,9},{9,10},{10,11},{11... | collective-permute-start | bytes 147464 | tf_op jit(solution)/shard_map/ppermute | solution.py:26
  33.5 49.8 %collective-permute-start.5 = (f32[2,17,16,128]{3,2,1,0:T(8,128)}, f32[2,17,16,128]{3,2,1,0:T(8,128)S(1)}, u32[]{:S(2)}, u32[]{:S(2)}) collective-permute-start(f32[2,17,16,128]{3,2,1,0:T(8,128)} %head.3), channel_id=1, source_target_pairs={{1,0},{2,1},{3,2},{4,3},{5,4},{6,5},{7,6},{9,8},{10,9},{11,10},{12... | collective-permute-start | bytes 835592 | tf_op jit(solution)/shard_map/ppermute | solution.py:26
  35.5 3.9 %copy-start.8 = (bf16[3,8192]{1,0:T(4,128)(2,1)}, bf16[3,8192]{1,0:T(4,128)(2,1)S(1)}, u32[]{:S(2)}) copy-start(bf16[3,8192]{1,0:T(4,128)(2,1)S(1)} %collective-permute-done.hist_ref) | copy-start | bytes 147460
  35.5 47.9 %collective-permute-start.6 = (f32[2,17,16,128]{3,2,1,0:T(8,128)}, f32[2,17,16,128]{3,2,1,0:T(8,128)S(1)}, u32[]{:S(2)}, u32[]{:S(2)}) collective-permute-start(f32[2,17,16,128]{3,2,1,0:T(8,128)} %head.3), channel_id=1, source_target_pairs={{2,0},{3,1},{4,2},{5,3},{6,4},{7,5},{10,8},{11,9},{12,10},{13,11},... | collective-permute-start | bytes 835592 | tf_op jit(solution)/shard_map/ppermute | solution.py:26
  37.4 2.0 %copy-start.1 = (f32[2,17,16,128]{3,2,1,0:T(8,128)}, f32[2,17,16,128]{3,2,1,0:T(8,128)S(1)}, u32[]{:S(2)}) copy-start(f32[2,17,16,128]{3,2,1,0:T(8,128)S(1)} %collective-permute-done.1.next_ref) | copy-start | bytes 835588
  37.4 46.0 %collective-permute-start.7 = (f32[2,17,16,128]{3,2,1,0:T(8,128)}, f32[2,17,16,128]{3,2,1,0:T(8,128)S(1)}, u32[]{:S(2)}, u32[]{:S(2)}) collective-permute-start(f32[2,17,16,128]{3,2,1,0:T(8,128)} %head.3), channel_id=1, source_target_pairs={{3,0},{4,1},{5,2},{6,3},{7,4},{11,8},{12,9},{13,10},{14,11},{15,12... | collective-permute-start | bytes 835592 | tf_op jit(solution)/shard_map/ppermute | solution.py:26
  39.4 0.7 copy-start.2
  39.4 0.8 copy-start.3
  80.3 52.1 %collective-permute-start.4 = (bf16[128,4096]{1,0:T(8,128)(2,1)}, bf16[128,4096]{1,0:T(8,128)(2,1)S(1)}, u32[]{:S(2)}, u32[]{:S(2)}) collective-permute-start(bf16[128,4096]{1,0:T(8,128)(2,1)} %get-tuple-element.31), channel_id=1, source_target_pairs={{8,0},{16,8},{24,16},{9,1},{17,9},{25,17},{10,2},{18,10},{26,18},{... | collective-permute-start | bytes 3145736 | tf_op jit(solution)/shard_map/ppermute | solution.py:26
  83.4 0.7 copy-start
  83.4 0.8 copy-start.4
  83.4 0.9 copy-start.5
  107.2 25.1 %collective-permute-start.8 = (bf16[128,2048]{1,0:T(8,128)(2,1)}, bf16[128,2048]{1,0:T(8,128)(2,1)S(1)}, u32[]{:S(2)}, u32[]{:S(2)}) collective-permute-start(bf16[128,2048]{1,0:T(8,128)(2,1)} %get-tuple-element.37), channel_id=1, source_target_pairs={{8,0},{16,8},{24,16},{9,1},{17,9},{25,17},{10,2},{18,10},{26,18},{... | collective-permute-start | bytes 1572872 | tf_op jit(solution)/shard_map/ppermute | solution.py:26
  132.3 16.3 %copy-start.6 = (f32[3,8192]{1,0:T(4,128)S(1)}, f32[3,8192]{1,0:T(4,128)}, u32[]{:S(2)}) copy-start(f32[3,8192]{1,0:T(4,128)} %get-tuple-element.49) | copy-start | bytes 294916
  132.4 19.2 %copy-start.7 = (f32[3,8192]{1,0:T(4,128)S(1)}, f32[3,8192]{1,0:T(4,128)}, u32[]{:S(2)}) copy-start(f32[3,8192]{1,0:T(4,128)} %get-tuple-element.50) | copy-start | bytes 294916
  133.5 2.0 %collective-permute-start.12 = (f32[4,24,1024]{2,1,0:T(8,128)S(1)}, f32[4,24,1024]{2,1,0:T(8,128)S(1)}, u32[]{:S(2)}, u32[]{:S(2)}) collective-permute-start(f32[4,24,1024]{2,1,0:T(8,128)S(1)} %dynamic-slice_bitcast_fusion), channel_id=1, source_target_pairs={{0,1},{1,0},{2,3},{3,2},{4,5},{5,4},{6,7},{7,6},{8,9},{9,8},{10,11... | collective-permute-start | bytes 1179656 | tf_op jit(solution)/shard_map/ppermute | solution.py:518
  133.6 15.1 %collective-permute-start.9 = (bf16[128,2048]{1,0:T(8,128)(2,1)}, bf16[128,2048]{1,0:T(8,128)(2,1)S(1)}, u32[]{:S(2)}, u32[]{:S(2)}) collective-permute-start(bf16[128,2048]{1,0:T(8,128)(2,1)} %get-tuple-element.43), channel_id=1, source_target_pairs={{8,0},{16,8},{24,16},{9,1},{17,9},{25,17},{10,2},{18,10},{26,18},{... | collective-permute-start | bytes 1572872 | tf_op jit(solution)/shard_map/ppermute | solution.py:26
  137.3 23.9 %all-to-all-start = ((f32[4,24,1024]{2,1,0:T(8,128)}), f32[4,24,1024]{2,1,0:T(8,128)S(1)}, u32[]{:S(2)}, u32[]{:S(2)}) async-start(f32[4,24,1024]{2,1,0:T(8,128)} %bitcast_add_fusion), calls=%async_computation | async-start | bytes 786432 | tf_op jit(solution)/shard_map/all_to_all | solution.py:521
  148.7 6.0 %collective-permute-start.10 = (f32[3,8192]{1,0:T(4,128)S(1)}, f32[3,8192]{1,0:T(4,128)S(1)}, u32[]{:S(2)}, u32[]{:S(2)}) collective-permute-start(f32[3,8192]{1,0:T(4,128)S(1)} %copy-done.6), channel_id=1, source_target_pairs={{8,0},{16,8},{24,16},{9,1},{17,9},{25,17},{10,2},{18,10},{26,18},{... | collective-permute-start | bytes 294920 | tf_op jit(solution)/shard_map/ppermute | solution.py:26
  151.5 8.2 %collective-permute-start.11 = (f32[3,8192]{1,0:T(4,128)S(1)}, f32[3,8192]{1,0:T(4,128)S(1)}, u32[]{:S(2)}, u32[]{:S(2)}) collective-permute-start(f32[3,8192]{1,0:T(4,128)S(1)} %copy-done.7), channel_id=1, source_target_pairs={{9,0},{10,1},{11,2},{12,3},{13,4},{14,5},{15,6},{17,8},{18,9},{19,... | collective-permute-start | bytes 294920 | tf_op jit(solution)/shard_map/ppermute | solution.py:514

commit v7 on v6

--- a/solution.py
+++ b/solution.py
@@ -507,7 +507,7 @@
     gdt, mine, spill, params, grad_maps = carried
     mine, spill, params, *_ = lax.optimization_barrier((mine, spill, params, *arrived[:-1]))
 
-    mine, spill, _ = lax.optimization_barrier((mine, spill, arrived[-1]))
+    spill = after(spill, arrived[-1])
     mine = shift_to(mine, "pipe", -1)
     pairs = [(s * shards + k, (s - 1) * shards + k - 1)
              for s in range(1, sections) for k in range(1, shards)]

time: 164 us -> 162 us (0.988)
  waiting for transfers between devices: 10.7 us -> 7 us
    ppermute x11, waiting for transfers between devices: 5.63 us -> 3.71 us  [shift_to(): return lax.ppermute(x, axis, pairs)]
    ppermute x1, starting transfers between devices: 3.13 us -> 4.94 us  [on_device(): spilled = lax.ppermute(spill, ('pipe', 'ctx'), pairs)]
    ppermute x1, waiting for transfers between devices: 5.02 us -> 3.28 us  [on_device(): spilled = lax.ppermute(spill, ('pipe', 'ctx'), pairs)]
  transfers between devices with their start and end apart: 14 -> 14, of which waited for: 2 -> 2; matrix products, arithmetic and copies ran while one was open for 2% -> 2% of each run, Pallas kernels for 61% -> 62%
where the time goes in v7:
time: 162 us; the launch traced here: 159 us
  Pallas kernels  109 us (67%)
  starting transfers between devices  35.5 us (22%)
  waiting for transfers between devices  7 us (4%)
  local copies, waits for them, and re-layouts  4.39 us (3%)
  other arithmetic  1.84 us (1%)
    pallas_call x3, Pallas kernels, main_call(): pl.pallas_call(functools.partial(main_kernel, group, part, blocks > 1), g...  86 us
    ppermute x11, starting transfers between devices, shift_to(): return lax.ppermute(x, axis, pairs)  24.7 us
    pallas_call x2, Pallas kernels, head_call(): pl.pallas_call(functools.partial(head_kernel, group, 8), grid=(blocks,),...  22 us
    all_to_all x1, starting transfers between devices, on_device(): lax.all_to_all(half, 'ctx', 0, 0, tiled=True, axis_index_groups=groups)  5.76 us
    ppermute x1, starting transfers between devices, on_device(): spilled = lax.ppermute(spill, ('pipe', 'ctx'), pairs)  4.94 us
    ppermute x11, waiting for transfers between devices, shift_to(): return lax.ppermute(x, axis, pairs)  3.71 us
    ppermute x1, waiting for transfers between devices, on_device(): spilled = lax.ppermute(spill, ('pipe', 'ctx'), pairs)  3.28 us
  transfers between devices with their start and end apart: 14, of which 2 were waited for; matrix products, arithmetic and copies ran while one was open for 2% of the time, Pallas kernels for 62%

profile of v7, /device:TPU:13, one launch (start us, length us, event | category | flops | bytes accessed | tf_op | source)
XLA Modules:
  0.0 159.2 jit_solution(14941051279090016024)
XLA Ops:
  0.6 11.0 %head.2 = f32[2,17,16,128]{3,2,1,0:T(8,128)} custom-call(s32[1]{0:T(128)} %bitcast.place_ref, s32[1,8]{1,0:T(1,128)} %len_ref.9, f32[32,128]{1,0:T(8,128)} %bitcast.47, bf16[128,8192]{1,0:T(8,128)(2,1)} %bitcast.26, bf16[128,8192]{1,0:T(8,128)(2,1)} %bitcast.31, f32[16,8192]{1,0:T(8,128)} %bitcast.39), custom_call_target="tpu_custom_call" | custom-call | flops 8388608000 | bytes 33554432 | tf_op jit(solution)/shard_map/head/pallas_call | solution.py:135
  11.6 2.6 %collective-permute-start.1 = (f32[2,17,16,128]{3,2,1,0:T(8,128)}, f32[2,17,16,128]{3,2,1,0:T(8,128)S(1)}, u32[]{:S(2)}, u32[]{:S(2)}) collective-permute-start(f32[2,17,16,128]{3,2,1,0:T(8,128)} %head.2), channel_id=1, source_target_pairs={{1,0},{2,1},{3,2},{4,3},{5,4},{6,5},{7,6},{9,8},{10,9},{11,10},{12... | collective-permute-start | bytes 835592 | tf_op jit(solution)/shard_map/ppermute | solution.py:26
  14.2 2.1 %collective-permute-start.2 = (f32[2,17,16,128]{3,2,1,0:T(8,128)}, f32[2,17,16,128]{3,2,1,0:T(8,128)S(1)}, u32[]{:S(2)}, u32[]{:S(2)}) collective-permute-start(f32[2,17,16,128]{3,2,1,0:T(8,128)} %head.2), channel_id=1, source_target_pairs={{2,0},{3,1},{4,2},{5,3},{6,4},{7,5},{10,8},{11,9},{12,10},{13,11},... | collective-permute-start | bytes 835592 | tf_op jit(solution)/shard_map/ppermute | solution.py:26
  16.3 1.9 %collective-permute-start.3 = (f32[2,17,16,128]{3,2,1,0:T(8,128)}, f32[2,17,16,128]{3,2,1,0:T(8,128)S(1)}, u32[]{:S(2)}, u32[]{:S(2)}) collective-permute-start(f32[2,17,16,128]{3,2,1,0:T(8,128)} %head.2), channel_id=1, source_target_pairs={{3,0},{4,1},{5,2},{6,3},{7,4},{11,8},{12,9},{13,10},{14,11},{15,12... | collective-permute-start | bytes 835592 | tf_op jit(solution)/shard_map/ppermute | solution.py:26
  18.2 0.9 slice_bitcast_fusion
  19.2 3.4 %collective-permute-start = (bf16[3,8192]{1,0:T(4,128)(2,1)S(1)}, bf16[3,8192]{1,0:T(4,128)(2,1)S(1)}, u32[]{:S(2)}, u32[]{:S(2)}) collective-permute-start(bf16[3,8192]{1,0:T(4,128)(2,1)S(1)} %slice_bitcast_fusion), channel_id=1, source_target_pairs={{0,1},{1,2},{2,3},{3,4},{4,5},{5,6},{6,7},{8,9},{9,10},{10,11},{11... | collective-permute-start | bytes 147464 | tf_op jit(solution)/shard_map/ppermute | solution.py:26
  22.5 11.0 %head.3 = f32[2,17,16,128]{3,2,1,0:T(8,128)} custom-call(s32[1]{0:T(128)} %bitcast.place_ref, s32[1,8]{1,0:T(1,128)} %len_ref.9, f32[32,128]{1,0:T(8,128)} %bitcast.48, bf16[128,8192]{1,0:T(8,128)(2,1)} %bitcast.27, bf16[128,8192]{1,0:T(8,128)(2,1)} %bitcast.32, f32[16,8192]{1,0:T(8,128)} %bitcast.40), custom_call_target="tpu_custom_call" | custom-call | flops 8388608000 | bytes 33554432 | tf_op jit(solution)/shard_map/head/pallas_call | solution.py:135
  33.5 1.9 %collective-permute-start.5 = (f32[2,17,16,128]{3,2,1,0:T(8,128)}, f32[2,17,16,128]{3,2,1,0:T(8,128)S(1)}, u32[]{:S(2)}, u32[]{:S(2)}) collective-permute-start(f32[2,17,16,128]{3,2,1,0:T(8,128)} %head.3), channel_id=1, source_target_pairs={{1,0},{2,1},{3,2},{4,3},{5,4},{6,5},{7,6},{9,8},{10,9},{11,10},{12... | collective-permute-start | bytes 835592 | tf_op jit(solution)/shard_map/ppermute | solution.py:26
  35.5 1.9 %collective-permute-start.6 = (f32[2,17,16,128]{3,2,1,0:T(8,128)}, f32[2,17,16,128]{3,2,1,0:T(8,128)S(1)}, u32[]{:S(2)}, u32[]{:S(2)}) collective-permute-start(f32[2,17,16,128]{3,2,1,0:T(8,128)} %head.3), channel_id=1, source_target_pairs={{2,0},{3,1},{4,2},{5,3},{6,4},{7,5},{10,8},{11,9},{12,10},{13,11},... | collective-permute-start | bytes 835592 | tf_op jit(solution)/shard_map/ppermute | solution.py:26
  37.4 1.9 %collective-permute-start.7 = (f32[2,17,16,128]{3,2,1,0:T(8,128)}, f32[2,17,16,128]{3,2,1,0:T(8,128)S(1)}, u32[]{:S(2)}, u32[]{:S(2)}) collective-permute-start(f32[2,17,16,128]{3,2,1,0:T(8,128)} %head.3), channel_id=1, source_target_pairs={{3,0},{4,1},{5,2},{6,3},{7,4},{11,8},{12,9},{13,10},{14,11},{15,12... | collective-permute-start | bytes 835592 | tf_op jit(solution)/shard_map/ppermute | solution.py:26
  40.2 40.1 %main.3 = (bf16[128,4096]{1,0:T(8,128)(2,1)}, bf16[128,8192]{1,0:T(8,128)(2,1)}, f32[3,8192]{1,0:T(4,128)}, f32[3,8192]{1,0:T(4,128)}, f32[8,24,1024]{2,1,0:T(8,128)}, /*index=5*/f32[32,128]{1,0:T(8,128)}) custom-call(s32[1]{0:T(128)} %bitcast.place_ref, s32[1,8]{1,0:T(1,128)} %len_ref.9, f32[32,128]{1,0:T(8,128)} %bitcast.49, bf16[128,8192]{1,0:T(8,128)(2,1)} %bitcast.23, ...), custom_call_target="tpu_custom_call" | custom-call | flops 41943040000 | bytes 150994944 | tf_op jit(solution)/shard_map/main/pallas_call | solution.py:406
  80.3 3.1 %collective-permute-start.4 = (bf16[128,4096]{1,0:T(8,128)(2,1)}, bf16[128,4096]{1,0:T(8,128)(2,1)S(1)}, u32[]{:S(2)}, u32[]{:S(2)}) collective-permute-start(bf16[128,4096]{1,0:T(8,128)(2,1)} %get-tuple-element.30), channel_id=1, source_target_pairs={{8,0},{16,8},{24,16},{9,1},{17,9},{25,17},{10,2},{18,10},{26,18},{... | collective-permute-start | bytes 3145736 | tf_op jit(solution)/shard_map/ppermute | solution.py:26
  84.3 22.9 %main.4 = (bf16[128,2048]{1,0:T(8,128)(2,1)}, bf16[128,8192]{1,0:T(8,128)(2,1)}, f32[3,8192]{1,0:T(4,128)}, f32[3,8192]{1,0:T(4,128)}, f32[8,24,1024]{2,1,0:T(8,128)}, /*index=5*/f32[32,128]{1,0:T(8,128)}) custom-call(s32[1]{0:T(128)} %bitcast.place_ref, ...), custom_call_target="tpu_custom_call", output_to_operand_aliasing={{1}: (15, {}), {2}: (16, {}), {3}: (17, {}), {4}: (18, {}),... | custom-call | flops 20971520000 | bytes 75497472 | tf_op jit(solution)/shard_map/main/pallas_call | solution.py:406
  107.2 2.2 %collective-permute-start.8 = (bf16[128,2048]{1,0:T(8,128)(2,1)}, bf16[128,2048]{1,0:T(8,128)(2,1)S(1)}, u32[]{:S(2)}, u32[]{:S(2)}) collective-permute-start(bf16[128,2048]{1,0:T(8,128)(2,1)} %get-tuple-element.36), channel_id=1, source_target_pairs={{8,0},{16,8},{24,16},{9,1},{17,9},{25,17},{10,2},{18,10},{26,18},{... | collective-permute-start | bytes 1572872 | tf_op jit(solution)/shard_map/ppermute | solution.py:26
  109.4 23.0 %main.5 = (bf16[128,2048]{1,0:T(8,128)(2,1)}, bf16[128,8192]{1,0:T(8,128)(2,1)}, f32[3,8192]{1,0:T(4,128)}, f32[3,8192]{1,0:T(4,128)}, f32[8,24,1024]{2,1,0:T(8,128)}, /*index=5*/f32[32,128]{1,0:T(8,128)}) custom-call(s32[1]{0:T(128)} %bitcast.place_ref, ...), custom_call_target="tpu_custom_call", output_to_operand_aliasing={{1}: (15, {}), {2}: (16, {}), {3}: (17, {}), {4}: (18, {}),... | custom-call | flops 20971520000 | bytes 75497472 | tf_op jit(solution)/shard_map/main/pallas_call | solution.py:406
  132.4 1.1 dynamic-slice_bitcast_fusion
  133.6 1.9 %collective-permute-start.9 = (bf16[128,2048]{1,0:T(8,128)(2,1)}, bf16[128,2048]{1,0:T(8,128)(2,1)S(1)}, u32[]{:S(2)}, u32[]{:S(2)}) collective-permute-start(bf16[128,2048]{1,0:T(8,128)(2,1)} %get-tuple-element.42), channel_id=1, source_target_pairs={{8,0},{16,8},{24,16},{9,1},{17,9},{25,17},{10,2},{18,10},{26,18},{... | collective-permute-start | bytes 1572872 | tf_op jit(solution)/shard_map/ppermute | solution.py:26
  135.5 1.8 %bitcast_add_fusion = f32[4,24,1024]{2,1,0:T(8,128)} fusion(f32[4,24,1024]{2,1,0:T(8,128)S(1)} %collective-permute-done.12, f32[4,2,24,1024]{3,2,1,0:T(8,128)} %bitcast.21, s32[]{:T(128)S(6)} %select_n.15), kind=kLoop, calls=%fused_computation | loop fusion | flops 98304 | bytes 1179652 | tf_op jit(solution)/shard_map/add | solution.py:519
  137.3 5.8 %all-to-all-start = ((f32[4,24,1024]{2,1,0:T(8,128)}), f32[4,24,1024]{2,1,0:T(8,128)S(1)}, u32[]{:S(2)}, u32[]{:S(2)}) async-start(f32[4,24,1024]{2,1,0:T(8,128)} %bitcast_add_fusion), calls=%async_computation | async-start | bytes 786432 | tf_op jit(solution)/shard_map/all_to_all | solution.py:521
  143.1 1.9 %collective-permute-start.10 = (f32[3,8192]{1,0:T(4,128)S(1)}, f32[3,8192]{1,0:T(4,128)S(1)}, u32[]{:S(2)}, u32[]{:S(2)}) collective-permute-start(f32[3,8192]{1,0:T(4,128)S(1)} %copy-done.6), channel_id=1, source_target_pairs={{8,0},{16,8},{24,16},{9,1},{17,9},{25,17},{10,2},{18,10},{26,18},{... | collective-permute-start | bytes 294920 | tf_op jit(solution)/shard_map/ppermute | solution.py:26
  145.0 3.7 %collective-permute-done.9.refs_2_ = bf16[128,2048]{1,0:T(8,128)(2,1)S(1)} collective-permute-done((bf16[128,2048]{1,0:T(8,128)(2,1)}, bf16[128,2048]{1,0:T(8,128)(2,1)S(1)}, u32[]{:S(2)}, u32[]{:S(2)}) %collective-permute-start.9) | collective-permute-done | bytes 524320 | tf_op jit(solution)/shard_map/ppermute | solution.py:26
  148.7 4.9 %collective-permute-start.11 = (f32[3,8192]{1,0:T(4,128)S(1)}, f32[3,8192]{1,0:T(4,128)S(1)}, u32[]{:S(2)}, u32[]{:S(2)}) collective-permute-start(f32[3,8192]{1,0:T(4,128)S(1)} %copy-done.7), channel_id=1, source_target_pairs={{9,0},{10,1},{11,2},{12,3},{13,4},{14,5},{15,6},{17,8},{18,9},{19,... | collective-permute-start | bytes 294920 | tf_op jit(solution)/shard_map/ppermute | solution.py:514
  153.7 3.3 %collective-permute-done.11.refs_4_ = f32[3,8192]{1,0:T(4,128)S(1)} collective-permute-done((f32[3,8192]{1,0:T(4,128)S(1)}, f32[3,8192]{1,0:T(4,128)S(1)}, u32[]{:S(2)}, u32[]{:S(2)}) %collective-permute-start.11) | collective-permute-done | bytes 98336 | tf_op jit(solution)/shard_map/ppermute | solution.py:514
  156.9 1.5 join.1
  (33 shorter events, 2.5 us)
Async XLA Ops:
  11.6 25.8 %collective-permute-start.1 = (f32[2,17,16,128]{3,2,1,0:T(8,128)}, f32[2,17,16,128]{3,2,1,0:T(8,128)S(1)}, u32[]{:S(2)}, u32[]{:S(2)}) collective-permute-start(f32[2,17,16,128]{3,2,1,0:T(8,128)} %head.2), channel_id=1, source_target_pairs={{1,0},{2,1},{3,2},{4,3},{5,4},{6,5},{7,6},{9,8},{10,9},{11,10},{12... | collective-permute-start | bytes 835592 | tf_op jit(solution)/shard_map/ppermute | solution.py:26
  14.2 25.2 %collective-permute-start.2 = (f32[2,17,16,128]{3,2,1,0:T(8,128)}, f32[2,17,16,128]{3,2,1,0:T(8,128)S(1)}, u32[]{:S(2)}, u32[]{:S(2)}) collective-permute-start(f32[2,17,16,128]{3,2,1,0:T(8,128)} %head.2), channel_id=1, source_target_pairs={{2,0},{3,1},{4,2},{5,3},{6,4},{7,5},{10,8},{11,9},{12,10},{13,11},... | collective-permute-start | bytes 835592 | tf_op jit(solution)/shard_map/ppermute | solution.py:26
  16.3 23.1 %collective-permute-start.3 = (f32[2,17,16,128]{3,2,1,0:T(8,128)}, f32[2,17,16,128]{3,2,1,0:T(8,128)S(1)}, u32[]{:S(2)}, u32[]{:S(2)}) collective-permute-start(f32[2,17,16,128]{3,2,1,0:T(8,128)} %head.2), channel_id=1, source_target_pairs={{3,0},{4,1},{5,2},{6,3},{7,4},{11,8},{12,9},{13,10},{14,11},{15,12... | collective-permute-start | bytes 835592 | tf_op jit(solution)/shard_map/ppermute | solution.py:26
  19.2 16.3 %collective-permute-start = (bf16[3,8192]{1,0:T(4,128)(2,1)S(1)}, bf16[3,8192]{1,0:T(4,128)(2,1)S(1)}, u32[]{:S(2)}, u32[]{:S(2)}) collective-permute-start(bf16[3,8192]{1,0:T(4,128)(2,1)S(1)} %slice_bitcast_fusion), channel_id=1, source_target_pairs={{0,1},{1,2},{2,3},{3,4},{4,5},{5,6},{6,7},{8,9},{9,10},{10,11},{11... | collective-permute-start | bytes 147464 | tf_op jit(solution)/shard_map/ppermute | solution.py:26
  33.5 49.8 %collective-permute-start.5 = (f32[2,17,16,128]{3,2,1,0:T(8,128)}, f32[2,17,16,128]{3,2,1,0:T(8,128)S(1)}, u32[]{:S(2)}, u32[]{:S(2)}) collective-permute-start(f32[2,17,16,128]{3,2,1,0:T(8,128)} %head.3), channel_id=1, source_target_pairs={{1,0},{2,1},{3,2},{4,3},{5,4},{6,5},{7,6},{9,8},{10,9},{11,10},{12... | collective-permute-start | bytes 835592 | tf_op jit(solution)/shard_map/ppermute | solution.py:26
  35.5 3.9 %copy-start.8 = (bf16[3,8192]{1,0:T(4,128)(2,1)}, bf16[3,8192]{1,0:T(4,128)(2,1)S(1)}, u32[]{:S(2)}) copy-start(bf16[3,8192]{1,0:T(4,128)(2,1)S(1)} %collective-permute-done.hist_ref) | copy-start | bytes 147460
  35.5 47.9 %collective-permute-start.6 = (f32[2,17,16,128]{3,2,1,0:T(8,128)}, f32[2,17,16,128]{3,2,1,0:T(8,128)S(1)}, u32[]{:S(2)}, u32[]{:S(2)}) collective-permute-start(f32[2,17,16,128]{3,2,1,0:T(8,128)} %head.3), channel_id=1, source_target_pairs={{2,0},{3,1},{4,2},{5,3},{6,4},{7,5},{10,8},{11,9},{12,10},{13,11},... | collective-permute-start | bytes 835592 | tf_op jit(solution)/shard_map/ppermute | solution.py:26
  37.4 2.0 %copy-start.1 = (f32[2,17,16,128]{3,2,1,0:T(8,128)}, f32[2,17,16,128]{3,2,1,0:T(8,128)S(1)}, u32[]{:S(2)}) copy-start(f32[2,17,16,128]{3,2,1,0:T(8,128)S(1)} %collective-permute-done.1.next_ref) | copy-start | bytes 835588
  37.4 46.0 %collective-permute-start.7 = (f32[2,17,16,128]{3,2,1,0:T(8,128)}, f32[2,17,16,128]{3,2,1,0:T(8,128)S(1)}, u32[]{:S(2)}, u32[]{:S(2)}) collective-permute-start(f32[2,17,16,128]{3,2,1,0:T(8,128)} %head.3), channel_id=1, source_target_pairs={{3,0},{4,1},{5,2},{6,3},{7,4},{11,8},{12,9},{13,10},{14,11},{15,12... | collective-permute-start | bytes 835592 | tf_op jit(solution)/shard_map/ppermute | solution.py:26
  39.4 0.7 copy-start.2
  39.4 0.8 copy-start.3
  80.3 52.1 %collective-permute-start.4 = (bf16[128,4096]{1,0:T(8,128)(2,1)}, bf16[128,4096]{1,0:T(8,128)(2,1)S(1)}, u32[]{:S(2)}, u32[]{:S(2)}) collective-permute-start(bf16[128,4096]{1,0:T(8,128)(2,1)} %get-tuple-element.30), channel_id=1, source_target_pairs={{8,0},{16,8},{24,16},{9,1},{17,9},{25,17},{10,2},{18,10},{26,18},{... | collective-permute-start | bytes 3145736 | tf_op jit(solution)/shard_map/ppermute | solution.py:26
  83.4 0.7 copy-start
  83.4 0.8 copy-start.4
  83.4 0.9 copy-start.5
  107.2 25.1 %collective-permute-start.8 = (bf16[128,2048]{1,0:T(8,128)(2,1)}, bf16[128,2048]{1,0:T(8,128)(2,1)S(1)}, u32[]{:S(2)}, u32[]{:S(2)}) collective-permute-start(bf16[128,2048]{1,0:T(8,128)(2,1)} %get-tuple-element.36), channel_id=1, source_target_pairs={{8,0},{16,8},{24,16},{9,1},{17,9},{25,17},{10,2},{18,10},{26,18},{... | collective-permute-start | bytes 1572872 | tf_op jit(solution)/shard_map/ppermute | solution.py:26
  132.3 10.7 %copy-start.6 = (f32[3,8192]{1,0:T(4,128)S(1)}, f32[3,8192]{1,0:T(4,128)}, u32[]{:S(2)}) copy-start(f32[3,8192]{1,0:T(4,128)} %get-tuple-element.46) | copy-start | bytes 294916
  132.4 16.3 %copy-start.7 = (f32[3,8192]{1,0:T(4,128)S(1)}, f32[3,8192]{1,0:T(4,128)}, u32[]{:S(2)}) copy-start(f32[3,8192]{1,0:T(4,128)} %get-tuple-element.48) | copy-start | bytes 294916
  133.5 2.0 %collective-permute-start.12 = (f32[4,24,1024]{2,1,0:T(8,128)S(1)}, f32[4,24,1024]{2,1,0:T(8,128)S(1)}, u32[]{:S(2)}, u32[]{:S(2)}) collective-permute-start(f32[4,24,1024]{2,1,0:T(8,128)S(1)} %dynamic-slice_bitcast_fusion), channel_id=1, source_target_pairs={{0,1},{1,0},{2,3},{3,2},{4,5},{5,4},{6,7},{7,6},{8,9},{9,8},{10,11... | collective-permute-start | bytes 1179656 | tf_op jit(solution)/shard_map/ppermute | solution.py:518
  133.6 15.1 %collective-permute-start.9 = (bf16[128,2048]{1,0:T(8,128)(2,1)}, bf16[128,2048]{1,0:T(8,128)(2,1)S(1)}, u32[]{:S(2)}, u32[]{:S(2)}) collective-permute-start(bf16[128,2048]{1,0:T(8,128)(2,1)} %get-tuple-element.42), channel_id=1, source_target_pairs={{8,0},{16,8},{24,16},{9,1},{17,9},{25,17},{10,2},{18,10},{26,18},{... | collective-permute-start | bytes 1572872 | tf_op jit(solution)/shard_map/ppermute | solution.py:26
  137.3 21.1 %all-to-all-start = ((f32[4,24,1024]{2,1,0:T(8,128)}), f32[4,24,1024]{2,1,0:T(8,128)S(1)}, u32[]{:S(2)}, u32[]{:S(2)}) async-start(f32[4,24,1024]{2,1,0:T(8,128)} %bitcast_add_fusion), calls=%async_computation | async-start | bytes 786432 | tf_op jit(solution)/shard_map/all_to_all | solution.py:521
  143.1 10.6 %collective-permute-start.10 = (f32[3,8192]{1,0:T(4,128)S(1)}, f32[3,8192]{1,0:T(4,128)S(1)}, u32[]{:S(2)}, u32[]{:S(2)}) collective-permute-start(f32[3,8192]{1,0:T(4,128)S(1)} %copy-done.6), channel_id=1, source_target_pairs={{8,0},{16,8},{24,16},{9,1},{17,9},{25,17},{10,2},{18,10},{26,18},{... | collective-permute-start | bytes 294920 | tf_op jit(solution)/shard_map/ppermute | solution.py:26
  148.7 8.2 %collective-permute-start.11 = (f32[3,8192]{1,0:T(4,128)S(1)}, f32[3,8192]{1,0:T(4,128)S(1)}, u32[]{:S(2)}, u32[]{:S(2)}) collective-permute-start(f32[3,8192]{1,0:T(4,128)S(1)} %copy-done.7), channel_id=1, source_target_pairs={{9,0},{10,1},{11,2},{12,3},{13,4},{14,5},{15,6},{17,8},{18,9},{19,... | collective-permute-start | bytes 294920 | tf_op jit(solution)/shard_map/ppermute | solution.py:514

commit v8 on v7

--- a/solution.py
+++ b/solution.py
@@ -16,6 +16,7 @@
 WIDE = 16
 MIB = 1 << 20
 HEAD_VMEM = 60 * MIB
+JOIN_COST = 1 << 32
 MAIN_VMEM = 60 * MIB
 REACH = 3
 
@@ -466,6 +467,8 @@
         functools.partial(join_kernel, count),
         out_shape=jax.ShapeDtypeStruct((rows, mine.shape[1]), blocks[0].dtype),
         compiler_params=pltpu.CompilerParams(vmem_limit_bytes=16 * MIB),
+        cost_estimate=pl.CostEstimate(
+            flops=JOIN_COST, transcendentals=0, bytes_accessed=JOIN_COST // 250),
         name="join",
     )(*blocks, mine, spilled)
 
@@ -507,7 +510,6 @@
     gdt, mine, spill, params, grad_maps = carried
     mine, spill, params, *_ = lax.optimization_barrier((mine, spill, params, *arrived[:-1]))
 
-    spill = after(spill, arrived[-1])
     mine = shift_to(mine, "pipe", -1)
     pairs = [(s * shards + k, (s - 1) * shards + k - 1)
              for s in range(1, sections) for k in range(1, shards)]

time: 162 us -> 159 us (0.981); the launches traced: 159 us -> 159 us
  starting transfers between devices: 35.5 us -> 33 us
  waiting for transfers between devices: 7 us -> 9.03 us
    ppermute x1, starting transfers between devices: 4.94 us -> 2.45 us  [on_device(): spilled = lax.ppermute(spill, ('pipe', 'ctx'), pairs)]
    ppermute x1, waiting for transfers between devices: 3.28 us -> 5 us  [on_device(): spilled = lax.ppermute(spill, ('pipe', 'ctx'), pairs)]
  transfers between devices with their start and end apart: 14 -> 14, of which waited for: 2 -> 3; matrix products, arithmetic and copies ran while one was open for 2% -> 2% of each run, Pallas kernels for 62% -> 62%
where the time goes in v8:
time: 159 us
  Pallas kernels  109 us (69%)
  starting transfers between devices  33 us (21%)
  waiting for transfers between devices  9.03 us (6%)
  local copies, waits for them, and re-layouts  4.39 us (3%)
  other arithmetic  1.84 us (1%)
    pallas_call x3, Pallas kernels, main_call(): pl.pallas_call(functools.partial(main_kernel, group, part, blocks > 1), g...  86 us
    ppermute x11, starting transfers between devices, shift_to(): return lax.ppermute(x, axis, pairs)  24.7 us
    pallas_call x2, Pallas kernels, head_call(): pl.pallas_call(functools.partial(head_kernel, group, 8), grid=(blocks,),...  22 us
    all_to_all x1, starting transfers between devices, on_device(): lax.all_to_all(half, 'ctx', 0, 0, tiled=True, axis_index_groups=groups)  5.77 us
    ppermute x1, waiting for transfers between devices, on_device(): spilled = lax.ppermute(spill, ('pipe', 'ctx'), pairs)  5 us
    ppermute x11, waiting for transfers between devices, shift_to(): return lax.ppermute(x, axis, pairs)  4.03 us
  transfers between devices with their start and end apart: 14, of which 3 were waited for; matrix products, arithmetic and copies ran while one was open for 2% of the time, Pallas kernels for 62%

profile of v8, /device:TPU:13, one launch (start us, length us, event | category | flops | bytes accessed | tf_op | source)
XLA Modules:
  0.0 158.7 jit_solution(373415338127316510)
XLA Ops:
  0.6 11.0 %head.2 = f32[2,17,16,128]{3,2,1,0:T(8,128)} custom-call(s32[1]{0:T(128)} %bitcast.place_ref, s32[1,8]{1,0:T(1,128)} %len_ref.9, f32[32,128]{1,0:T(8,128)} %bitcast.46, bf16[128,8192]{1,0:T(8,128)(2,1)} %bitcast.25, bf16[128,8192]{1,0:T(8,128)(2,1)} %bitcast.30, f32[16,8192]{1,0:T(8,128)} %bitcast.38), custom_call_target="tpu_custom_call" | custom-call | flops 8388608000 | bytes 33554432 | tf_op jit(solution)/shard_map/head/pallas_call | solution.py:136
  11.6 2.6 %collective-permute-start.1 = (f32[2,17,16,128]{3,2,1,0:T(8,128)}, f32[2,17,16,128]{3,2,1,0:T(8,128)S(1)}, u32[]{:S(2)}, u32[]{:S(2)}) collective-permute-start(f32[2,17,16,128]{3,2,1,0:T(8,128)} %head.2), channel_id=1, source_target_pairs={{1,0},{2,1},{3,2},{4,3},{5,4},{6,5},{7,6},{9,8},{10,9},{11,10},{12... | collective-permute-start | bytes 835592 | tf_op jit(solution)/shard_map/ppermute | solution.py:27
  14.2 2.1 %collective-permute-start.2 = (f32[2,17,16,128]{3,2,1,0:T(8,128)}, f32[2,17,16,128]{3,2,1,0:T(8,128)S(1)}, u32[]{:S(2)}, u32[]{:S(2)}) collective-permute-start(f32[2,17,16,128]{3,2,1,0:T(8,128)} %head.2), channel_id=1, source_target_pairs={{2,0},{3,1},{4,2},{5,3},{6,4},{7,5},{10,8},{11,9},{12,10},{13,11},... | collective-permute-start | bytes 835592 | tf_op jit(solution)/shard_map/ppermute | solution.py:27
  16.3 1.9 %collective-permute-start.3 = (f32[2,17,16,128]{3,2,1,0:T(8,128)}, f32[2,17,16,128]{3,2,1,0:T(8,128)S(1)}, u32[]{:S(2)}, u32[]{:S(2)}) collective-permute-start(f32[2,17,16,128]{3,2,1,0:T(8,128)} %head.2), channel_id=1, source_target_pairs={{3,0},{4,1},{5,2},{6,3},{7,4},{11,8},{12,9},{13,10},{14,11},{15,12... | collective-permute-start | bytes 835592 | tf_op jit(solution)/shard_map/ppermute | solution.py:27
  19.2 3.4 %collective-permute-start = (bf16[3,8192]{1,0:T(4,128)(2,1)S(1)}, bf16[3,8192]{1,0:T(4,128)(2,1)S(1)}, u32[]{:S(2)}, u32[]{:S(2)}) collective-permute-start(bf16[3,8192]{1,0:T(4,128)(2,1)S(1)} %slice_bitcast_fusion), channel_id=1, source_target_pairs={{0,1},{1,2},{2,3},{3,4},{4,5},{5,6},{6,7},{8,9},{9,10},{10,11},{11... | collective-permute-start | bytes 147464 | tf_op jit(solution)/shard_map/ppermute | solution.py:27
  22.5 11.0 %head.3 = f32[2,17,16,128]{3,2,1,0:T(8,128)} custom-call(s32[1]{0:T(128)} %bitcast.place_ref, s32[1,8]{1,0:T(1,128)} %len_ref.9, f32[32,128]{1,0:T(8,128)} %bitcast.47, bf16[128,8192]{1,0:T(8,128)(2,1)} %bitcast.26, bf16[128,8192]{1,0:T(8,128)(2,1)} %bitcast.31, f32[16,8192]{1,0:T(8,128)} %bitcast.39), custom_call_target="tpu_custom_call" | custom-call | flops 8388608000 | bytes 33554432 | tf_op jit(solution)/shard_map/head/pallas_call | solution.py:136
  33.5 1.9 %collective-permute-start.5 = (f32[2,17,16,128]{3,2,1,0:T(8,128)}, f32[2,17,16,128]{3,2,1,0:T(8,128)S(1)}, u32[]{:S(2)}, u32[]{:S(2)}) collective-permute-start(f32[2,17,16,128]{3,2,1,0:T(8,128)} %head.3), channel_id=1, source_target_pairs={{1,0},{2,1},{3,2},{4,3},{5,4},{6,5},{7,6},{9,8},{10,9},{11,10},{12... | collective-permute-start | bytes 835592 | tf_op jit(solution)/shard_map/ppermute | solution.py:27
  35.5 1.9 %collective-permute-start.6 = (f32[2,17,16,128]{3,2,1,0:T(8,128)}, f32[2,17,16,128]{3,2,1,0:T(8,128)S(1)}, u32[]{:S(2)}, u32[]{:S(2)}) collective-permute-start(f32[2,17,16,128]{3,2,1,0:T(8,128)} %head.3), channel_id=1, source_target_pairs={{2,0},{3,1},{4,2},{5,3},{6,4},{7,5},{10,8},{11,9},{12,10},{13,11},... | collective-permute-start | bytes 835592 | tf_op jit(solution)/shard_map/ppermute | solution.py:27
  37.4 1.9 %collective-permute-start.7 = (f32[2,17,16,128]{3,2,1,0:T(8,128)}, f32[2,17,16,128]{3,2,1,0:T(8,128)S(1)}, u32[]{:S(2)}, u32[]{:S(2)}) collective-permute-start(f32[2,17,16,128]{3,2,1,0:T(8,128)} %head.3), channel_id=1, source_target_pairs={{3,0},{4,1},{5,2},{6,3},{7,4},{11,8},{12,9},{13,10},{14,11},{15,12... | collective-permute-start | bytes 835592 | tf_op jit(solution)/shard_map/ppermute | solution.py:27
  40.2 40.1 %main.3 = (bf16[128,4096]{1,0:T(8,128)(2,1)}, bf16[128,8192]{1,0:T(8,128)(2,1)}, f32[3,8192]{1,0:T(4,128)}, f32[3,8192]{1,0:T(4,128)}, f32[8,24,1024]{2,1,0:T(8,128)}, /*index=5*/f32[32,128]{1,0:T(8,128)}) custom-call(s32[1]{0:T(128)} %bitcast.place_ref, s32[1,8]{1,0:T(1,128)} %len_ref.9, f32[32,128]{1,0:T(8,128)} %bitcast.48, bf16[128,8192]{1,0:T(8,128)(2,1)} %bitcast.22, ...), custom_call_target="tpu_custom_call" | custom-call | flops 41943040000 | bytes 150994944 | tf_op jit(solution)/shard_map/main/pallas_call | solution.py:407
  80.3 3.1 %collective-permute-start.4 = (bf16[128,4096]{1,0:T(8,128)(2,1)}, bf16[128,4096]{1,0:T(8,128)(2,1)S(1)}, u32[]{:S(2)}, u32[]{:S(2)}) collective-permute-start(bf16[128,4096]{1,0:T(8,128)(2,1)} %get-tuple-element.29), channel_id=1, source_target_pairs={{8,0},{16,8},{24,16},{9,1},{17,9},{25,17},{10,2},{18,10},{26,18},{... | collective-permute-start | bytes 3145736 | tf_op jit(solution)/shard_map/ppermute | solution.py:27
  84.3 22.9 %main.4 = (bf16[128,2048]{1,0:T(8,128)(2,1)}, bf16[128,8192]{1,0:T(8,128)(2,1)}, f32[3,8192]{1,0:T(4,128)}, f32[3,8192]{1,0:T(4,128)}, f32[8,24,1024]{2,1,0:T(8,128)}, /*index=5*/f32[32,128]{1,0:T(8,128)}) custom-call(s32[1]{0:T(128)} %bitcast.place_ref, ...), custom_call_target="tpu_custom_call", output_to_operand_aliasing={{1}: (15, {}), {2}: (16, {}), {3}: (17, {}), {4}: (18, {}),... | custom-call | flops 20971520000 | bytes 75497472 | tf_op jit(solution)/shard_map/main/pallas_call | solution.py:407
  107.2 2.2 %collective-permute-start.8 = (bf16[128,2048]{1,0:T(8,128)(2,1)}, bf16[128,2048]{1,0:T(8,128)(2,1)S(1)}, u32[]{:S(2)}, u32[]{:S(2)}) collective-permute-start(bf16[128,2048]{1,0:T(8,128)(2,1)} %get-tuple-element.35), channel_id=1, source_target_pairs={{8,0},{16,8},{24,16},{9,1},{17,9},{25,17},{10,2},{18,10},{26,18},{... | collective-permute-start | bytes 1572872 | tf_op jit(solution)/shard_map/ppermute | solution.py:27
  109.4 23.0 %main.5 = (bf16[128,2048]{1,0:T(8,128)(2,1)}, bf16[128,8192]{1,0:T(8,128)(2,1)}, f32[3,8192]{1,0:T(4,128)}, f32[3,8192]{1,0:T(4,128)}, f32[8,24,1024]{2,1,0:T(8,128)}, /*index=5*/f32[32,128]{1,0:T(8,128)}) custom-call(s32[1]{0:T(128)} %bitcast.place_ref, ...), custom_call_target="tpu_custom_call", output_to_operand_aliasing={{1}: (15, {}), {2}: (16, {}), {3}: (17, {}), {4}: (18, {}),... | custom-call | flops 20971520000 | bytes 75497472 | tf_op jit(solution)/shard_map/main/pallas_call | solution.py:407
  132.4 1.1 dynamic-slice_bitcast_fusion
  133.6 1.9 %collective-permute-start.9 = (bf16[128,2048]{1,0:T(8,128)(2,1)}, bf16[128,2048]{1,0:T(8,128)(2,1)S(1)}, u32[]{:S(2)}, u32[]{:S(2)}) collective-permute-start(bf16[128,2048]{1,0:T(8,128)(2,1)} %get-tuple-element.41), channel_id=1, source_target_pairs={{8,0},{16,8},{24,16},{9,1},{17,9},{25,17},{10,2},{18,10},{26,18},{... | collective-permute-start | bytes 1572872 | tf_op jit(solution)/shard_map/ppermute | solution.py:27
  135.5 1.8 %bitcast_add_fusion = f32[4,24,1024]{2,1,0:T(8,128)} fusion(f32[4,24,1024]{2,1,0:T(8,128)S(1)} %collective-permute-done.12, f32[4,2,24,1024]{3,2,1,0:T(8,128)} %bitcast.20, s32[]{:T(128)S(6)} %select_n.15), kind=kLoop, calls=%fused_computation | loop fusion | flops 98304 | bytes 1179652 | tf_op jit(solution)/shard_map/add | solution.py:521
  137.3 5.8 %all-to-all-start = ((f32[4,24,1024]{2,1,0:T(8,128)}), f32[4,24,1024]{2,1,0:T(8,128)S(1)}, u32[]{:S(2)}, u32[]{:S(2)}) async-start(f32[4,24,1024]{2,1,0:T(8,128)} %bitcast_add_fusion), calls=%async_computation | async-start | bytes 786432 | tf_op jit(solution)/shard_map/all_to_all | solution.py:523
  143.1 1.9 %collective-permute-start.10 = (f32[3,8192]{1,0:T(4,128)S(1)}, f32[3,8192]{1,0:T(4,128)S(1)}, u32[]{:S(2)}, u32[]{:S(2)}) collective-permute-start(f32[3,8192]{1,0:T(4,128)S(1)} %copy-done.6), channel_id=1, source_target_pairs={{8,0},{16,8},{24,16},{9,1},{17,9},{25,17},{10,2},{18,10},{26,18},{... | collective-permute-start | bytes 294920 | tf_op jit(solution)/shard_map/ppermute | solution.py:27
  145.0 2.4 %collective-permute-start.11 = (f32[3,8192]{1,0:T(4,128)S(1)}, f32[3,8192]{1,0:T(4,128)S(1)}, u32[]{:S(2)}, u32[]{:S(2)}) collective-permute-start(f32[3,8192]{1,0:T(4,128)S(1)} %copy-done.7), channel_id=1, source_target_pairs={{9,0},{10,1},{11,2},{12,3},{13,4},{14,5},{15,6},{17,8},{18,9},{19,... | collective-permute-start | bytes 294920 | tf_op jit(solution)/shard_map/ppermute | solution.py:516
  147.5 1.2 collective-permute-done.9.refs_2_
  148.7 2.8 %collective-permute-done.10.refs_3_ = f32[3,8192]{1,0:T(4,128)S(1)} collective-permute-done((f32[3,8192]{1,0:T(4,128)S(1)}, f32[3,8192]{1,0:T(4,128)S(1)}, u32[]{:S(2)}, u32[]{:S(2)}) %collective-permute-start.10) | collective-permute-done | bytes 98336 | tf_op jit(solution)/shard_map/ppermute | solution.py:27
  151.5 5.0 %collective-permute-done.11.refs_4_ = f32[3,8192]{1,0:T(4,128)S(1)} collective-permute-done((f32[3,8192]{1,0:T(4,128)S(1)}, f32[3,8192]{1,0:T(4,128)S(1)}, u32[]{:S(2)}, u32[]{:S(2)}) %collective-permute-start.11) | collective-permute-done | bytes 98336 | tf_op jit(solution)/shard_map/ppermute | solution.py:516
  156.5 1.5 join.1
  (33 shorter events, 3.4 us)
Async XLA Ops:
  11.6 25.8 %collective-permute-start.1 = (f32[2,17,16,128]{3,2,1,0:T(8,128)}, f32[2,17,16,128]{3,2,1,0:T(8,128)S(1)}, u32[]{:S(2)}, u32[]{:S(2)}) collective-permute-start(f32[2,17,16,128]{3,2,1,0:T(8,128)} %head.2), channel_id=1, source_target_pairs={{1,0},{2,1},{3,2},{4,3},{5,4},{6,5},{7,6},{9,8},{10,9},{11,10},{12... | collective-permute-start | bytes 835592 | tf_op jit(solution)/shard_map/ppermute | solution.py:27
  14.2 25.2 %collective-permute-start.2 = (f32[2,17,16,128]{3,2,1,0:T(8,128)}, f32[2,17,16,128]{3,2,1,0:T(8,128)S(1)}, u32[]{:S(2)}, u32[]{:S(2)}) collective-permute-start(f32[2,17,16,128]{3,2,1,0:T(8,128)} %head.2), channel_id=1, source_target_pairs={{2,0},{3,1},{4,2},{5,3},{6,4},{7,5},{10,8},{11,9},{12,10},{13,11},... | collective-permute-start | bytes 835592 | tf_op jit(solution)/shard_map/ppermute | solution.py:27
  16.3 23.1 %collective-permute-start.3 = (f32[2,17,16,128]{3,2,1,0:T(8,128)}, f32[2,17,16,128]{3,2,1,0:T(8,128)S(1)}, u32[]{:S(2)}, u32[]{:S(2)}) collective-permute-start(f32[2,17,16,128]{3,2,1,0:T(8,128)} %head.2), channel_id=1, source_target_pairs={{3,0},{4,1},{5,2},{6,3},{7,4},{11,8},{12,9},{13,10},{14,11},{15,12... | collective-permute-start | bytes 835592 | tf_op jit(solution)/shard_map/ppermute | solution.py:27
  19.2 16.3 %collective-permute-start = (bf16[3,8192]{1,0:T(4,128)(2,1)S(1)}, bf16[3,8192]{1,0:T(4,128)(2,1)S(1)}, u32[]{:S(2)}, u32[]{:S(2)}) collective-permute-start(bf16[3,8192]{1,0:T(4,128)(2,1)S(1)} %slice_bitcast_fusion), channel_id=1, source_target_pairs={{0,1},{1,2},{2,3},{3,4},{4,5},{5,6},{6,7},{8,9},{9,10},{10,11},{11... | collective-permute-start | bytes 147464 | tf_op jit(solution)/shard_map/ppermute | solution.py:27
  33.5 49.8 %collective-permute-start.5 = (f32[2,17,16,128]{3,2,1,0:T(8,128)}, f32[2,17,16,128]{3,2,1,0:T(8,128)S(1)}, u32[]{:S(2)}, u32[]{:S(2)}) collective-permute-start(f32[2,17,16,128]{3,2,1,0:T(8,128)} %head.3), channel_id=1, source_target_pairs={{1,0},{2,1},{3,2},{4,3},{5,4},{6,5},{7,6},{9,8},{10,9},{11,10},{12... | collective-permute-start | bytes 835592 | tf_op jit(solution)/shard_map/ppermute | solution.py:27
  35.5 3.9 %copy-start.8 = (bf16[3,8192]{1,0:T(4,128)(2,1)}, bf16[3,8192]{1,0:T(4,128)(2,1)S(1)}, u32[]{:S(2)}) copy-start(bf16[3,8192]{1,0:T(4,128)(2,1)S(1)} %collective-permute-done.hist_ref) | copy-start | bytes 147460
  35.5 47.9 %collective-permute-start.6 = (f32[2,17,16,128]{3,2,1,0:T(8,128)}, f32[2,17,16,128]{3,2,1,0:T(8,128)S(1)}, u32[]{:S(2)}, u32[]{:S(2)}) collective-permute-start(f32[2,17,16,128]{3,2,1,0:T(8,128)} %head.3), channel_id=1, source_target_pairs={{2,0},{3,1},{4,2},{5,3},{6,4},{7,5},{10,8},{11,9},{12,10},{13,11},... | collective-permute-start | bytes 835592 | tf_op jit(solution)/shard_map/ppermute | solution.py:27
  37.4 2.0 %copy-start.1 = (f32[2,17,16,128]{3,2,1,0:T(8,128)}, f32[2,17,16,128]{3,2,1,0:T(8,128)S(1)}, u32[]{:S(2)}) copy-start(f32[2,17,16,128]{3,2,1,0:T(8,128)S(1)} %collective-permute-done.1.next_ref) | copy-start | bytes 835588
  37.4 46.0 %collective-permute-start.7 = (f32[2,17,16,128]{3,2,1,0:T(8,128)}, f32[2,17,16,128]{3,2,1,0:T(8,128)S(1)}, u32[]{:S(2)}, u32[]{:S(2)}) collective-permute-start(f32[2,17,16,128]{3,2,1,0:T(8,128)} %head.3), channel_id=1, source_target_pairs={{3,0},{4,1},{5,2},{6,3},{7,4},{11,8},{12,9},{13,10},{14,11},{15,12... | collective-permute-start | bytes 835592 | tf_op jit(solution)/shard_map/ppermute | solution.py:27
  39.4 0.7 copy-start.2
  39.4 0.8 copy-start.3
  80.3 52.1 %collective-permute-start.4 = (bf16[128,4096]{1,0:T(8,128)(2,1)}, bf16[128,4096]{1,0:T(8,128)(2,1)S(1)}, u32[]{:S(2)}, u32[]{:S(2)}) collective-permute-start(bf16[128,4096]{1,0:T(8,128)(2,1)} %get-tuple-element.29), channel_id=1, source_target_pairs={{8,0},{16,8},{24,16},{9,1},{17,9},{25,17},{10,2},{18,10},{26,18},{... | collective-permute-start | bytes 3145736 | tf_op jit(solution)/shard_map/ppermute | solution.py:27
  83.4 0.7 copy-start
  83.4 0.8 copy-start.4
  83.4 0.9 copy-start.5
  107.2 25.1 %collective-permute-start.8 = (bf16[128,2048]{1,0:T(8,128)(2,1)}, bf16[128,2048]{1,0:T(8,128)(2,1)S(1)}, u32[]{:S(2)}, u32[]{:S(2)}) collective-permute-start(bf16[128,2048]{1,0:T(8,128)(2,1)} %get-tuple-element.35), channel_id=1, source_target_pairs={{8,0},{16,8},{24,16},{9,1},{17,9},{25,17},{10,2},{18,10},{26,18},{... | collective-permute-start | bytes 1572872 | tf_op jit(solution)/shard_map/ppermute | solution.py:27
  132.3 10.7 %copy-start.6 = (f32[3,8192]{1,0:T(4,128)S(1)}, f32[3,8192]{1,0:T(4,128)}, u32[]{:S(2)}) copy-start(f32[3,8192]{1,0:T(4,128)} %get-tuple-element.45) | copy-start | bytes 294916
  132.4 12.7 %copy-start.7 = (f32[3,8192]{1,0:T(4,128)S(1)}, f32[3,8192]{1,0:T(4,128)}, u32[]{:S(2)}) copy-start(f32[3,8192]{1,0:T(4,128)} %get-tuple-element.46) | copy-start | bytes 294916
  133.5 2.0 %collective-permute-start.12 = (f32[4,24,1024]{2,1,0:T(8,128)S(1)}, f32[4,24,1024]{2,1,0:T(8,128)S(1)}, u32[]{:S(2)}, u32[]{:S(2)}) collective-permute-start(f32[4,24,1024]{2,1,0:T(8,128)S(1)} %dynamic-slice_bitcast_fusion), channel_id=1, source_target_pairs={{0,1},{1,0},{2,3},{3,2},{4,5},{5,4},{6,7},{7,6},{8,9},{9,8},{10,11... | collective-permute-start | bytes 1179656 | tf_op jit(solution)/shard_map/ppermute | solution.py:520
  133.6 15.1 %collective-permute-start.9 = (bf16[128,2048]{1,0:T(8,128)(2,1)}, bf16[128,2048]{1,0:T(8,128)(2,1)S(1)}, u32[]{:S(2)}, u32[]{:S(2)}) collective-permute-start(bf16[128,2048]{1,0:T(8,128)(2,1)} %get-tuple-element.41), channel_id=1, source_target_pairs={{8,0},{16,8},{24,16},{9,1},{17,9},{25,17},{10,2},{18,10},{26,18},{... | collective-permute-start | bytes 1572872 | tf_op jit(solution)/shard_map/ppermute | solution.py:27
  137.3 20.7 %all-to-all-start = ((f32[4,24,1024]{2,1,0:T(8,128)}), f32[4,24,1024]{2,1,0:T(8,128)S(1)}, u32[]{:S(2)}, u32[]{:S(2)}) async-start(f32[4,24,1024]{2,1,0:T(8,128)} %bitcast_add_fusion), calls=%async_computation | async-start | bytes 786432 | tf_op jit(solution)/shard_map/all_to_all | solution.py:523
  143.1 8.4 %collective-permute-start.10 = (f32[3,8192]{1,0:T(4,128)S(1)}, f32[3,8192]{1,0:T(4,128)S(1)}, u32[]{:S(2)}, u32[]{:S(2)}) collective-permute-start(f32[3,8192]{1,0:T(4,128)S(1)} %copy-done.6), channel_id=1, source_target_pairs={{8,0},{16,8},{24,16},{9,1},{17,9},{25,17},{10,2},{18,10},{26,18},{... | collective-permute-start | bytes 294920 | tf_op jit(solution)/shard_map/ppermute | solution.py:27
  145.0 11.5 %collective-permute-start.11 = (f32[3,8192]{1,0:T(4,128)S(1)}, f32[3,8192]{1,0:T(4,128)S(1)}, u32[]{:S(2)}, u32[]{:S(2)}) collective-permute-start(f32[3,8192]{1,0:T(4,128)S(1)} %copy-done.7), channel_id=1, source_target_pairs={{9,0},{10,1},{11,2},{12,3},{13,4},{14,5},{15,6},{17,8},{18,9},{19,... | collective-permute-start | bytes 294920 | tf_op jit(solution)/shard_map/ppermute | solution.py:516

commit v9 on v8

--- a/solution.py
+++ b/solution.py
@@ -12,7 +12,7 @@
 LN2 = 0.6931471805599453
 RESET_STEP = 1e4
 PAST = 8
-CHUNK = 8
+CHUNK = 16
 WIDE = 16
 MIB = 1 << 20
 HEAD_VMEM = 60 * MIB
@@ -249,7 +249,7 @@
                 return tuple(out)
 
             final = lax.fori_loop(
-                0, rows, forward, tuple(start_s[n] for n in range(lo, hi)), unroll=16)
+                0, rows, forward, tuple(start_s[n] for n in range(lo, hi)), unroll=32)
             for n in range(lo, hi):
                 put(accc_s, n, rows, fold(final[n - lo] * gy_t[rows]))
 
@@ -356,7 +356,7 @@
                 maps_t[pl.ds((base + n) * rows + tb * 8, 8), :] = parts[0]
             return 0
 
-        lax.fori_loop(0, states, add_state, 0)
+        lax.fori_loop(0, states, add_state, 0, unroll=2)
 
     def add_lanes(n, _):
         flat = maps_t[pl.ds(at_chunk(n, rows), rows), :].T
@@ -370,7 +370,7 @@
     def _():
         add_sublanes(accb_s, 0, 0)
         add_sublanes(accc_s, 1, states)
-        lax.fori_loop(0, 2 * states, add_lanes, 0, unroll=4)
+        lax.fori_loop(0, 2 * states, add_lanes, 0, unroll=8)
 
 
 def main_call(group, part, shards, block, blocks, skip, place, lengths, maps, x, hist, dt, gy, start,

time: 159 us -> 156 us (0.981)
  Pallas kernels: 109 us -> 106 us
    pallas_call x3, Pallas kernels: 86 us -> 83.2 us  [main_call(): pl.pallas_call(functools.partial(main_kernel, group, part, blocks > 1), g...]
  transfers between devices with their start and end apart: 14 -> 14, of which waited for: 3 -> 3; matrix products, arithmetic and copies ran while one was open for 2% -> 2% of each run, Pallas kernels for 62% -> 61%
where the time goes in v9:
time: 156 us
  Pallas kernels  106 us (68%)
  starting transfers between devices  33.2 us (21%)
  waiting for transfers between devices  9.03 us (6%)
  local copies, waits for them, and re-layouts  4.39 us (3%)
  other arithmetic  1.84 us (1%)
    pallas_call x3, Pallas kernels, main_call(): pl.pallas_call(functools.partial(main_kernel, group, part, blocks > 1), g...  83.2 us
    ppermute x11, starting transfers between devices, shift_to(): return lax.ppermute(x, axis, pairs)  24.9 us
    pallas_call x2, Pallas kernels, head_call(): pl.pallas_call(functools.partial(head_kernel, group, 8), grid=(blocks,),...  21.4 us
    all_to_all x1, starting transfers between devices, on_device(): lax.all_to_all(half, 'ctx', 0, 0, tiled=True, axis_index_groups=groups)  5.77 us
    ppermute x1, waiting for transfers between devices, on_device(): spilled = lax.ppermute(spill, ('pipe', 'ctx'), pairs)  5 us
    ppermute x11, waiting for transfers between devices, shift_to(): return lax.ppermute(x, axis, pairs)  4.03 us
  transfers between devices with their start and end apart: 14, of which 3 were waited for; matrix products, arithmetic and copies ran while one was open for 2% of the time, Pallas kernels for 61%

profile of v9, /device:TPU:13, one launch (start us, length us, event | category | flops | bytes accessed | tf_op | source)
XLA Modules:
  0.0 155.5 jit_solution(5853417240773723055)
XLA Ops:
  0.6 10.7 %head.2 = f32[2,17,16,128]{3,2,1,0:T(8,128)} custom-call(s32[1]{0:T(128)} %bitcast.place_ref, s32[1,8]{1,0:T(1,128)} %len_ref.9, f32[32,128]{1,0:T(8,128)} %bitcast.46, bf16[128,8192]{1,0:T(8,128)(2,1)} %bitcast.25, bf16[128,8192]{1,0:T(8,128)(2,1)} %bitcast.30, f32[16,8192]{1,0:T(8,128)} %bitcast.38), custom_call_target="tpu_custom_call" | custom-call | flops 8388608000 | bytes 33554432 | tf_op jit(solution)/shard_map/head/pallas_call | solution.py:136
  11.3 2.6 %collective-permute-start.1 = (f32[2,17,16,128]{3,2,1,0:T(8,128)}, f32[2,17,16,128]{3,2,1,0:T(8,128)S(1)}, u32[]{:S(2)}, u32[]{:S(2)}) collective-permute-start(f32[2,17,16,128]{3,2,1,0:T(8,128)} %head.2), channel_id=1, source_target_pairs={{1,0},{2,1},{3,2},{4,3},{5,4},{6,5},{7,6},{9,8},{10,9},{11,10},{12... | collective-permute-start | bytes 835592 | tf_op jit(solution)/shard_map/ppermute | solution.py:27
  13.9 2.1 %collective-permute-start.2 = (f32[2,17,16,128]{3,2,1,0:T(8,128)}, f32[2,17,16,128]{3,2,1,0:T(8,128)S(1)}, u32[]{:S(2)}, u32[]{:S(2)}) collective-permute-start(f32[2,17,16,128]{3,2,1,0:T(8,128)} %head.2), channel_id=1, source_target_pairs={{2,0},{3,1},{4,2},{5,3},{6,4},{7,5},{10,8},{11,9},{12,10},{13,11},... | collective-permute-start | bytes 835592 | tf_op jit(solution)/shard_map/ppermute | solution.py:27
  16.0 1.9 %collective-permute-start.3 = (f32[2,17,16,128]{3,2,1,0:T(8,128)}, f32[2,17,16,128]{3,2,1,0:T(8,128)S(1)}, u32[]{:S(2)}, u32[]{:S(2)}) collective-permute-start(f32[2,17,16,128]{3,2,1,0:T(8,128)} %head.2), channel_id=1, source_target_pairs={{3,0},{4,1},{5,2},{6,3},{7,4},{11,8},{12,9},{13,10},{14,11},{15,12... | collective-permute-start | bytes 835592 | tf_op jit(solution)/shard_map/ppermute | solution.py:27
  18.9 3.4 %collective-permute-start = (bf16[3,8192]{1,0:T(4,128)(2,1)S(1)}, bf16[3,8192]{1,0:T(4,128)(2,1)S(1)}, u32[]{:S(2)}, u32[]{:S(2)}) collective-permute-start(bf16[3,8192]{1,0:T(4,128)(2,1)S(1)} %slice_bitcast_fusion), channel_id=1, source_target_pairs={{0,1},{1,2},{2,3},{3,4},{4,5},{5,6},{6,7},{8,9},{9,10},{10,11},{11... | collective-permute-start | bytes 147464 | tf_op jit(solution)/shard_map/ppermute | solution.py:27
  22.3 10.7 %head.3 = f32[2,17,16,128]{3,2,1,0:T(8,128)} custom-call(s32[1]{0:T(128)} %bitcast.place_ref, s32[1,8]{1,0:T(1,128)} %len_ref.9, f32[32,128]{1,0:T(8,128)} %bitcast.47, bf16[128,8192]{1,0:T(8,128)(2,1)} %bitcast.26, bf16[128,8192]{1,0:T(8,128)(2,1)} %bitcast.31, f32[16,8192]{1,0:T(8,128)} %bitcast.39), custom_call_target="tpu_custom_call" | custom-call | flops 8388608000 | bytes 33554432 | tf_op jit(solution)/shard_map/head/pallas_call | solution.py:136
  33.0 1.9 %collective-permute-start.5 = (f32[2,17,16,128]{3,2,1,0:T(8,128)}, f32[2,17,16,128]{3,2,1,0:T(8,128)S(1)}, u32[]{:S(2)}, u32[]{:S(2)}) collective-permute-start(f32[2,17,16,128]{3,2,1,0:T(8,128)} %head.3), channel_id=1, source_target_pairs={{1,0},{2,1},{3,2},{4,3},{5,4},{6,5},{7,6},{9,8},{10,9},{11,10},{12... | collective-permute-start | bytes 835592 | tf_op jit(solution)/shard_map/ppermute | solution.py:27
  34.9 1.9 %collective-permute-start.6 = (f32[2,17,16,128]{3,2,1,0:T(8,128)}, f32[2,17,16,128]{3,2,1,0:T(8,128)S(1)}, u32[]{:S(2)}, u32[]{:S(2)}) collective-permute-start(f32[2,17,16,128]{3,2,1,0:T(8,128)} %head.3), channel_id=1, source_target_pairs={{2,0},{3,1},{4,2},{5,3},{6,4},{7,5},{10,8},{11,9},{12,10},{13,11},... | collective-permute-start | bytes 835592 | tf_op jit(solution)/shard_map/ppermute | solution.py:27
  36.9 1.9 %collective-permute-start.7 = (f32[2,17,16,128]{3,2,1,0:T(8,128)}, f32[2,17,16,128]{3,2,1,0:T(8,128)S(1)}, u32[]{:S(2)}, u32[]{:S(2)}) collective-permute-start(f32[2,17,16,128]{3,2,1,0:T(8,128)} %head.3), channel_id=1, source_target_pairs={{3,0},{4,1},{5,2},{6,3},{7,4},{11,8},{12,9},{13,10},{14,11},{15,12... | collective-permute-start | bytes 835592 | tf_op jit(solution)/shard_map/ppermute | solution.py:27
  39.6 39.0 %main.3 = (bf16[128,4096]{1,0:T(8,128)(2,1)}, bf16[128,8192]{1,0:T(8,128)(2,1)}, f32[3,8192]{1,0:T(4,128)}, f32[3,8192]{1,0:T(4,128)}, f32[8,24,1024]{2,1,0:T(8,128)}, /*index=5*/f32[32,128]{1,0:T(8,128)}) custom-call(s32[1]{0:T(128)} %bitcast.place_ref, s32[1,8]{1,0:T(1,128)} %len_ref.9, f32[32,128]{1,0:T(8,128)} %bitcast.48, bf16[128,8192]{1,0:T(8,128)(2,1)} %bitcast.22, ...), custom_call_target="tpu_custom_call" | custom-call | flops 41943040000 | bytes 150994944 | tf_op jit(solution)/shard_map/main/pallas_call | solution.py:407
  78.6 3.1 %collective-permute-start.4 = (bf16[128,4096]{1,0:T(8,128)(2,1)}, bf16[128,4096]{1,0:T(8,128)(2,1)S(1)}, u32[]{:S(2)}, u32[]{:S(2)}) collective-permute-start(bf16[128,4096]{1,0:T(8,128)(2,1)} %get-tuple-element.29), channel_id=1, source_target_pairs={{8,0},{16,8},{24,16},{9,1},{17,9},{25,17},{10,2},{18,10},{26,18},{... | collective-permute-start | bytes 3145736 | tf_op jit(solution)/shard_map/ppermute | solution.py:27
  82.6 22.1 %main.4 = (bf16[128,2048]{1,0:T(8,128)(2,1)}, bf16[128,8192]{1,0:T(8,128)(2,1)}, f32[3,8192]{1,0:T(4,128)}, f32[3,8192]{1,0:T(4,128)}, f32[8,24,1024]{2,1,0:T(8,128)}, /*index=5*/f32[32,128]{1,0:T(8,128)}) custom-call(s32[1]{0:T(128)} %bitcast.place_ref, ...), custom_call_target="tpu_custom_call", output_to_operand_aliasing={{1}: (15, {}), {2}: (16, {}), {3}: (17, {}), {4}: (18, {}),... | custom-call | flops 20971520000 | bytes 75497472 | tf_op jit(solution)/shard_map/main/pallas_call | solution.py:407
  104.7 2.3 %collective-permute-start.8 = (bf16[128,2048]{1,0:T(8,128)(2,1)}, bf16[128,2048]{1,0:T(8,128)(2,1)S(1)}, u32[]{:S(2)}, u32[]{:S(2)}) collective-permute-start(bf16[128,2048]{1,0:T(8,128)(2,1)} %get-tuple-element.35), channel_id=1, source_target_pairs={{8,0},{16,8},{24,16},{9,1},{17,9},{25,17},{10,2},{18,10},{26,18},{... | collective-permute-start | bytes 1572872 | tf_op jit(solution)/shard_map/ppermute | solution.py:27
  107.0 22.1 %main.5 = (bf16[128,2048]{1,0:T(8,128)(2,1)}, bf16[128,8192]{1,0:T(8,128)(2,1)}, f32[3,8192]{1,0:T(4,128)}, f32[3,8192]{1,0:T(4,128)}, f32[8,24,1024]{2,1,0:T(8,128)}, /*index=5*/f32[32,128]{1,0:T(8,128)}) custom-call(s32[1]{0:T(128)} %bitcast.place_ref, ...), custom_call_target="tpu_custom_call", output_to_operand_aliasing={{1}: (15, {}), {2}: (16, {}), {3}: (17, {}), {4}: (18, {}),... | custom-call | flops 20971520000 | bytes 75497472 | tf_op jit(solution)/shard_map/main/pallas_call | solution.py:407
  129.2 1.1 dynamic-slice_bitcast_fusion
  130.4 1.9 %collective-permute-start.9 = (bf16[128,2048]{1,0:T(8,128)(2,1)}, bf16[128,2048]{1,0:T(8,128)(2,1)S(1)}, u32[]{:S(2)}, u32[]{:S(2)}) collective-permute-start(bf16[128,2048]{1,0:T(8,128)(2,1)} %get-tuple-element.41), channel_id=1, source_target_pairs={{8,0},{16,8},{24,16},{9,1},{17,9},{25,17},{10,2},{18,10},{26,18},{... | collective-permute-start | bytes 1572872 | tf_op jit(solution)/shard_map/ppermute | solution.py:27
  132.3 1.8 %bitcast_add_fusion = f32[4,24,1024]{2,1,0:T(8,128)} fusion(f32[4,24,1024]{2,1,0:T(8,128)S(1)} %collective-permute-done.12, f32[4,2,24,1024]{3,2,1,0:T(8,128)} %bitcast.20, s32[]{:T(128)S(6)} %select_n.15), kind=kLoop, calls=%fused_computation | loop fusion | flops 98304 | bytes 1179652 | tf_op jit(solution)/shard_map/add | solution.py:521
  134.1 5.8 %all-to-all-start = ((f32[4,24,1024]{2,1,0:T(8,128)}), f32[4,24,1024]{2,1,0:T(8,128)S(1)}, u32[]{:S(2)}, u32[]{:S(2)}) async-start(f32[4,24,1024]{2,1,0:T(8,128)} %bitcast_add_fusion), calls=%async_computation | async-start | bytes 786432 | tf_op jit(solution)/shard_map/all_to_all | solution.py:523
  139.9 1.9 %collective-permute-start.10 = (f32[3,8192]{1,0:T(4,128)S(1)}, f32[3,8192]{1,0:T(4,128)S(1)}, u32[]{:S(2)}, u32[]{:S(2)}) collective-permute-start(f32[3,8192]{1,0:T(4,128)S(1)} %copy-done.6), channel_id=1, source_target_pairs={{8,0},{16,8},{24,16},{9,1},{17,9},{25,17},{10,2},{18,10},{26,18},{... | collective-permute-start | bytes 294920 | tf_op jit(solution)/shard_map/ppermute | solution.py:27
  141.8 2.4 %collective-permute-start.11 = (f32[3,8192]{1,0:T(4,128)S(1)}, f32[3,8192]{1,0:T(4,128)S(1)}, u32[]{:S(2)}, u32[]{:S(2)}) collective-permute-start(f32[3,8192]{1,0:T(4,128)S(1)} %copy-done.7), channel_id=1, source_target_pairs={{9,0},{10,1},{11,2},{12,3},{13,4},{14,5},{15,6},{17,8},{18,9},{19,... | collective-permute-start | bytes 294920 | tf_op jit(solution)/shard_map/ppermute | solution.py:516
  144.3 1.2 collective-permute-done.9.refs_2_
  145.5 2.8 %collective-permute-done.10.refs_3_ = f32[3,8192]{1,0:T(4,128)S(1)} collective-permute-done((f32[3,8192]{1,0:T(4,128)S(1)}, f32[3,8192]{1,0:T(4,128)S(1)}, u32[]{:S(2)}, u32[]{:S(2)}) %collective-permute-start.10) | collective-permute-done | bytes 98336 | tf_op jit(solution)/shard_map/ppermute | solution.py:27
  148.3 5.0 %collective-permute-done.11.refs_4_ = f32[3,8192]{1,0:T(4,128)S(1)} collective-permute-done((f32[3,8192]{1,0:T(4,128)S(1)}, f32[3,8192]{1,0:T(4,128)S(1)}, u32[]{:S(2)}, u32[]{:S(2)}) %collective-permute-start.11) | collective-permute-done | bytes 98336 | tf_op jit(solution)/shard_map/ppermute | solution.py:516
  153.3 1.5 join.1
  (33 shorter events, 3.4 us)
Async XLA Ops:
  11.3 25.5 %collective-permute-start.1 = (f32[2,17,16,128]{3,2,1,0:T(8,128)}, f32[2,17,16,128]{3,2,1,0:T(8,128)S(1)}, u32[]{:S(2)}, u32[]{:S(2)}) collective-permute-start(f32[2,17,16,128]{3,2,1,0:T(8,128)} %head.2), channel_id=1, source_target_pairs={{1,0},{2,1},{3,2},{4,3},{5,4},{6,5},{7,6},{9,8},{10,9},{11,10},{12... | collective-permute-start | bytes 835592 | tf_op jit(solution)/shard_map/ppermute | solution.py:27
  13.9 24.9 %collective-permute-start.2 = (f32[2,17,16,128]{3,2,1,0:T(8,128)}, f32[2,17,16,128]{3,2,1,0:T(8,128)S(1)}, u32[]{:S(2)}, u32[]{:S(2)}) collective-permute-start(f32[2,17,16,128]{3,2,1,0:T(8,128)} %head.2), channel_id=1, source_target_pairs={{2,0},{3,1},{4,2},{5,3},{6,4},{7,5},{10,8},{11,9},{12,10},{13,11},... | collective-permute-start | bytes 835592 | tf_op jit(solution)/shard_map/ppermute | solution.py:27
  16.0 22.8 %collective-permute-start.3 = (f32[2,17,16,128]{3,2,1,0:T(8,128)}, f32[2,17,16,128]{3,2,1,0:T(8,128)S(1)}, u32[]{:S(2)}, u32[]{:S(2)}) collective-permute-start(f32[2,17,16,128]{3,2,1,0:T(8,128)} %head.2), channel_id=1, source_target_pairs={{3,0},{4,1},{5,2},{6,3},{7,4},{11,8},{12,9},{13,10},{14,11},{15,12... | collective-permute-start | bytes 835592 | tf_op jit(solution)/shard_map/ppermute | solution.py:27
  18.9 16.0 %collective-permute-start = (bf16[3,8192]{1,0:T(4,128)(2,1)S(1)}, bf16[3,8192]{1,0:T(4,128)(2,1)S(1)}, u32[]{:S(2)}, u32[]{:S(2)}) collective-permute-start(bf16[3,8192]{1,0:T(4,128)(2,1)S(1)} %slice_bitcast_fusion), channel_id=1, source_target_pairs={{0,1},{1,2},{2,3},{3,4},{4,5},{5,6},{6,7},{8,9},{9,10},{10,11},{11... | collective-permute-start | bytes 147464 | tf_op jit(solution)/shard_map/ppermute | solution.py:27
  33.0 48.7 %collective-permute-start.5 = (f32[2,17,16,128]{3,2,1,0:T(8,128)}, f32[2,17,16,128]{3,2,1,0:T(8,128)S(1)}, u32[]{:S(2)}, u32[]{:S(2)}) collective-permute-start(f32[2,17,16,128]{3,2,1,0:T(8,128)} %head.3), channel_id=1, source_target_pairs={{1,0},{2,1},{3,2},{4,3},{5,4},{6,5},{7,6},{9,8},{10,9},{11,10},{12... | collective-permute-start | bytes 835592 | tf_op jit(solution)/shard_map/ppermute | solution.py:27
  34.9 3.9 %copy-start.8 = (bf16[3,8192]{1,0:T(4,128)(2,1)}, bf16[3,8192]{1,0:T(4,128)(2,1)S(1)}, u32[]{:S(2)}) copy-start(bf16[3,8192]{1,0:T(4,128)(2,1)S(1)} %collective-permute-done.hist_ref) | copy-start | bytes 147460
  34.9 46.8 %collective-permute-start.6 = (f32[2,17,16,128]{3,2,1,0:T(8,128)}, f32[2,17,16,128]{3,2,1,0:T(8,128)S(1)}, u32[]{:S(2)}, u32[]{:S(2)}) collective-permute-start(f32[2,17,16,128]{3,2,1,0:T(8,128)} %head.3), channel_id=1, source_target_pairs={{2,0},{3,1},{4,2},{5,3},{6,4},{7,5},{10,8},{11,9},{12,10},{13,11},... | collective-permute-start | bytes 835592 | tf_op jit(solution)/shard_map/ppermute | solution.py:27
  36.9 2.0 %copy-start.1 = (f32[2,17,16,128]{3,2,1,0:T(8,128)}, f32[2,17,16,128]{3,2,1,0:T(8,128)S(1)}, u32[]{:S(2)}) copy-start(f32[2,17,16,128]{3,2,1,0:T(8,128)S(1)} %collective-permute-done.1.next_ref) | copy-start | bytes 835588
  36.9 44.9 %collective-permute-start.7 = (f32[2,17,16,128]{3,2,1,0:T(8,128)}, f32[2,17,16,128]{3,2,1,0:T(8,128)S(1)}, u32[]{:S(2)}, u32[]{:S(2)}) collective-permute-start(f32[2,17,16,128]{3,2,1,0:T(8,128)} %head.3), channel_id=1, source_target_pairs={{3,0},{4,1},{5,2},{6,3},{7,4},{11,8},{12,9},{13,10},{14,11},{15,12... | collective-permute-start | bytes 835592 | tf_op jit(solution)/shard_map/ppermute | solution.py:27
  38.8 0.7 copy-start.2
  38.8 0.8 copy-start.3
  78.6 50.6 %collective-permute-start.4 = (bf16[128,4096]{1,0:T(8,128)(2,1)}, bf16[128,4096]{1,0:T(8,128)(2,1)S(1)}, u32[]{:S(2)}, u32[]{:S(2)}) collective-permute-start(bf16[128,4096]{1,0:T(8,128)(2,1)} %get-tuple-element.29), channel_id=1, source_target_pairs={{8,0},{16,8},{24,16},{9,1},{17,9},{25,17},{10,2},{18,10},{26,18},{... | collective-permute-start | bytes 3145736 | tf_op jit(solution)/shard_map/ppermute | solution.py:27
  81.7 0.7 copy-start
  81.7 0.8 copy-start.4
  81.7 0.9 copy-start.5
  104.7 24.5 %collective-permute-start.8 = (bf16[128,2048]{1,0:T(8,128)(2,1)}, bf16[128,2048]{1,0:T(8,128)(2,1)S(1)}, u32[]{:S(2)}, u32[]{:S(2)}) collective-permute-start(bf16[128,2048]{1,0:T(8,128)(2,1)} %get-tuple-element.35), channel_id=1, source_target_pairs={{8,0},{16,8},{24,16},{9,1},{17,9},{25,17},{10,2},{18,10},{26,18},{... | collective-permute-start | bytes 1572872 | tf_op jit(solution)/shard_map/ppermute | solution.py:27
  129.1 10.7 %copy-start.6 = (f32[3,8192]{1,0:T(4,128)S(1)}, f32[3,8192]{1,0:T(4,128)}, u32[]{:S(2)}) copy-start(f32[3,8192]{1,0:T(4,128)} %get-tuple-element.45) | copy-start | bytes 294916
  129.2 12.7 %copy-start.7 = (f32[3,8192]{1,0:T(4,128)S(1)}, f32[3,8192]{1,0:T(4,128)}, u32[]{:S(2)}) copy-start(f32[3,8192]{1,0:T(4,128)} %get-tuple-element.46) | copy-start | bytes 294916
  130.3 2.0 %collective-permute-start.12 = (f32[4,24,1024]{2,1,0:T(8,128)S(1)}, f32[4,24,1024]{2,1,0:T(8,128)S(1)}, u32[]{:S(2)}, u32[]{:S(2)}) collective-permute-start(f32[4,24,1024]{2,1,0:T(8,128)S(1)} %dynamic-slice_bitcast_fusion), channel_id=1, source_target_pairs={{0,1},{1,0},{2,3},{3,2},{4,5},{5,4},{6,7},{7,6},{8,9},{9,8},{10,11... | collective-permute-start | bytes 1179656 | tf_op jit(solution)/shard_map/ppermute | solution.py:520
  130.4 15.1 %collective-permute-start.9 = (bf16[128,2048]{1,0:T(8,128)(2,1)}, bf16[128,2048]{1,0:T(8,128)(2,1)S(1)}, u32[]{:S(2)}, u32[]{:S(2)}) collective-permute-start(bf16[128,2048]{1,0:T(8,128)(2,1)} %get-tuple-element.41), channel_id=1, source_target_pairs={{8,0},{16,8},{24,16},{9,1},{17,9},{25,17},{10,2},{18,10},{26,18},{... | collective-permute-start | bytes 1572872 | tf_op jit(solution)/shard_map/ppermute | solution.py:27
  134.1 20.7 %all-to-all-start = ((f32[4,24,1024]{2,1,0:T(8,128)}), f32[4,24,1024]{2,1,0:T(8,128)S(1)}, u32[]{:S(2)}, u32[]{:S(2)}) async-start(f32[4,24,1024]{2,1,0:T(8,128)} %bitcast_add_fusion), calls=%async_computation | async-start | bytes 786432 | tf_op jit(solution)/shard_map/all_to_all | solution.py:523
  139.9 8.4 %collective-permute-start.10 = (f32[3,8192]{1,0:T(4,128)S(1)}, f32[3,8192]{1,0:T(4,128)S(1)}, u32[]{:S(2)}, u32[]{:S(2)}) collective-permute-start(f32[3,8192]{1,0:T(4,128)S(1)} %copy-done.6), channel_id=1, source_target_pairs={{8,0},{16,8},{24,16},{9,1},{17,9},{25,17},{10,2},{18,10},{26,18},{... | collective-permute-start | bytes 294920 | tf_op jit(solution)/shard_map/ppermute | solution.py:27
  141.8 11.5 %collective-permute-start.11 = (f32[3,8192]{1,0:T(4,128)S(1)}, f32[3,8192]{1,0:T(4,128)S(1)}, u32[]{:S(2)}, u32[]{:S(2)}) collective-permute-start(f32[3,8192]{1,0:T(4,128)S(1)} %copy-done.7), channel_id=1, source_target_pairs={{9,0},{10,1},{11,2},{12,3},{13,4},{14,5},{15,6},{17,8},{18,9},{19,... | collective-permute-start | bytes 294920 | tf_op jit(solution)/shard_map/ppermute | solution.py:516

commit v10 on v9

--- a/solution.py
+++ b/solution.py
@@ -69,7 +69,7 @@
         dst[pl.ds(first + t, WIDE)] = wide.reshape(WIDE, group, LANES)
         return 0
 
-    lax.fori_loop(0, rows // WIDE, move, 0)
+    lax.fori_loop(0, rows // WIDE, move, 0, unroll=2)
 
 
 def scatter_positions(src, dst_ref, group):
@@ -81,7 +81,7 @@
         dst_ref[pl.ds(t, WIDE), :] = wide.astype(dst_ref.dtype)
         return 0
 
-    lax.fori_loop(0, rows // WIDE, move, 0)
+    lax.fori_loop(0, rows // WIDE, move, 0, unroll=2)
 
 
 def head_kernel(group, unroll, place_ref, len_ref, maps_ref, dt_ref, gy_ref, alog_ref, head_ref,
@@ -356,7 +356,7 @@
                 maps_t[pl.ds((base + n) * rows + tb * 8, 8), :] = parts[0]
             return 0
 
-        lax.fori_loop(0, states, add_state, 0, unroll=2)
+        lax.fori_loop(0, states, add_state, 0, unroll=4)
 
     def add_lanes(n, _):
         flat = maps_t[pl.ds(at_chunk(n, rows), rows), :].T

time: 156 us -> 155 us (level)
  no operation moved by 1% of the time
where the time goes in v10:
time: 155 us
  Pallas kernels  105 us (68%)
  starting transfers between devices  33.2 us (21%)
  waiting for transfers between devices  9.03 us (6%)
  local copies, waits for them, and re-layouts  4.39 us (3%)
  other arithmetic  1.84 us (1%)
    pallas_call x3, Pallas kernels, main_call(): pl.pallas_call(functools.partial(main_kernel, group, part, blocks > 1), g...  82.5 us
    ppermute x11, starting transfers between devices, shift_to(): return lax.ppermute(x, axis, pairs)  24.9 us
    pallas_call x2, Pallas kernels, head_call(): pl.pallas_call(functools.partial(head_kernel, group, 8), grid=(blocks,),...  21.2 us
    all_to_all x1, starting transfers between devices, on_device(): lax.all_to_all(half, 'ctx', 0, 0, tiled=True, axis_index_groups=groups)  5.77 us
    ppermute x1, waiting for transfers between devices, on_device(): spilled = lax.ppermute(spill, ('pipe', 'ctx'), pairs)  5 us
    ppermute x11, waiting for transfers between devices, shift_to(): return lax.ppermute(x, axis, pairs)  4.03 us
  transfers between devices with their start and end apart: 14, of which 3 were waited for; matrix products, arithmetic and copies ran while one was open for 2% of the time, Pallas kernels for 61%

profile of v10, /device:TPU:13, one launch (start us, length us, event | category | flops | bytes accessed | tf_op | source)
XLA Modules:
  0.0 154.6 jit_solution(2777142461726922318)
XLA Ops:
  0.6 10.6 %head.2 = f32[2,17,16,128]{3,2,1,0:T(8,128)} custom-call(s32[1]{0:T(128)} %bitcast.place_ref, s32[1,8]{1,0:T(1,128)} %len_ref.9, f32[32,128]{1,0:T(8,128)} %bitcast.46, bf16[128,8192]{1,0:T(8,128)(2,1)} %bitcast.25, bf16[128,8192]{1,0:T(8,128)(2,1)} %bitcast.30, f32[16,8192]{1,0:T(8,128)} %bitcast.38), custom_call_target="tpu_custom_call" | custom-call | flops 8388608000 | bytes 33554432 | tf_op jit(solution)/shard_map/head/pallas_call | solution.py:136
  11.2 2.6 %collective-permute-start.1 = (f32[2,17,16,128]{3,2,1,0:T(8,128)}, f32[2,17,16,128]{3,2,1,0:T(8,128)S(1)}, u32[]{:S(2)}, u32[]{:S(2)}) collective-permute-start(f32[2,17,16,128]{3,2,1,0:T(8,128)} %head.2), channel_id=1, source_target_pairs={{1,0},{2,1},{3,2},{4,3},{5,4},{6,5},{7,6},{9,8},{10,9},{11,10},{12... | collective-permute-start | bytes 835592 | tf_op jit(solution)/shard_map/ppermute | solution.py:27
  13.8 2.1 %collective-permute-start.2 = (f32[2,17,16,128]{3,2,1,0:T(8,128)}, f32[2,17,16,128]{3,2,1,0:T(8,128)S(1)}, u32[]{:S(2)}, u32[]{:S(2)}) collective-permute-start(f32[2,17,16,128]{3,2,1,0:T(8,128)} %head.2), channel_id=1, source_target_pairs={{2,0},{3,1},{4,2},{5,3},{6,4},{7,5},{10,8},{11,9},{12,10},{13,11},... | collective-permute-start | bytes 835592 | tf_op jit(solution)/shard_map/ppermute | solution.py:27
  15.9 1.9 %collective-permute-start.3 = (f32[2,17,16,128]{3,2,1,0:T(8,128)}, f32[2,17,16,128]{3,2,1,0:T(8,128)S(1)}, u32[]{:S(2)}, u32[]{:S(2)}) collective-permute-start(f32[2,17,16,128]{3,2,1,0:T(8,128)} %head.2), channel_id=1, source_target_pairs={{3,0},{4,1},{5,2},{6,3},{7,4},{11,8},{12,9},{13,10},{14,11},{15,12... | collective-permute-start | bytes 835592 | tf_op jit(solution)/shard_map/ppermute | solution.py:27
  18.8 3.4 %collective-permute-start = (bf16[3,8192]{1,0:T(4,128)(2,1)S(1)}, bf16[3,8192]{1,0:T(4,128)(2,1)S(1)}, u32[]{:S(2)}, u32[]{:S(2)}) collective-permute-start(bf16[3,8192]{1,0:T(4,128)(2,1)S(1)} %slice_bitcast_fusion), channel_id=1, source_target_pairs={{0,1},{1,2},{2,3},{3,4},{4,5},{5,6},{6,7},{8,9},{9,10},{10,11},{11... | collective-permute-start | bytes 147464 | tf_op jit(solution)/shard_map/ppermute | solution.py:27
  22.2 10.6 %head.3 = f32[2,17,16,128]{3,2,1,0:T(8,128)} custom-call(s32[1]{0:T(128)} %bitcast.place_ref, s32[1,8]{1,0:T(1,128)} %len_ref.9, f32[32,128]{1,0:T(8,128)} %bitcast.47, bf16[128,8192]{1,0:T(8,128)(2,1)} %bitcast.26, bf16[128,8192]{1,0:T(8,128)(2,1)} %bitcast.31, f32[16,8192]{1,0:T(8,128)} %bitcast.39), custom_call_target="tpu_custom_call" | custom-call | flops 8388608000 | bytes 33554432 | tf_op jit(solution)/shard_map/head/pallas_call | solution.py:136
  32.8 1.9 %collective-permute-start.5 = (f32[2,17,16,128]{3,2,1,0:T(8,128)}, f32[2,17,16,128]{3,2,1,0:T(8,128)S(1)}, u32[]{:S(2)}, u32[]{:S(2)}) collective-permute-start(f32[2,17,16,128]{3,2,1,0:T(8,128)} %head.3), channel_id=1, source_target_pairs={{1,0},{2,1},{3,2},{4,3},{5,4},{6,5},{7,6},{9,8},{10,9},{11,10},{12... | collective-permute-start | bytes 835592 | tf_op jit(solution)/shard_map/ppermute | solution.py:27
  34.7 1.9 %collective-permute-start.6 = (f32[2,17,16,128]{3,2,1,0:T(8,128)}, f32[2,17,16,128]{3,2,1,0:T(8,128)S(1)}, u32[]{:S(2)}, u32[]{:S(2)}) collective-permute-start(f32[2,17,16,128]{3,2,1,0:T(8,128)} %head.3), channel_id=1, source_target_pairs={{2,0},{3,1},{4,2},{5,3},{6,4},{7,5},{10,8},{11,9},{12,10},{13,11},... | collective-permute-start | bytes 835592 | tf_op jit(solution)/shard_map/ppermute | solution.py:27
  36.7 1.9 %collective-permute-start.7 = (f32[2,17,16,128]{3,2,1,0:T(8,128)}, f32[2,17,16,128]{3,2,1,0:T(8,128)S(1)}, u32[]{:S(2)}, u32[]{:S(2)}) collective-permute-start(f32[2,17,16,128]{3,2,1,0:T(8,128)} %head.3), channel_id=1, source_target_pairs={{3,0},{4,1},{5,2},{6,3},{7,4},{11,8},{12,9},{13,10},{14,11},{15,12... | collective-permute-start | bytes 835592 | tf_op jit(solution)/shard_map/ppermute | solution.py:27
  39.4 38.7 %main.3 = (bf16[128,4096]{1,0:T(8,128)(2,1)}, bf16[128,8192]{1,0:T(8,128)(2,1)}, f32[3,8192]{1,0:T(4,128)}, f32[3,8192]{1,0:T(4,128)}, f32[8,24,1024]{2,1,0:T(8,128)}, /*index=5*/f32[32,128]{1,0:T(8,128)}) custom-call(s32[1]{0:T(128)} %bitcast.place_ref, s32[1,8]{1,0:T(1,128)} %len_ref.9, f32[32,128]{1,0:T(8,128)} %bitcast.48, bf16[128,8192]{1,0:T(8,128)(2,1)} %bitcast.22, ...), custom_call_target="tpu_custom_call" | custom-call | flops 41943040000 | bytes 150994944 | tf_op jit(solution)/shard_map/main/pallas_call | solution.py:407
  78.1 3.1 %collective-permute-start.4 = (bf16[128,4096]{1,0:T(8,128)(2,1)}, bf16[128,4096]{1,0:T(8,128)(2,1)S(1)}, u32[]{:S(2)}, u32[]{:S(2)}) collective-permute-start(bf16[128,4096]{1,0:T(8,128)(2,1)} %get-tuple-element.29), channel_id=1, source_target_pairs={{8,0},{16,8},{24,16},{9,1},{17,9},{25,17},{10,2},{18,10},{26,18},{... | collective-permute-start | bytes 3145736 | tf_op jit(solution)/shard_map/ppermute | solution.py:27
  82.1 21.9 %main.4 = (bf16[128,2048]{1,0:T(8,128)(2,1)}, bf16[128,8192]{1,0:T(8,128)(2,1)}, f32[3,8192]{1,0:T(4,128)}, f32[3,8192]{1,0:T(4,128)}, f32[8,24,1024]{2,1,0:T(8,128)}, /*index=5*/f32[32,128]{1,0:T(8,128)}) custom-call(s32[1]{0:T(128)} %bitcast.place_ref, ...), custom_call_target="tpu_custom_call", output_to_operand_aliasing={{1}: (15, {}), {2}: (16, {}), {3}: (17, {}), {4}: (18, {}),... | custom-call | flops 20971520000 | bytes 75497472 | tf_op jit(solution)/shard_map/main/pallas_call | solution.py:407
  104.0 2.3 %collective-permute-start.8 = (bf16[128,2048]{1,0:T(8,128)(2,1)}, bf16[128,2048]{1,0:T(8,128)(2,1)S(1)}, u32[]{:S(2)}, u32[]{:S(2)}) collective-permute-start(bf16[128,2048]{1,0:T(8,128)(2,1)} %get-tuple-element.35), channel_id=1, source_target_pairs={{8,0},{16,8},{24,16},{9,1},{17,9},{25,17},{10,2},{18,10},{26,18},{... | collective-permute-start | bytes 1572872 | tf_op jit(solution)/shard_map/ppermute | solution.py:27
  106.3 21.9 %main.5 = (bf16[128,2048]{1,0:T(8,128)(2,1)}, bf16[128,8192]{1,0:T(8,128)(2,1)}, f32[3,8192]{1,0:T(4,128)}, f32[3,8192]{1,0:T(4,128)}, f32[8,24,1024]{2,1,0:T(8,128)}, /*index=5*/f32[32,128]{1,0:T(8,128)}) custom-call(s32[1]{0:T(128)} %bitcast.place_ref, ...), custom_call_target="tpu_custom_call", output_to_operand_aliasing={{1}: (15, {}), {2}: (16, {}), {3}: (17, {}), {4}: (18, {}),... | custom-call | flops 20971520000 | bytes 75497472 | tf_op jit(solution)/shard_map/main/pallas_call | solution.py:407
  128.3 1.1 dynamic-slice_bitcast_fusion
  129.4 1.9 %collective-permute-start.9 = (bf16[128,2048]{1,0:T(8,128)(2,1)}, bf16[128,2048]{1,0:T(8,128)(2,1)S(1)}, u32[]{:S(2)}, u32[]{:S(2)}) collective-permute-start(bf16[128,2048]{1,0:T(8,128)(2,1)} %get-tuple-element.41), channel_id=1, source_target_pairs={{8,0},{16,8},{24,16},{9,1},{17,9},{25,17},{10,2},{18,10},{26,18},{... | collective-permute-start | bytes 1572872 | tf_op jit(solution)/shard_map/ppermute | solution.py:27
  131.4 1.8 %bitcast_add_fusion = f32[4,24,1024]{2,1,0:T(8,128)} fusion(f32[4,24,1024]{2,1,0:T(8,128)S(1)} %collective-permute-done.12, f32[4,2,24,1024]{3,2,1,0:T(8,128)} %bitcast.20, s32[]{:T(128)S(6)} %select_n.15), kind=kLoop, calls=%fused_computation | loop fusion | flops 98304 | bytes 1179652 | tf_op jit(solution)/shard_map/add | solution.py:521
  133.2 5.8 %all-to-all-start = ((f32[4,24,1024]{2,1,0:T(8,128)}), f32[4,24,1024]{2,1,0:T(8,128)S(1)}, u32[]{:S(2)}, u32[]{:S(2)}) async-start(f32[4,24,1024]{2,1,0:T(8,128)} %bitcast_add_fusion), calls=%async_computation | async-start | bytes 786432 | tf_op jit(solution)/shard_map/all_to_all | solution.py:523
  139.0 1.9 %collective-permute-start.10 = (f32[3,8192]{1,0:T(4,128)S(1)}, f32[3,8192]{1,0:T(4,128)S(1)}, u32[]{:S(2)}, u32[]{:S(2)}) collective-permute-start(f32[3,8192]{1,0:T(4,128)S(1)} %copy-done.6), channel_id=1, source_target_pairs={{8,0},{16,8},{24,16},{9,1},{17,9},{25,17},{10,2},{18,10},{26,18},{... | collective-permute-start | bytes 294920 | tf_op jit(solution)/shard_map/ppermute | solution.py:27
  140.9 2.4 %collective-permute-start.11 = (f32[3,8192]{1,0:T(4,128)S(1)}, f32[3,8192]{1,0:T(4,128)S(1)}, u32[]{:S(2)}, u32[]{:S(2)}) collective-permute-start(f32[3,8192]{1,0:T(4,128)S(1)} %copy-done.7), channel_id=1, source_target_pairs={{9,0},{10,1},{11,2},{12,3},{13,4},{14,5},{15,6},{17,8},{18,9},{19,... | collective-permute-start | bytes 294920 | tf_op jit(solution)/shard_map/ppermute | solution.py:516
  143.4 1.2 collective-permute-done.9.refs_2_
  144.6 2.8 %collective-permute-done.10.refs_3_ = f32[3,8192]{1,0:T(4,128)S(1)} collective-permute-done((f32[3,8192]{1,0:T(4,128)S(1)}, f32[3,8192]{1,0:T(4,128)S(1)}, u32[]{:S(2)}, u32[]{:S(2)}) %collective-permute-start.10) | collective-permute-done | bytes 98336 | tf_op jit(solution)/shard_map/ppermute | solution.py:27
  147.4 5.0 %collective-permute-done.11.refs_4_ = f32[3,8192]{1,0:T(4,128)S(1)} collective-permute-done((f32[3,8192]{1,0:T(4,128)S(1)}, f32[3,8192]{1,0:T(4,128)S(1)}, u32[]{:S(2)}, u32[]{:S(2)}) %collective-permute-start.11) | collective-permute-done | bytes 98336 | tf_op jit(solution)/shard_map/ppermute | solution.py:516
  152.4 1.5 join.1
  (33 shorter events, 3.4 us)
Async XLA Ops:
  11.2 25.4 %collective-permute-start.1 = (f32[2,17,16,128]{3,2,1,0:T(8,128)}, f32[2,17,16,128]{3,2,1,0:T(8,128)S(1)}, u32[]{:S(2)}, u32[]{:S(2)}) collective-permute-start(f32[2,17,16,128]{3,2,1,0:T(8,128)} %head.2), channel_id=1, source_target_pairs={{1,0},{2,1},{3,2},{4,3},{5,4},{6,5},{7,6},{9,8},{10,9},{11,10},{12... | collective-permute-start | bytes 835592 | tf_op jit(solution)/shard_map/ppermute | solution.py:27
  13.8 24.8 %collective-permute-start.2 = (f32[2,17,16,128]{3,2,1,0:T(8,128)}, f32[2,17,16,128]{3,2,1,0:T(8,128)S(1)}, u32[]{:S(2)}, u32[]{:S(2)}) collective-permute-start(f32[2,17,16,128]{3,2,1,0:T(8,128)} %head.2), channel_id=1, source_target_pairs={{2,0},{3,1},{4,2},{5,3},{6,4},{7,5},{10,8},{11,9},{12,10},{13,11},... | collective-permute-start | bytes 835592 | tf_op jit(solution)/shard_map/ppermute | solution.py:27
  15.9 22.7 %collective-permute-start.3 = (f32[2,17,16,128]{3,2,1,0:T(8,128)}, f32[2,17,16,128]{3,2,1,0:T(8,128)S(1)}, u32[]{:S(2)}, u32[]{:S(2)}) collective-permute-start(f32[2,17,16,128]{3,2,1,0:T(8,128)} %head.2), channel_id=1, source_target_pairs={{3,0},{4,1},{5,2},{6,3},{7,4},{11,8},{12,9},{13,10},{14,11},{15,12... | collective-permute-start | bytes 835592 | tf_op jit(solution)/shard_map/ppermute | solution.py:27
  18.8 15.9 %collective-permute-start = (bf16[3,8192]{1,0:T(4,128)(2,1)S(1)}, bf16[3,8192]{1,0:T(4,128)(2,1)S(1)}, u32[]{:S(2)}, u32[]{:S(2)}) collective-permute-start(bf16[3,8192]{1,0:T(4,128)(2,1)S(1)} %slice_bitcast_fusion), channel_id=1, source_target_pairs={{0,1},{1,2},{2,3},{3,4},{4,5},{5,6},{6,7},{8,9},{9,10},{10,11},{11... | collective-permute-start | bytes 147464 | tf_op jit(solution)/shard_map/ppermute | solution.py:27
  32.8 48.4 %collective-permute-start.5 = (f32[2,17,16,128]{3,2,1,0:T(8,128)}, f32[2,17,16,128]{3,2,1,0:T(8,128)S(1)}, u32[]{:S(2)}, u32[]{:S(2)}) collective-permute-start(f32[2,17,16,128]{3,2,1,0:T(8,128)} %head.3), channel_id=1, source_target_pairs={{1,0},{2,1},{3,2},{4,3},{5,4},{6,5},{7,6},{9,8},{10,9},{11,10},{12... | collective-permute-start | bytes 835592 | tf_op jit(solution)/shard_map/ppermute | solution.py:27
  34.7 3.9 %copy-start.8 = (bf16[3,8192]{1,0:T(4,128)(2,1)}, bf16[3,8192]{1,0:T(4,128)(2,1)S(1)}, u32[]{:S(2)}) copy-start(bf16[3,8192]{1,0:T(4,128)(2,1)S(1)} %collective-permute-done.hist_ref) | copy-start | bytes 147460
  34.7 46.5 %collective-permute-start.6 = (f32[2,17,16,128]{3,2,1,0:T(8,128)}, f32[2,17,16,128]{3,2,1,0:T(8,128)S(1)}, u32[]{:S(2)}, u32[]{:S(2)}) collective-permute-start(f32[2,17,16,128]{3,2,1,0:T(8,128)} %head.3), channel_id=1, source_target_pairs={{2,0},{3,1},{4,2},{5,3},{6,4},{7,5},{10,8},{11,9},{12,10},{13,11},... | collective-permute-start | bytes 835592 | tf_op jit(solution)/shard_map/ppermute | solution.py:27
  36.7 2.0 %copy-start.1 = (f32[2,17,16,128]{3,2,1,0:T(8,128)}, f32[2,17,16,128]{3,2,1,0:T(8,128)S(1)}, u32[]{:S(2)}) copy-start(f32[2,17,16,128]{3,2,1,0:T(8,128)S(1)} %collective-permute-done.1.next_ref) | copy-start | bytes 835588
  36.7 44.5 %collective-permute-start.7 = (f32[2,17,16,128]{3,2,1,0:T(8,128)}, f32[2,17,16,128]{3,2,1,0:T(8,128)S(1)}, u32[]{:S(2)}, u32[]{:S(2)}) collective-permute-start(f32[2,17,16,128]{3,2,1,0:T(8,128)} %head.3), channel_id=1, source_target_pairs={{3,0},{4,1},{5,2},{6,3},{7,4},{11,8},{12,9},{13,10},{14,11},{15,12... | collective-permute-start | bytes 835592 | tf_op jit(solution)/shard_map/ppermute | solution.py:27
  38.6 0.7 copy-start.2
  38.6 0.8 copy-start.3
  78.1 50.2 %collective-permute-start.4 = (bf16[128,4096]{1,0:T(8,128)(2,1)}, bf16[128,4096]{1,0:T(8,128)(2,1)S(1)}, u32[]{:S(2)}, u32[]{:S(2)}) collective-permute-start(bf16[128,4096]{1,0:T(8,128)(2,1)} %get-tuple-element.29), channel_id=1, source_target_pairs={{8,0},{16,8},{24,16},{9,1},{17,9},{25,17},{10,2},{18,10},{26,18},{... | collective-permute-start | bytes 3145736 | tf_op jit(solution)/shard_map/ppermute | solution.py:27
  81.2 0.7 copy-start
  81.2 0.8 copy-start.4
  81.2 0.9 copy-start.5
  104.0 24.3 %collective-permute-start.8 = (bf16[128,2048]{1,0:T(8,128)(2,1)}, bf16[128,2048]{1,0:T(8,128)(2,1)S(1)}, u32[]{:S(2)}, u32[]{:S(2)}) collective-permute-start(bf16[128,2048]{1,0:T(8,128)(2,1)} %get-tuple-element.35), channel_id=1, source_target_pairs={{8,0},{16,8},{24,16},{9,1},{17,9},{25,17},{10,2},{18,10},{26,18},{... | collective-permute-start | bytes 1572872 | tf_op jit(solution)/shard_map/ppermute | solution.py:27
  128.2 10.7 %copy-start.6 = (f32[3,8192]{1,0:T(4,128)S(1)}, f32[3,8192]{1,0:T(4,128)}, u32[]{:S(2)}) copy-start(f32[3,8192]{1,0:T(4,128)} %get-tuple-element.45) | copy-start | bytes 294916
  128.2 12.7 %copy-start.7 = (f32[3,8192]{1,0:T(4,128)S(1)}, f32[3,8192]{1,0:T(4,128)}, u32[]{:S(2)}) copy-start(f32[3,8192]{1,0:T(4,128)} %get-tuple-element.46) | copy-start | bytes 294916
  129.4 2.0 %collective-permute-start.12 = (f32[4,24,1024]{2,1,0:T(8,128)S(1)}, f32[4,24,1024]{2,1,0:T(8,128)S(1)}, u32[]{:S(2)}, u32[]{:S(2)}) collective-permute-start(f32[4,24,1024]{2,1,0:T(8,128)S(1)} %dynamic-slice_bitcast_fusion), channel_id=1, source_target_pairs={{0,1},{1,0},{2,3},{3,2},{4,5},{5,4},{6,7},{7,6},{8,9},{9,8},{10,11... | collective-permute-start | bytes 1179656 | tf_op jit(solution)/shard_map/ppermute | solution.py:520
  129.4 15.1 %collective-permute-start.9 = (bf16[128,2048]{1,0:T(8,128)(2,1)}, bf16[128,2048]{1,0:T(8,128)(2,1)S(1)}, u32[]{:S(2)}, u32[]{:S(2)}) collective-permute-start(bf16[128,2048]{1,0:T(8,128)(2,1)} %get-tuple-element.41), channel_id=1, source_target_pairs={{8,0},{16,8},{24,16},{9,1},{17,9},{25,17},{10,2},{18,10},{26,18},{... | collective-permute-start | bytes 1572872 | tf_op jit(solution)/shard_map/ppermute | solution.py:27
  133.2 20.7 %all-to-all-start = ((f32[4,24,1024]{2,1,0:T(8,128)}), f32[4,24,1024]{2,1,0:T(8,128)S(1)}, u32[]{:S(2)}, u32[]{:S(2)}) async-start(f32[4,24,1024]{2,1,0:T(8,128)} %bitcast_add_fusion), calls=%async_computation | async-start | bytes 786432 | tf_op jit(solution)/shard_map/all_to_all | solution.py:523
  139.0 8.4 %collective-permute-start.10 = (f32[3,8192]{1,0:T(4,128)S(1)}, f32[3,8192]{1,0:T(4,128)S(1)}, u32[]{:S(2)}, u32[]{:S(2)}) collective-permute-start(f32[3,8192]{1,0:T(4,128)S(1)} %copy-done.6), channel_id=1, source_target_pairs={{8,0},{16,8},{24,16},{9,1},{17,9},{25,17},{10,2},{18,10},{26,18},{... | collective-permute-start | bytes 294920 | tf_op jit(solution)/shard_map/ppermute | solution.py:27
  140.9 11.5 %collective-permute-start.11 = (f32[3,8192]{1,0:T(4,128)S(1)}, f32[3,8192]{1,0:T(4,128)S(1)}, u32[]{:S(2)}, u32[]{:S(2)}) collective-permute-start(f32[3,8192]{1,0:T(4,128)S(1)} %copy-done.7), channel_id=1, source_target_pairs={{9,0},{10,1},{11,2},{12,3},{13,4},{14,5},{15,6},{17,8},{18,9},{19,... | collective-permute-start | bytes 294920 | tf_op jit(solution)/shard_map/ppermute | solution.py:516
